TPU v7x, 32 devices: a whole 2x2x4 slice. The times are simulated.
32 devices in a mesh: seg: 4 (over x, core), blk: 8 (over z, y).
Axes of the slice: x: 2, y: 2, z: 4, core: 2. Of those that a mesh axis runs over, the one named last changes fastest.
Arguments:
- start_vector: bfloat16 [4, 32, 128, 128], P('seg', 'blk'), may hold values from -6 to 6
- left_environment: bfloat16 [4, 32, 34, 128, 128], P('seg', 'blk'), may hold values from -0.5 to 0.5
- right_environment: bfloat16 [4, 32, 34, 128, 128], P('seg', 'blk'), may hold values from -0.5 to 0.5
- block_energy: float32 [4, 32], P('seg', 'blk'), may hold values from -2 to 2
- sector_rows: int32 [4, 32], P('seg', 'blk'), may hold values from 32 to 128, as said below
- sector_cols: int32 [4, 32], P('seg', 'blk'), may hold values from 32 to 128, as said below
- feed_block: int32 [4, 32, 34], P('seg', 'blk'), may hold values from 0 to 32, as said below
Outputs:
- coefficients: float32 [4, 6], P('seg')
- residual: float32 [4, 32, 128, 128], P('seg', 'blk')
Inputs may be any that keep to these rules, and one draw needn't show every extreme that they name: `sector_rows`: the first block of every segment fills its tile. `sector_cols`: the first block of every segment fills its tile. `feed_block`: 32 marks an absent channel; absent channels come after the present ones of a block, and the first block of every segment has all 34 channels.
All inputs are finite; a program needn't handle non-finite values.
Results may differ from a plain program's by a relative error of at most 0.014.
Values may be sent and summed in bfloat16 or wider, within the bound.
No kernel may reach another device: no remote copies, remote signals or barrier semaphores. Data moves between devices by JAX's collectives and lax.ppermute only.
A program may use at most 128 MiB of HBM per device.

v0:
```python
import jax
import jax.numpy as jnp
from jax import lax
from jax.sharding import PartitionSpec as P

STEPS = 3


epsilon = 1e-06


def passed_along(block, axis, distance):
    devices = range(lax.axis_size(axis))
    route = [(i - distance, i) for i in devices if i - distance in devices]
    return lax.ppermute(block, axis, route)


def local(
    start_vector,
    left_environment,
    right_environment,
    block_energy,
    sector_rows,
    sector_cols,
    feed_block,
):
    arrived = passed_along(left_environment, "seg", 1)
    left_tiles = arrived[0]
    right_tiles = right_environment[0]
    local_blocks = start_vector.shape[1]
    channels = left_environment.shape[2]
    tile_width = start_vector.shape[2]
    all_blocks = local_blocks * lax.axis_size("blk")
    positions = jnp.arange(tile_width, dtype=jnp.int32)
    row_mask = (positions[None, :] < sector_rows[0][:, None]).astype(jnp.float32)
    col_mask = (positions[None, :] < sector_cols[0][:, None]).astype(jnp.float32)
    mask_tiles = row_mask[:, :, None] * col_mask[:, None, :]
    energy = block_energy[0]
    feeds = feed_block[0].reshape(local_blocks * channels)
    entries = float(all_blocks * tile_width * tile_width)
    vector = mask_tiles * start_vector[0].astype(jnp.float32)
    start_sum = lax.psum(jnp.sum(vector * vector), "blk")
    vector = vector * lax.rsqrt(start_sum / entries + epsilon)
    before = jnp.zeros_like(vector)
    coef_beta = jnp.float32(0.0)
    alphas = []
    betas = []
    image = vector
    for turn_index in range(STEPS):
        low_vector = vector.astype(jnp.bfloat16)
        half_product = jnp.einsum(
            "kwab,kbc->kwac", left_tiles, low_vector, preferred_element_type=jnp.float32
        ).astype(jnp.bfloat16)
        contrib = jnp.einsum(
            "kwac,kwcd->kwad", half_product, right_tiles, preferred_element_type=jnp.float32
        )
        contrib = contrib.reshape(local_blocks * channels, tile_width * tile_width)
        partial_value = jax.ops.segment_sum(contrib, feeds, num_segments=all_blocks + 1)
        partial_value = partial_value[:all_blocks].reshape(all_blocks, tile_width, tile_width)
        summed = lax.psum_scatter(
            partial_value.astype(jnp.bfloat16), "blk", scatter_dimension=0, tiled=True
        ).astype(jnp.float32)
        image = mask_tiles * summed + energy[:, None, None] * vector
        coef_alpha = lax.psum(jnp.sum(vector * image), "blk") / entries
        image = image - coef_alpha * vector - coef_beta * before
        mean_square = lax.psum(jnp.sum(image * image), "blk") / entries
        coef_beta = jnp.sqrt(mean_square)
        before = vector
        vector = image * lax.rsqrt(mean_square + epsilon)
        alphas.append(coef_alpha)
        betas.append(coef_beta)
    coefficients = jnp.stack(alphas + betas)[None, :]
    return (coefficients, image[None])


def solution(mesh):
    return jax.shard_map(
        local,
        mesh=mesh,
        in_specs=(
            P("seg", "blk", None, None),
            P("seg", "blk", None, None, None),
            P("seg", "blk", None, None, None),
            P("seg", "blk"),
            P("seg", "blk"),
            P("seg", "blk"),
            P("seg", "blk", None),
        ),
        out_specs=(P("seg", None), P("seg", "blk", None, None)),
        check_vma=False,
    )
```

profile of v0, /device:TPU:6, one launch (start us, length us, event | category | flops | bytes accessed | tf_op | source)
XLA Modules:
  0.0 480.7 jit_solution(9267787511390663121)
XLA Ops:
  7.2 1.9 collective-permute-start
  11.5 18.6 %psum.49 = f32[]{:T(128)} all-reduce(f32[]{:T(128)} %fusion.58), channel_id=1, replica_groups=mesh['seg'=4,'blk'=8] {'blk'}, use_global_device_ids=true, to_apply=%region_1.0 | all-reduce | flops 1 | bytes 8 | tf_op jit(solution)/shard_map/psum | solution.py:42
  31.6 28.5 %collective-permute-done = bf16[1,4,34,128,128]{4,3,2,1,0:T(8,128)(2,1)} collective-permute-done((bf16[1,4,34,128,128]{4,3,2,1,0:T(8,128)(2,1)}, bf16[1,4,34,128,128]{4,3,2,1,0:T(8,128)(2,1)}, u32[]{:S(2)}, u32[]{:S(2)}) %collective-permute-start) | collective-permute-done | bytes 4456480 | tf_op jit(solution)/shard_map/ppermute | solution.py:15
  60.2 9.6 %fusion.15 = f32[4,34,128,128]{3,2,1,0:T(8,128)} fusion(bf16[1,4,34,128,128]{4,3,2,1,0:T(8,128)(2,1)} %param.9, bf16[1,4,34,128,128]{4,3,2,1,0:T(8,128)(2,1)} %collective-permute-done, bf16[1,4,128,128]{3,2,1,0:T(8,128)(2,1)} %param.7, f32[]{:T(128)S(6)} %rsqrt.9, f32[4,128]{1,0:T(4,128)S(1)} %get-tuple-element.7, f32[4,128]{1,0:T(4,128)S(1)} %get-tuple-element.6), kind=kOutput, calls=%fused_computation.18 | convolution fusion | flops 1143406592 | bytes 17960964 | tf_op jit(solution)/shard_map/kwac,kwcd->kwad/dot_general | solution.py:54
  69.8 19.3 %scatter_custom_fusion = f32[33,16384]{1,0:T(8,128)S(1)} fusion(s32[136]{0:T(256)S(1)} %reshape.74, f32[17,8,128,128]{3,2,1,0:T(8,128)} %bitcast.113, f32[]{:T(128)} %constant.11.clone.1), kind=kCustom, calls=%fused_computation.9 | custom fusion | flops 2228224 | bytes 11075588 | tf_op jit(solution)/shard_map/scatter-add | solution.py:58
  90.5 65.5 %reduce-scatter.4.cloned.1.call-done = bf16[4,128,128]{2,1,0:T(8,128)(2,1)} async-done(((bf16[32,128,128]{2,1,0:T(8,128)(2,1)}), bf16[4,128,128]{2,1,0:T(8,128)(2,1)}) %reduce-scatter.4.cloned.1.call-update) | async-done | bytes 131088 | tf_op jit(solution)/shard_map/reduce_scatter | solution.py:60
  156.1 1.7 fusion.55
  157.7 18.6 %psum.50 = f32[]{:T(128)} all-reduce(f32[]{:T(128)} %fusion.55), channel_id=1, replica_groups=mesh['seg'=4,'blk'=8] {'blk'}, use_global_device_ids=true, to_apply=%region_5.0 | all-reduce | flops 1 | bytes 8 | tf_op jit(solution)/shard_map/psum | solution.py:64
  177.0 1.7 multiply_reduce_fusion.4
  178.7 20.4 %psum.51 = f32[]{:T(128)} all-reduce(f32[]{:T(128)} %multiply_reduce_fusion.4), channel_id=1, replica_groups=mesh['seg'=4,'blk'=8] {'blk'}, use_global_device_ids=true, to_apply=%region_7.0 | all-reduce | flops 1 | bytes 8 | tf_op jit(solution)/shard_map/psum | solution.py:66
  199.8 9.7 %fusion.11 = f32[4,34,128,128]{3,2,1,0:T(8,128)} fusion(bf16[1,4,34,128,128]{4,3,2,1,0:T(8,128)(2,1)} %param.9, bf16[1,4,34,128,128]{4,3,2,1,0:T(8,128)(2,1)} %collective-permute-done, f32[]{:T(128)S(6)} %rsqrt.10, bf16[4,128,128]{2,1,0:T(8,128)(2,1)} %reduce-scatter.4.cloned.1.call-done, bf16[1,4,128,128]{3,2,1,0:T(8,128)(2,1)S(1)} %copy-done, f32[]{:T(128)} %div.22, ...), kind=kOutput, calls=%fused_computation.14 | convolution fusion | flops 1143865344 | bytes 18092060 | tf_op jit(solution)/shard_map/kwac,kwcd->kwad/dot_general | solution.py:54
  209.4 19.2 %scatter_custom_fusion.1 = f32[33,16384]{1,0:T(8,128)S(1)} fusion(s32[136]{0:T(256)S(1)} %reshape.74, f32[17,8,128,128]{3,2,1,0:T(8,128)} %bitcast.115, f32[]{:T(128)} %constant.11.clone.1), kind=kCustom, calls=%fused_computation.6 | custom fusion | flops 2228224 | bytes 11075588 | tf_op jit(solution)/shard_map/scatter-add | solution.py:58
  230.1 62.5 %reduce-scatter.6.cloned.1.call-done = bf16[4,128,128]{2,1,0:T(8,128)(2,1)} async-done(((bf16[32,128,128]{2,1,0:T(8,128)(2,1)}), bf16[4,128,128]{2,1,0:T(8,128)(2,1)}) %reduce-scatter.6.cloned.1.call-update) | async-done | bytes 131088 | tf_op jit(solution)/shard_map/reduce_scatter | solution.py:60
  292.6 1.7 multiply_reduce_fusion.3
  294.4 18.7 %psum.52 = f32[]{:T(128)} all-reduce(f32[]{:T(128)} %multiply_reduce_fusion.3), channel_id=1, replica_groups=mesh['seg'=4,'blk'=8] {'blk'}, use_global_device_ids=true, to_apply=%region_11.0 | all-reduce | flops 1 | bytes 8 | tf_op jit(solution)/shard_map/psum | solution.py:64
  313.7 1.8 multiply_reduce_fusion.2
  315.5 20.2 %psum.53 = f32[]{:T(128)} all-reduce(f32[]{:T(128)} %get-tuple-element.4), channel_id=1, replica_groups=mesh['seg'=4,'blk'=8] {'blk'}, use_global_device_ids=true, to_apply=%region_13.0 | all-reduce | flops 1 | bytes 8 | tf_op jit(solution)/shard_map/psum | solution.py:66
  336.4 9.6 %fusion.9 = f32[4,34,128,128]{3,2,1,0:T(8,128)} fusion(bf16[1,4,34,128,128]{4,3,2,1,0:T(8,128)(2,1)} %param.9, bf16[1,4,34,128,128]{4,3,2,1,0:T(8,128)(2,1)} %collective-permute-done, f32[4,128,128]{2,1,0:T(8,128)S(1)} %get-tuple-element.5, f32[]{:T(128)S(6)} %rsqrt.11), kind=kOutput, calls=%fused_computation.12 | convolution fusion | flops 1143209984 | bytes 18087940 | tf_op jit(solution)/shard_map/kwac,kwcd->kwad/dot_general | solution.py:54
  345.9 19.3 %scatter_custom_fusion.2 = f32[33,16384]{1,0:T(8,128)S(1)} fusion(s32[136]{0:T(256)S(1)} %reshape.74, f32[17,8,128,128]{3,2,1,0:T(8,128)} %bitcast.114, f32[]{:T(128)} %constant.11.clone.1), kind=kCustom, calls=%fused_computation.3 | custom fusion | flops 2228224 | bytes 11075588 | tf_op jit(solution)/shard_map/scatter-add | solution.py:58
  366.6 62.4 %reduce-scatter.8.cloned.1.call-done = bf16[4,128,128]{2,1,0:T(8,128)(2,1)} async-done(((bf16[32,128,128]{2,1,0:T(8,128)(2,1)}), bf16[4,128,128]{2,1,0:T(8,128)(2,1)}) %reduce-scatter.8.cloned.1.call-update) | async-done | bytes 131088 | tf_op jit(solution)/shard_map/reduce_scatter | solution.py:60
  429.0 1.7 multiply_reduce_fusion.1
  430.8 18.7 %psum.54 = f32[]{:T(128)} all-reduce(f32[]{:T(128)} %multiply_reduce_fusion.1), channel_id=1, replica_groups=mesh['seg'=4,'blk'=8] {'blk'}, use_global_device_ids=true, to_apply=%region_17.0 | all-reduce | flops 1 | bytes 8 | tf_op jit(solution)/shard_map/psum | solution.py:64
  450.1 2.5 multiply_reduce_fusion
  452.6 19.9 %psum.55 = f32[]{:T(128)} all-reduce(f32[]{:T(128)} %get-tuple-element.2), channel_id=1, replica_groups=mesh['seg'=4,'blk'=8] {'blk'}, use_global_device_ids=true, to_apply=%region_19.0 | all-reduce | flops 1 | bytes 8 | tf_op jit(solution)/shard_map/psum | solution.py:66
  (22 shorter events, 8.0 us)
Async XLA Ops:
  7.2 148.9 %reduce-scatter.4.cloned.1.call-start = ((), (), s32[]{:S(2)}) async-start(), calls=%async_computation.3 | async-start | bytes 1179648 | tf_op jit(solution)/shard_map/reduce_scatter | solution.py:60
  7.2 52.9 %collective-permute-start = (bf16[1,4,34,128,128]{4,3,2,1,0:T(8,128)(2,1)}, bf16[1,4,34,128,128]{4,3,2,1,0:T(8,128)(2,1)}, u32[]{:S(2)}, u32[]{:S(2)}) collective-permute-start(bf16[1,4,34,128,128]{4,3,2,1,0:T(8,128)(2,1)} %param.8), channel_id=1, source_target_pairs={{0,8},{8,16},{16,24},{1,9},{9,17},{17,25},{2,10},{10,18},{18,26},{... | collective-permute-start | bytes 13369352 | tf_op jit(solution)/shard_map/ppermute | solution.py:15
  89.1 67.0 %copy-start = (bf16[1,4,128,128]{3,2,1,0:T(8,128)(2,1)S(1)}, bf16[1,4,128,128]{3,2,1,0:T(8,128)(2,1)}, u32[]{:S(2)}) copy-start(bf16[1,4,128,128]{3,2,1,0:T(8,128)(2,1)} %param.7) | copy-start | bytes 393220
  89.1 67.0 %copy-start.2 = (f32[1,4]{1,0:T(1,128)S(1)}, f32[1,4]{1,0:T(1,128)}, u32[]{:S(2)}) copy-start(f32[1,4]{1,0:T(1,128)} %param.10) | copy-start | bytes 52
  90.5 202.1 %reduce-scatter.6.cloned.1.call-start = ((), (), s32[]{:S(2)}) async-start(), calls=%async_computation.4 | async-start | bytes 1179648 | tf_op jit(solution)/shard_map/reduce_scatter | solution.py:60
  228.7 63.9 %copy-start.1 = (bf16[4,128,128]{2,1,0:T(8,128)(2,1)S(1)}, bf16[4,128,128]{2,1,0:T(8,128)(2,1)}, u32[]{:S(2)}) copy-start(bf16[4,128,128]{2,1,0:T(8,128)(2,1)} %reduce-scatter.4.cloned.1.call-done) | copy-start | bytes 393220
  230.1 199.0 %reduce-scatter.8.cloned.1.call-start = ((), (), s32[]{:S(2)}) async-start(), calls=%async_computation.5 | async-start | bytes 1179648 | tf_op jit(solution)/shard_map/reduce_scatter | solution.py:60
Sparse Core Ops, SparseCore 0:
  90.6 65.4 reduce-scatter.3
  230.2 62.3 reduce-scatter.5
  366.8 62.2 reduce-scatter.7
where the time goes:
time: 489 us; the launch traced here: 481 us
  waiting for transfers between devices  219 us (45%)
  blocking collectives  135 us (28%)
  other arithmetic  71.1 us (15%)
  matrix products  28.9 us (6%)
  between operations  19.1 us (4%)
  local copies, waits for them, and re-layouts  5.48 us (1%)
    reduce_scatter x3, waiting for transfers between devices, local(): lax.psum_scatter(partial_value.astype(jnp.bfloat16), 'blk', scatter_dimen...  190 us
    psum x3, blocking collectives, local(): mean_square = lax.psum(jnp.sum(image * image), 'blk') / entries  60.4 us
    scatter-add x3, other arithmetic, local(): jax.ops.segment_sum(contrib, feeds, num_segments=all_blocks + 1)  57.8 us
    psum x3, blocking collectives, local(): coef_alpha = lax.psum(jnp.sum(vector * image), 'blk') / entries  56 us
    dot_general x3, matrix products, local(): jnp.einsum('kwac,kwcd->kwad', half_product, right_tiles, preferred_elemen...  28.9 us
    ppermute x1, waiting for transfers between devices, passed_along(): return lax.ppermute(block, axis, route)  28.5 us
    psum x1, blocking collectives, local(): start_sum = lax.psum(jnp.sum(vector * vector), 'blk')  18.6 us
  transfers between devices with their start and end apart: 4, of which 4 were waited for; matrix products, arithmetic and copies ran while one was open for 1% of the time, Pallas kernels for 0%

commit v1 on v0

v1 whole, which is shorter than its diff:
```python
import functools

import jax
import jax.numpy as jnp
from jax import lax
from jax.experimental import pallas as pl
from jax.experimental.pallas import tpu as pltpu
from jax.sharding import PartitionSpec as P

epsilon = 1e-06
F32 = jnp.float32
BF16 = jnp.bfloat16
PAD = 16
VMEM = pltpu.VMEM
SMEM = pltpu.SMEM


def passed_along(block, axis, distance):
    devices = range(lax.axis_size(axis))
    route = [(i - distance, i) for i in devices if i - distance in devices]
    return lax.ppermute(block, axis, route)


def swapped(block, mask):
    return lax.ppermute(block, "blk", [(i, i ^ mask) for i in range(lax.axis_size("blk"))])


class Plan:
    def __init__(self, tiles, channels, tile, blk):
        self.T, self.W, self.D, self.B = tiles, channels, tile, blk
        self.Z = blk // 2
        self.Ta = tiles // 2
        self.Tb = tiles - self.Ta
        self.entries = float(tiles * blk * tile * tile)
        self.n = tiles * blk
        self.wc = next(c for c in range(max(1, channels // 2), 0, -1) if channels % c == 0)

    def slots(self, feeds, me):
        device = feeds // self.T
        tile = feeds % self.T
        zr = (device // 2) ^ (me // 2)
        yr = (device % 2) ^ (me % 2)
        a = yr * (self.Z * self.Ta) + zr * self.Ta + tile
        b = 2 * self.Z * self.Ta + zr * (2 * self.Tb) + yr * self.Tb + (tile - self.Ta)
        return jnp.where(feeds >= self.n, self.n, jnp.where(tile < self.Ta, a, b)).astype(jnp.int32)


def packed_row(scalars, tile):
    lane = lax.broadcasted_iota(jnp.int32, (1, tile), 1)
    row = jnp.zeros((1, tile), F32)
    for index, value in enumerate(scalars):
        row = row + jnp.where(lane == index, value, 0.0)
    return split_row(row, tile)


def split_row(row, tile):
    high = row.astype(BF16).astype(F32)
    middle = (row - high).astype(BF16).astype(F32)
    low = row - high - middle
    at = lax.broadcasted_iota(jnp.int32, (PAD, tile), 0)
    rows = jnp.where(at == 0, high, jnp.where(at == 1, middle, jnp.where(at == 2, low, 0.0)))
    return rows.astype(BF16)


def joined_row(rows):
    rows = rows.astype(F32)
    return rows[0:1] + rows[1:2] + rows[2:3]


def total(value):
    return jnp.sum(value, keepdims=True).reshape(1, 1)


def live_mask(plan, rows_ref, cols_ref, k):
    down = lax.broadcasted_iota(jnp.int32, (plan.D, plan.D), 0)
    across = lax.broadcasted_iota(jnp.int32, (plan.D, plan.D), 1)
    return jnp.logical_and(down < rows_ref[k], across < cols_ref[k])


def received_sums(plan, arrived):
    a_parts, b_parts = arrived[: plan.Z], arrived[plan.Z :]
    D = plan.D

    def tile(k):
        if k < plan.Ta:
            parts = [p[pl.ds(k * D, D), :].astype(F32) for p in a_parts]
        else:
            parts = [p[pl.ds((k - plan.Ta) * D, D), :].astype(F32) for p in b_parts]
        return functools.reduce(lambda x, y: x + y, parts)

    level = [joined_row(p[pl.ds(plan.Ta * D, PAD), :]) for p in a_parts]
    while len(level) > 1:
        level = [level[i] + level[i + 1] for i in range(0, len(level), 2)]
    return tile, level[0]


def lane(row, index):
    return row[:, index : index + 1]


def shift_of(plan, a, b, d, e):
    alpha = a / plan.entries
    m = jnp.maximum(b - 2.0 * alpha * d + alpha * alpha * e, 0.0) / plan.entries
    return alpha, m


def update_first(plan, ins, outs, send):
    (start, rows, cols, energy), (x_out,) = ins, outs
    norm = jnp.zeros((1, 1), F32)
    for k in range(plan.T):
        at = pl.ds(k * plan.D, plan.D)
        x = jnp.where(live_mask(plan, rows, cols, k), start[at, :].astype(F32), 0.0)
        x_out[at, :] = x
        send(k, x)
        norm = norm + total(x * x)
    return [norm]


def update_second(plan, ins, outs, send):
    (x_in, rows, cols, energy), arrived = ins[:4], ins[4:]
    q_out, h_out, known_out = outs
    tile, row = received_sums(plan, arrived)
    square = lane(row, 0)
    scale = lax.rsqrt(square / plan.entries + epsilon)
    known_out[...] = jnp.broadcast_to(scale * scale * square, known_out.shape)
    a = b = jnp.zeros((1, 1), F32)
    for k in range(plan.T):
        at = pl.ds(k * plan.D, plan.D)
        x = x_in[at, :]
        image = jnp.where(live_mask(plan, rows, cols, k), tile(k), 0.0) + energy[k] * x
        q = scale * x
        h = scale * image
        q_out[at, :] = q
        h_out[at, :] = h
        send(k, h)
        a = a + total(q * h)
        b = b + total(h * h)
    return [a, b]


def update_third(plan, ins, outs, send):
    (q_in, h_in, known, rows, cols, energy), arrived = ins[:6], ins[6:]
    q_out, h_out, z_out, coef_out = outs
    tile, row = received_sums(plan, arrived)
    a, b = lane(row, 0), lane(row, 1)
    alpha, m = shift_of(plan, a, b, a, known[0:1, 0:1])
    beta, scale = jnp.sqrt(m), lax.rsqrt(m + epsilon)
    coef_out[0:1, :] = jnp.broadcast_to(alpha, (1, plan.D))
    coef_out[1:2, :] = jnp.broadcast_to(beta, (1, plan.D))
    sums = [jnp.zeros((1, 1), F32)] * 4
    for k in range(plan.T):
        at = pl.ds(k * plan.D, plan.D)
        q0, h0 = q_in[at, :], h_in[at, :]
        image = jnp.where(live_mask(plan, rows, cols, k), tile(k), 0.0) + energy[k] * h0
        q = scale * (h0 - alpha * q0)
        h = scale * (image - alpha * h0)
        z = h - beta * q0
        q_out[at, :] = q
        h_out[at, :] = h
        z_out[at, :] = z
        send(k, z)
        sums = [s + total(p) for s, p in zip(sums, (q * h, z * z, z * q, q * q))]
    return sums


def update_last(plan, ins, outs, send):
    (q_in, h_in, z_in, rows, cols, energy), arrived = ins[:6], ins[6:]
    q_out, z_out, coef_out = outs
    tile, row = received_sums(plan, arrived)
    alpha, m = shift_of(plan, *[lane(row, i) for i in range(4)])
    beta, scale = jnp.sqrt(m), lax.rsqrt(m + epsilon)
    coef_out[0:1, :] = jnp.broadcast_to(alpha, (1, plan.D))
    coef_out[1:2, :] = jnp.broadcast_to(beta, (1, plan.D))
    sums = [jnp.zeros((1, 1), F32)] * 4
    for k in range(plan.T):
        at = pl.ds(k * plan.D, plan.D)
        q1, h1, z1 = q_in[at, :], h_in[at, :], z_in[at, :]
        image = jnp.where(live_mask(plan, rows, cols, k), tile(k), 0.0) + energy[k] * z1
        q = scale * (z1 - alpha * q1)
        h = scale * (image - alpha * h1)
        z = h - beta * q1
        q_out[at, :] = q
        z_out[at, :] = z
        sums = [s + total(p) for s, p in zip(sums, (q * h, z * z, z * q, q * q))]
    return sums


def whole(shape, space=VMEM):
    return pl.BlockSpec(shape, lambda *_: (0,) * len(shape), memory_space=space)


def message_shapes(plan):
    D = plan.D
    a = jax.ShapeDtypeStruct((plan.Z * plan.Ta * D + PAD, D), BF16)
    b = jax.ShapeDtypeStruct((2 * plan.Tb * D, D), BF16)
    return [a, a] + [b] * plan.Z


def operator_step(plan, name, update, ins, spaces, state_shapes, left, right, slots):
    D, T, wc = plan.D, plan.T, plan.wc
    per_tile = plan.W // wc
    messages = message_shapes(plan)
    n_in, n_state, n_msg = len(ins), len(state_shapes), len(messages)

    def body(*refs):
        in_refs = refs[:n_in]
        left_ref, right_ref, slot_ref = refs[n_in : n_in + 3]
        state_refs = refs[n_in + 3 : n_in + 3 + n_state]
        message_refs = refs[n_in + 3 + n_state : n_in + 3 + n_state + n_msg]
        low_ref, half_ref, sum_ref = refs[n_in + 3 + n_state + n_msg :]
        step = pl.program_id(0)

        @pl.when(step == 0)
        def _():
            def send(k, value):
                low_ref[pl.ds(k * D, D), :] = value.astype(BF16)

            scalars = update(plan, in_refs, state_refs, send)
            row = packed_row(scalars, D)
            message_refs[0][pl.ds(plan.Z * plan.Ta * D, PAD), :] = row
            message_refs[1][pl.ds(plan.Z * plan.Ta * D, PAD), :] = row
            sum_ref[...] = jnp.zeros(sum_ref.shape, F32)

        tile = step // per_tile
        low = low_ref[pl.ds(pl.multiple_of(tile * D, D), D), :]
        half_ref[...] = jnp.dot(left_ref[...], low, preferred_element_type=F32).astype(BF16)
        for w in range(wc):
            product = jnp.dot(
                half_ref[pl.ds(w * D, D), :],
                right_ref[pl.ds(w * D, D), :],
                preferred_element_type=F32,
            )
            slot = slot_ref[step * wc + w]
            at = pl.ds(pl.multiple_of(slot * D, D), D)
            sum_ref[at, :] += product

        @pl.when(step == T * per_tile - 1)
        def _():
            first = 0
            for ref in message_refs:
                rows = ref.shape[0] // D * D
                ref[pl.ds(0, rows), :] = sum_ref[pl.ds(first, rows), :].astype(BF16)
                first += rows

    stream = pl.BlockSpec((wc * D, D), lambda i: (i, 0))
    outs = list(state_shapes) + messages
    results = pl.pallas_call(
        body,
        grid=(T * per_tile,),
        in_specs=[whole(x.shape, s) for x, s in zip(ins, spaces)]
        + [stream, stream, whole(slots.shape, SMEM)],
        out_specs=[whole(s.shape) for s in outs],
        out_shape=outs,
        scratch_shapes=[
            VMEM((T * D, D), BF16),
            VMEM((wc * D, D), BF16),
            VMEM(((plan.n + 1) * D, D), F32),
        ],
        name=name,
    )(*ins, left, right, slots)
    return results[:n_state], results[n_state:]


def last_step(plan, ins, spaces, state_shapes):
    n_in = len(ins)
    row = jax.ShapeDtypeStruct((8, plan.D), F32)

    def body(*refs):
        outs = refs[n_in:-1]
        sums = update_last(plan, refs[:n_in], outs, None)
        across = lax.broadcasted_iota(jnp.int32, (8, plan.D), 1)
        packed = jnp.zeros((8, plan.D), F32)
        for index, value in enumerate(sums):
            packed = packed + jnp.where(across == index, value, 0.0)
        refs[-1][...] = packed

    outs = list(state_shapes) + [row]
    return pl.pallas_call(
        body,
        in_specs=[whole(x.shape, s) for x, s in zip(ins, spaces)],
        out_specs=[whole(s.shape) for s in outs],
        out_shape=outs,
        name="last_step",
    )(*ins)


def middle_a(plan, keep, got):
    rows = plan.Ta * plan.D

    def body(keep_ref, got_ref, *outs):
        end = pl.ds(plan.Z * rows, PAD)
        scalars = split_row(joined_row(keep_ref[end, :]) + joined_row(got_ref[end, :]), plan.D)
        for z, out in enumerate(outs):
            at = pl.ds(z * rows, rows)
            added = keep_ref[at, :].astype(F32) + got_ref[at, :].astype(F32)
            out[pl.ds(0, rows), :] = added.astype(BF16)
            out[pl.ds(rows, PAD), :] = scalars

    shape = jax.ShapeDtypeStruct((rows + PAD, plan.D), BF16)
    return pl.pallas_call(
        body,
        in_specs=[whole(keep.shape)] * 2,
        out_specs=[whole(shape.shape)] * plan.Z,
        out_shape=[shape] * plan.Z,
        name="middle_a",
    )(keep, got)


def middle_b(plan, parts):
    rows = plan.Tb * plan.D

    def body(*refs):
        outs = refs[plan.Z :]
        for y, out in enumerate(outs):
            at = pl.ds(y * rows, rows)
            added = functools.reduce(
                lambda x, z: x + z, [p[at, :].astype(F32) for p in refs[: plan.Z]]
            )
            out[...] = added.astype(out.dtype)

    shapes = [jax.ShapeDtypeStruct((rows, plan.D), d) for d in (F32, BF16)]
    return pl.pallas_call(
        body,
        in_specs=[whole(parts[0].shape)] * plan.Z,
        out_specs=[whole(s.shape) for s in shapes],
        out_shape=shapes,
        name="middle_b",
    )(*parts)


def exchanged(plan, messages):
    a_keep, a_send = messages[:2]
    b_parts = messages[2:]
    others = range(plan.Z - 1, 0, -1)
    a_got = swapped(a_send, 1)
    b_got = [swapped(b_parts[z], 2 * z) for z in others]
    a_parts = middle_a(plan, a_keep, a_got)
    a_last = [swapped(a_parts[z], 2 * z) for z in others][::-1]
    b_keep, b_send = middle_b(plan, [b_parts[0]] + b_got)
    b_last = swapped(b_send, 1)
    return [a_parts[0]] + a_last + [b_keep, b_last]


def local(
    start_vector,
    left_environment,
    right_environment,
    block_energy,
    sector_rows,
    sector_cols,
    feed_block,
):
    T, W, D = left_environment.shape[1:4]
    plan = Plan(T, W, D, lax.axis_size("blk"))
    left = passed_along(left_environment, "seg", 1).reshape(T * W * D, D)
    right = right_environment.reshape(T * W * D, D)
    slots = plan.slots(feed_block.reshape(T * W), lax.axis_index("blk"))
    sizes = [sector_rows[0], sector_cols[0], block_energy[0]]
    scalar = [SMEM] * 3
    vector = jax.ShapeDtypeStruct((T * D, D), F32)
    row = jax.ShapeDtypeStruct((8, D), F32)
    start = start_vector.reshape(T * D, D)

    (x,), messages = operator_step(
        plan, "step_0", update_first, [start] + sizes, [VMEM] + scalar, [vector], left, right, slots
    )
    arrived = exchanged(plan, messages)
    (q0, h0, known), messages = operator_step(
        plan,
        "step_1",
        update_second,
        [x] + sizes + arrived,
        [VMEM] + scalar + [VMEM] * len(arrived),
        [vector, vector, row],
        left,
        right,
        slots,
    )
    arrived = exchanged(plan, messages)
    (q1, h1, z1, first), messages = operator_step(
        plan,
        "step_2",
        update_third,
        [q0, h0, known] + sizes + arrived,
        [VMEM] * 3 + scalar + [VMEM] * len(arrived),
        [vector, vector, vector, row],
        left,
        right,
        slots,
    )
    arrived = exchanged(plan, messages)
    q2, z2, second, sums = last_step(
        plan,
        [q1, h1, z1] + sizes + arrived,
        [VMEM] * 3 + scalar + [VMEM] * len(arrived),
        [vector, vector, row],
    )
    mask = 1
    while mask < plan.B:
        sums = sums + swapped(sums, mask)
        mask *= 2
    alpha, m = shift_of(plan, *[sums[0, i] for i in range(4)])
    residual = z2 - alpha * q2
    coefficients = jnp.stack(
        [first[0, 0], second[0, 0], alpha, first[1, 0], second[1, 0], jnp.sqrt(m)]
    )
    return (coefficients[None, :], residual.reshape(1, T, D, D))


def solution(mesh):
    return jax.shard_map(
        local,
        mesh=mesh,
        in_specs=(
            P("seg", "blk", None, None),
            P("seg", "blk", None, None, None),
            P("seg", "blk", None, None, None),
            P("seg", "blk"),
            P("seg", "blk"),
            P("seg", "blk"),
            P("seg", "blk", None),
        ),
        out_specs=(P("seg", None), P("seg", "blk", None, None)),
        check_vma=False,
    )
```

time: 489 us -> 176 us (0.36); the launches traced: 481 us -> 175 us
  waiting for transfers between devices: 219 us -> 74.1 us
  blocking collectives: 135 us -> 0 us
  other arithmetic: 71.1 us -> 3.05 us
  Pallas kernels: 0 us -> 44.7 us
  starting transfers between devices: 2.04 us -> 34.3 us
  matrix products: 28.9 us -> 0 us
  between operations: 19.1 us -> 5.47 us
  local copies, waits for them, and re-layouts: 5.48 us -> 13.5 us
    reduce_scatter x3 -> x0, waiting for transfers between devices: 190 us -> none  [local(): lax.psum_scatter(partial_value.astype(jnp.bfloat16), 'blk', scatter_dimen...]
    psum x7 -> x0, blocking collectives: 135 us -> none  [the longest x3 60.4 us: local(): mean_square = lax.psum(jnp.sum(image * image), 'blk') / entries]
    scatter-add x3 -> x0, other arithmetic: 57.8 us -> none  [local(): jax.ops.segment_sum(contrib, feeds, num_segments=all_blocks + 1)]
    pallas_call x0 -> x10, Pallas kernels: none -> 44.7 us  [the longest x3 31.4 us: operator_step(): pl.pallas_call(body, grid=(T * per_tile,), in_specs=[whole(x.shape, s) fo...]
    ppermute x0 -> x27, starting transfers between devices: none -> 32.4 us  [swapped(): lax.ppermute(block, 'blk', [(i, i ^ mask) for i in range(lax.axis_size('b...]
    dot_general x3 -> x0, matrix products: 28.9 us -> none  [local(): jnp.einsum('kwac,kwcd->kwad', half_product, right_tiles, preferred_elemen...]
    ppermute x0 -> x27, waiting for transfers between devices: none -> 24.5 us  [swapped(): lax.ppermute(block, 'blk', [(i, i ^ mask) for i in range(lax.axis_size('b...]
    ppermute x1, waiting for transfers between devices: 28.5 us -> 49.6 us  [passed_along(): return lax.ppermute(block, axis, route)]
  transfers between devices with their start and end apart: 4 -> 28, of which waited for: 4 -> 10; matrix products, arithmetic and copies ran while one was open for 1% -> 2% of each run, Pallas kernels for 0% -> 6%
where the time goes in v1:
time: 176 us; the launch traced here: 175 us
  waiting for transfers between devices  74.1 us (42%)
  Pallas kernels  44.7 us (25%)
  starting transfers between devices  34.3 us (19%)
  local copies, waits for them, and re-layouts  13.5 us (8%)
  between operations  5.47 us (3%)
  other arithmetic  3.05 us (2%)
    ppermute x1, waiting for transfers between devices, passed_along(): return lax.ppermute(block, axis, route)  49.6 us
    ppermute x27, starting transfers between devices, swapped(): lax.ppermute(block, 'blk', [(i, i ^ mask) for i in range(lax.axis_size('b...  32.4 us
    pallas_call x3, Pallas kernels, operator_step(): pl.pallas_call(body, grid=(T * per_tile,), in_specs=[whole(x.shape, s) fo...  31.4 us
    ppermute x27, waiting for transfers between devices, swapped(): lax.ppermute(block, 'blk', [(i, i ^ mask) for i in range(lax.axis_size('b...  24.5 us
    unnamed x48, local copies, waits for them, and re-layouts  6.24 us
    pallas_call x3, Pallas kernels, middle_b(): pl.pallas_call(body, in_specs=[whole(parts[0].shape)] * plan.Z, out_specs...  5.41 us
    pallas_call x3, Pallas kernels, middle_a(): pl.pallas_call(body, in_specs=[whole(keep.shape)] * 2, out_specs=[whole(s...  5.37 us
  transfers between devices with their start and end apart: 28, of which 10 were waited for; matrix products, arithmetic and copies ran while one was open for 2% of the time, Pallas kernels for 6%

profile of v1, /device:TPU:6, one launch (start us, length us, event | category | flops | bytes accessed | tf_op | source)
XLA Modules:
  0.0 175.0 jit_solution(15946843007032754522)
XLA Ops:
  0.6 1.9 %collective-permute-start = (bf16[1,4,34,128,128]{4,3,2,1,0:T(8,128)(2,1)}, bf16[1,4,34,128,128]{4,3,2,1,0:T(8,128)(2,1)}, u32[]{:S(2)}, u32[]{:S(2)}) collective-permute-start(bf16[1,4,34,128,128]{4,3,2,1,0:T(8,128)(2,1)} %param.8), channel_id=1, source_target_pairs={{0,8},{8,16},{16,24},{1,9},{9,17},{17,25},{2,10},{10,18},{18,26},{... | collective-permute-start | bytes 13369352 | tf_op jit(solution)/shard_map/ppermute | solution.py:21
  3.9 49.6 %collective-permute-done = bf16[1,4,34,128,128]{4,3,2,1,0:T(8,128)(2,1)} collective-permute-done((bf16[1,4,34,128,128]{4,3,2,1,0:T(8,128)(2,1)}, bf16[1,4,34,128,128]{4,3,2,1,0:T(8,128)(2,1)}, u32[]{:S(2)}, u32[]{:S(2)}) %collective-permute-start) | collective-permute-done | bytes 4456480 | tf_op jit(solution)/shard_map/ppermute | solution.py:21
  53.6 10.0 %step_0.1 = (f32[512,128]{1,0:T(8,128)}, bf16[1040,128]{1,0:T(8,128)(2,1)}, bf16[1040,128]{1,0:T(8,128)(2,1)}, bf16[512,128]{1,0:T(8,128)(2,1)}, bf16[512,128]{1...) custom-call(bf16[512,128]{1,0:T(8,128)(2,1)} %bitcast.19, s32[4]{0:T(128)} %bitcast.20, s32[4]{0:T(128)} %bitcast.24, ...), custom_call_target="tpu_custom_call" | custom-call | tf_op jit(solution)/shard_map/step_0/pallas_call | solution.py:247
  64.1 3.6 %collective-permute-start.5 = (bf16[512,128]{1,0:T(8,128)(2,1)}, bf16[512,128]{1,0:T(8,128)(2,1)S(1)}, u32[]{:S(2)}, u32[]{:S(2)}) collective-permute-start(bf16[512,128]{1,0:T(8,128)(2,1)} %get-tuple-element.58), channel_id=1, source_target_pairs={{0,6},{1,7},{2,4},{3,5},{4,2},{5,3},{6,0},{7,1},{8,14},{9,15},{10,... | collective-permute-start | bytes 393224 | tf_op jit(solution)/shard_map/ppermute | solution.py:25
  68.5 1.9 %collective-permute-done.1.got_ref = bf16[1040,128]{1,0:T(8,128)(2,1)S(1)} collective-permute-done((bf16[1040,128]{1,0:T(8,128)(2,1)}, bf16[1040,128]{1,0:T(8,128)(2,1)S(1)}, u32[]{:S(2)}, u32[]{:S(2)}) %collective-permute-start.1) | collective-permute-done | bytes 266272 | tf_op jit(solution)/shard_map/ppermute | solution.py:25
  74.3 2.7 %collective-permute-start.3 = (bf16[272,128]{1,0:T(8,128)(2,1)}, bf16[272,128]{1,0:T(8,128)(2,1)S(1)}, u32[]{:S(2)}, u32[]{:S(2)}) collective-permute-start(bf16[272,128]{1,0:T(8,128)(2,1)} %get-tuple-element.55), channel_id=1, source_target_pairs={{0,4},{1,5},{2,6},{3,7},{4,0},{5,1},{6,2},{7,3},{8,12},{9,13},{10,... | collective-permute-start | bytes 208904 | tf_op jit(solution)/shard_map/ppermute | solution.py:25
  78.0 1.8 %middle_b.3 = (f32[256,128]{1,0:T(8,128)}, bf16[256,128]{1,0:T(8,128)(2,1)}) custom-call(bf16[512,128]{1,0:T(8,128)(2,1)} %get-tuple-element.57.refs_0_, bf16[512,128]{1,0:T(8,128)(2,1)} %copy-done.3, bf16[512,128]{1,0:T(8,128)(2,1)} %copy-done.6, bf16[512,128]{1,0:T(8,128)(2,1)} %copy-done.9), custom_call_target="tpu_custom_call" | custom-call | tf_op jit(solution)/shard_map/middle_b/pallas_call | solution.py:322
  80.4 4.7 %collective-permute-done.8.refs_9_ = bf16[256,128]{1,0:T(8,128)(2,1)S(1)} collective-permute-done((bf16[256,128]{1,0:T(8,128)(2,1)}, bf16[256,128]{1,0:T(8,128)(2,1)S(1)}, u32[]{:S(2)}, u32[]{:S(2)}) %collective-permute-start.8) | collective-permute-done | bytes 65568 | tf_op jit(solution)/shard_map/ppermute | solution.py:25
  85.7 10.5 %step_1.1 = (f32[512,128]{1,0:T(8,128)}, f32[512,128]{1,0:T(8,128)}, f32[8,128]{1,0:T(8,128)}, bf16[1040,128]{1,0:T(8,128)(2,1)}, bf16[1040,128]{1,0:T(8,128)(2,...) custom-call(f32[512,128]{1,0:T(8,128)} %get-tuple-element.50.refs_0_, ...), custom_call_target="tpu_custom_call" | custom-call | tf_op jit(solution)/shard_map/step_1/pallas_call | solution.py:247
  96.8 3.5 %collective-permute-start.13 = (bf16[512,128]{1,0:T(8,128)(2,1)}, bf16[512,128]{1,0:T(8,128)(2,1)S(1)}, u32[]{:S(2)}, u32[]{:S(2)}) collective-permute-start(bf16[512,128]{1,0:T(8,128)(2,1)} %get-tuple-element.73), channel_id=1, source_target_pairs={{0,6},{1,7},{2,4},{3,5},{4,2},{5,3},{6,0},{7,1},{8,14},{9,15},{10,... | collective-permute-start | bytes 393224 | tf_op jit(solution)/shard_map/ppermute | solution.py:25
  105.9 3.6 %collective-permute-start.11 = (bf16[272,128]{1,0:T(8,128)(2,1)}, bf16[272,128]{1,0:T(8,128)(2,1)S(1)}, u32[]{:S(2)}, u32[]{:S(2)}) collective-permute-start(bf16[272,128]{1,0:T(8,128)(2,1)} %get-tuple-element.70), channel_id=1, source_target_pairs={{0,4},{1,5},{2,6},{3,7},{4,0},{5,1},{6,2},{7,3},{8,12},{9,13},{10,... | collective-permute-start | bytes 208904 | tf_op jit(solution)/shard_map/ppermute | solution.py:25
  110.6 1.8 %middle_b.4 = (f32[256,128]{1,0:T(8,128)}, bf16[256,128]{1,0:T(8,128)(2,1)}) custom-call(bf16[512,128]{1,0:T(8,128)(2,1)} %get-tuple-element.72.refs_0_, bf16[512,128]{1,0:T(8,128)(2,1)} %copy-done.4, bf16[512,128]{1,0:T(8,128)(2,1)} %copy-done.7, bf16[512,128]{1,0:T(8,128)(2,1)} %copy-done.10), custom_call_target="tpu_custom_call" | custom-call | tf_op jit(solution)/shard_map/middle_b/pallas_call | solution.py:322
  112.9 4.0 %collective-permute-done.16.refs_11_ = bf16[256,128]{1,0:T(8,128)(2,1)S(1)} collective-permute-done((bf16[256,128]{1,0:T(8,128)(2,1)}, bf16[256,128]{1,0:T(8,128)(2,1)S(1)}, u32[]{:S(2)}, u32[]{:S(2)}) %collective-permute-start.16) | collective-permute-done | bytes 65568 | tf_op jit(solution)/shard_map/ppermute | solution.py:25
  117.6 10.9 %step_2.1 = (f32[512,128]{1,0:T(8,128)}, f32[512,128]{1,0:T(8,128)}, f32[512,128]{1,0:T(8,128)}, f32[8,128]{1,0:T(8,128)}, bf16[1040,128]{1,0:T(8,128)(2,1)}, /*...) custom-call(f32[512,128]{1,0:T(8,128)} %get-tuple-element.63.refs_0_, ...), custom_call_target="tpu_custom_call" | custom-call | tf_op jit(solution)/shard_map/step_2/pallas_call | solution.py:247
  129.0 3.5 %collective-permute-start.21 = (bf16[512,128]{1,0:T(8,128)(2,1)}, bf16[512,128]{1,0:T(8,128)(2,1)S(1)}, u32[]{:S(2)}, u32[]{:S(2)}) collective-permute-start(bf16[512,128]{1,0:T(8,128)(2,1)} %get-tuple-element.89), channel_id=1, source_target_pairs={{0,6},{1,7},{2,4},{3,5},{4,2},{5,3},{6,0},{7,1},{8,14},{9,15},{10,... | collective-permute-start | bytes 393224 | tf_op jit(solution)/shard_map/ppermute | solution.py:25
  135.8 1.8 %middle_a.5 = (bf16[272,128]{1,0:T(8,128)(2,1)}, bf16[272,128]{1,0:T(8,128)(2,1)}, bf16[272,128]{1,0:T(8,128)(2,1)}, bf16[272,128]{1,0:T(8,128)(2,1)}) custom-call(bf16[1040,128]{1,0:T(8,128)(2,1)} %get-tuple-element.82.keep_ref, bf16[1040,128]{1,0:T(8,128)(2,1)} %copy-done.2), custom_call_target="tpu_custom_call" | custom-call | tf_op jit(solution)/shard_map/middle_a/pallas_call | solution.py:300
  138.0 3.8 %collective-permute-start.19 = (bf16[272,128]{1,0:T(8,128)(2,1)}, bf16[272,128]{1,0:T(8,128)(2,1)S(1)}, u32[]{:S(2)}, u32[]{:S(2)}) collective-permute-start(bf16[272,128]{1,0:T(8,128)(2,1)} %get-tuple-element.86), channel_id=1, source_target_pairs={{0,4},{1,5},{2,6},{3,7},{4,0},{5,1},{6,2},{7,3},{8,12},{9,13},{10,... | collective-permute-start | bytes 208904 | tf_op jit(solution)/shard_map/ppermute | solution.py:25
  142.8 1.8 %middle_b.5 = (f32[256,128]{1,0:T(8,128)}, bf16[256,128]{1,0:T(8,128)(2,1)}) custom-call(bf16[512,128]{1,0:T(8,128)(2,1)} %get-tuple-element.88.refs_0_, bf16[512,128]{1,0:T(8,128)(2,1)} %copy-done.5, bf16[512,128]{1,0:T(8,128)(2,1)} %copy-done.8, bf16[512,128]{1,0:T(8,128)(2,1)} %copy-done.11), custom_call_target="tpu_custom_call" | custom-call | tf_op jit(solution)/shard_map/middle_b/pallas_call | solution.py:322
  145.1 4.0 %collective-permute-done.24.refs_11_ = bf16[256,128]{1,0:T(8,128)(2,1)S(1)} collective-permute-done((bf16[256,128]{1,0:T(8,128)(2,1)}, bf16[256,128]{1,0:T(8,128)(2,1)S(1)}, u32[]{:S(2)}, u32[]{:S(2)}) %collective-permute-start.24) | collective-permute-done | bytes 65568 | tf_op jit(solution)/shard_map/ppermute | solution.py:25
  149.7 2.5 %last_step.1 = (f32[512,128]{1,0:T(8,128)}, f32[512,128]{1,0:T(8,128)}, f32[8,128]{1,0:T(8,128)}, f32[8,128]{1,0:T(8,128)}) custom-call(f32[512,128]{1,0:T(8,128)} %get-tuple-element.79.refs_0_, f32[512,128]{1,0:T(8,128)} %get-tuple-element.80.refs_1_, f32[512,128]{1,0:T(8,128)} %get-tuple-element.81.refs_2_, s32[4]{0:T(128)} %bitcast.23, s32[4]{0:T(128)} %bitcast.27, ...), custom_call_target="tpu_custom_call" | custom-call | tf_op jit(solution)/shard_map/last_step/pallas_call | solution.py:278
  152.7 3.3 %collective-permute-done.25 = f32[8,128]{1,0:T(8,128)S(1)} collective-permute-done((f32[8,128]{1,0:T(8,128)}, f32[8,128]{1,0:T(8,128)S(1)}, u32[]{:S(2)}, u32[]{:S(2)}) %collective-permute-start.25) | collective-permute-done | bytes 4128 | tf_op jit(solution)/shard_map/ppermute | solution.py:25
  158.4 1.9 %collective-permute-done.26 = f32[8,128]{1,0:T(8,128)S(1)} collective-permute-done((f32[8,128]{1,0:T(8,128)S(1)}, f32[8,128]{1,0:T(8,128)S(1)}, u32[]{:S(2)}, u32[]{:S(2)}) %collective-permute-start.26) | collective-permute-done | bytes 4128 | tf_op jit(solution)/shard_map/ppermute | solution.py:25
  160.3 2.1 %collective-permute-start.27 = (f32[8,128]{1,0:T(8,128)S(1)}, f32[8,128]{1,0:T(8,128)S(1)}, u32[]{:S(2)}, u32[]{:S(2)}) collective-permute-start(f32[8,128]{1,0:T(8,128)S(1)} %add.61), channel_id=1, source_target_pairs={{0,4},{1,5},{2,6},{3,7},{4,0},{5,1},{6,2},{7,3},{8,12},{9,13},{10,... | collective-permute-start | bytes 12296 | tf_op jit(solution)/shard_map/ppermute | solution.py:25
  171.9 3.2 %stack.11 = f32[6]{0:T(128)} concatenate(f32[1]{0:T(128)} %bitcast.6, f32[1]{0:T(128)} %bitcast.7, f32[1]{0:T(128)} %bitcast.8, f32[1]{0:T(128)} %bitcast.9, f32[1]{0:T(128)} %bitcast.10, f32[1]{0:T(128)} %bitcast.11), dimensions={0} | concatenate | bytes 48 | tf_op jit(solution)/shard_map/stack | solution.py:404
  (100 shorter events, 31.2 us)
Async XLA Ops:
  0.6 52.9 %collective-permute-start = (bf16[1,4,34,128,128]{4,3,2,1,0:T(8,128)(2,1)}, bf16[1,4,34,128,128]{4,3,2,1,0:T(8,128)(2,1)}, u32[]{:S(2)}, u32[]{:S(2)}) collective-permute-start(bf16[1,4,34,128,128]{4,3,2,1,0:T(8,128)(2,1)} %param.8), channel_id=1, source_target_pairs={{0,8},{8,16},{16,24},{1,9},{9,17},{17,25},{2,10},{10,18},{18,26},{... | collective-permute-start | bytes 13369352 | tf_op jit(solution)/shard_map/ppermute | solution.py:21
  63.6 6.9 %collective-permute-start.1 = (bf16[1040,128]{1,0:T(8,128)(2,1)}, bf16[1040,128]{1,0:T(8,128)(2,1)S(1)}, u32[]{:S(2)}, u32[]{:S(2)}) collective-permute-start(bf16[1040,128]{1,0:T(8,128)(2,1)} %get-tuple-element.52), channel_id=1, source_target_pairs={{0,1},{1,0},{2,3},{3,2},{4,5},{5,4},{6,7},{7,6},{8,9},{9,8},{10,11... | collective-permute-start | bytes 798728 | tf_op jit(solution)/shard_map/ppermute | solution.py:25
  64.1 12.9 %collective-permute-start.5 = (bf16[512,128]{1,0:T(8,128)(2,1)}, bf16[512,128]{1,0:T(8,128)(2,1)S(1)}, u32[]{:S(2)}, u32[]{:S(2)}) collective-permute-start(bf16[512,128]{1,0:T(8,128)(2,1)} %get-tuple-element.58), channel_id=1, source_target_pairs={{0,6},{1,7},{2,4},{3,5},{4,2},{5,3},{6,0},{7,1},{8,14},{9,15},{10,... | collective-permute-start | bytes 393224 | tf_op jit(solution)/shard_map/ppermute | solution.py:25
  67.7 9.6 %collective-permute-start.6 = (bf16[512,128]{1,0:T(8,128)(2,1)}, bf16[512,128]{1,0:T(8,128)(2,1)S(1)}, u32[]{:S(2)}, u32[]{:S(2)}) collective-permute-start(bf16[512,128]{1,0:T(8,128)(2,1)} %get-tuple-element.59), channel_id=1, source_target_pairs={{0,4},{1,5},{2,6},{3,7},{4,0},{5,1},{6,2},{7,3},{8,12},{9,13},{10,... | collective-permute-start | bytes 393224 | tf_op jit(solution)/shard_map/ppermute | solution.py:25
  67.7 9.6 %collective-permute-start.7 = (bf16[512,128]{1,0:T(8,128)(2,1)}, bf16[512,128]{1,0:T(8,128)(2,1)S(1)}, u32[]{:S(2)}, u32[]{:S(2)}) collective-permute-start(bf16[512,128]{1,0:T(8,128)(2,1)} %get-tuple-element.60), channel_id=1, source_target_pairs={{0,2},{1,3},{2,0},{3,1},{4,6},{5,7},{6,4},{7,5},{8,10},{9,11},{10,... | collective-permute-start | bytes 393224 | tf_op jit(solution)/shard_map/ppermute | solution.py:25
  72.9 12.1 %collective-permute-start.2 = (bf16[272,128]{1,0:T(8,128)(2,1)}, bf16[272,128]{1,0:T(8,128)(2,1)S(1)}, u32[]{:S(2)}, u32[]{:S(2)}) collective-permute-start(bf16[272,128]{1,0:T(8,128)(2,1)} %get-tuple-element.54), channel_id=1, source_target_pairs={{0,2},{1,3},{2,0},{3,1},{4,6},{5,7},{6,4},{7,5},{8,10},{9,11},{10,... | collective-permute-start | bytes 208904 | tf_op jit(solution)/shard_map/ppermute | solution.py:25
  74.3 10.7 %collective-permute-start.3 = (bf16[272,128]{1,0:T(8,128)(2,1)}, bf16[272,128]{1,0:T(8,128)(2,1)S(1)}, u32[]{:S(2)}, u32[]{:S(2)}) collective-permute-start(bf16[272,128]{1,0:T(8,128)(2,1)} %get-tuple-element.55), channel_id=1, source_target_pairs={{0,4},{1,5},{2,6},{3,7},{4,0},{5,1},{6,2},{7,3},{8,12},{9,13},{10,... | collective-permute-start | bytes 208904 | tf_op jit(solution)/shard_map/ppermute | solution.py:25
  77.0 8.0 %collective-permute-start.4 = (bf16[272,128]{1,0:T(8,128)(2,1)}, bf16[272,128]{1,0:T(8,128)(2,1)S(1)}, u32[]{:S(2)}, u32[]{:S(2)}) collective-permute-start(bf16[272,128]{1,0:T(8,128)(2,1)} %get-tuple-element.56), channel_id=1, source_target_pairs={{0,6},{1,7},{2,4},{3,5},{4,2},{5,3},{6,0},{7,1},{8,14},{9,15},{10,... | collective-permute-start | bytes 208904 | tf_op jit(solution)/shard_map/ppermute | solution.py:25
  79.8 5.2 %collective-permute-start.8 = (bf16[256,128]{1,0:T(8,128)(2,1)}, bf16[256,128]{1,0:T(8,128)(2,1)S(1)}, u32[]{:S(2)}, u32[]{:S(2)}) collective-permute-start(bf16[256,128]{1,0:T(8,128)(2,1)} %get-tuple-element.62), channel_id=1, source_target_pairs={{0,1},{1,0},{2,3},{3,2},{4,5},{5,4},{6,7},{7,6},{8,9},{9,8},{10,11... | collective-permute-start | bytes 196616 | tf_op jit(solution)/shard_map/ppermute | solution.py:25
  96.3 6.7 %collective-permute-start.9 = (bf16[1040,128]{1,0:T(8,128)(2,1)}, bf16[1040,128]{1,0:T(8,128)(2,1)S(1)}, u32[]{:S(2)}, u32[]{:S(2)}) collective-permute-start(bf16[1040,128]{1,0:T(8,128)(2,1)} %get-tuple-element.67), channel_id=1, source_target_pairs={{0,1},{1,0},{2,3},{3,2},{4,5},{5,4},{6,7},{7,6},{8,9},{9,8},{10,11... | collective-permute-start | bytes 798728 | tf_op jit(solution)/shard_map/ppermute | solution.py:25
  96.8 12.7 %collective-permute-start.13 = (bf16[512,128]{1,0:T(8,128)(2,1)}, bf16[512,128]{1,0:T(8,128)(2,1)S(1)}, u32[]{:S(2)}, u32[]{:S(2)}) collective-permute-start(bf16[512,128]{1,0:T(8,128)(2,1)} %get-tuple-element.73), channel_id=1, source_target_pairs={{0,6},{1,7},{2,4},{3,5},{4,2},{5,3},{6,0},{7,1},{8,14},{9,15},{10,... | collective-permute-start | bytes 393224 | tf_op jit(solution)/shard_map/ppermute | solution.py:25
  100.3 9.5 %collective-permute-start.14 = (bf16[512,128]{1,0:T(8,128)(2,1)}, bf16[512,128]{1,0:T(8,128)(2,1)S(1)}, u32[]{:S(2)}, u32[]{:S(2)}) collective-permute-start(bf16[512,128]{1,0:T(8,128)(2,1)} %get-tuple-element.74), channel_id=1, source_target_pairs={{0,4},{1,5},{2,6},{3,7},{4,0},{5,1},{6,2},{7,3},{8,12},{9,13},{10,... | collective-permute-start | bytes 393224 | tf_op jit(solution)/shard_map/ppermute | solution.py:25
  100.3 9.5 %collective-permute-start.15 = (bf16[512,128]{1,0:T(8,128)(2,1)}, bf16[512,128]{1,0:T(8,128)(2,1)S(1)}, u32[]{:S(2)}, u32[]{:S(2)}) collective-permute-start(bf16[512,128]{1,0:T(8,128)(2,1)} %get-tuple-element.75), channel_id=1, source_target_pairs={{0,2},{1,3},{2,0},{3,1},{4,6},{5,7},{6,4},{7,5},{8,10},{9,11},{10,... | collective-permute-start | bytes 393224 | tf_op jit(solution)/shard_map/ppermute | solution.py:25
  105.5 11.4 %collective-permute-start.10 = (bf16[272,128]{1,0:T(8,128)(2,1)}, bf16[272,128]{1,0:T(8,128)(2,1)S(1)}, u32[]{:S(2)}, u32[]{:S(2)}) collective-permute-start(bf16[272,128]{1,0:T(8,128)(2,1)} %get-tuple-element.69), channel_id=1, source_target_pairs={{0,2},{1,3},{2,0},{3,1},{4,6},{5,7},{6,4},{7,5},{8,10},{9,11},{10,... | collective-permute-start | bytes 208904 | tf_op jit(solution)/shard_map/ppermute | solution.py:25
  105.9 10.9 %collective-permute-start.11 = (bf16[272,128]{1,0:T(8,128)(2,1)}, bf16[272,128]{1,0:T(8,128)(2,1)S(1)}, u32[]{:S(2)}, u32[]{:S(2)}) collective-permute-start(bf16[272,128]{1,0:T(8,128)(2,1)} %get-tuple-element.70), channel_id=1, source_target_pairs={{0,4},{1,5},{2,6},{3,7},{4,0},{5,1},{6,2},{7,3},{8,12},{9,13},{10,... | collective-permute-start | bytes 208904 | tf_op jit(solution)/shard_map/ppermute | solution.py:25
  109.5 7.3 %collective-permute-start.12 = (bf16[272,128]{1,0:T(8,128)(2,1)}, bf16[272,128]{1,0:T(8,128)(2,1)S(1)}, u32[]{:S(2)}, u32[]{:S(2)}) collective-permute-start(bf16[272,128]{1,0:T(8,128)(2,1)} %get-tuple-element.71), channel_id=1, source_target_pairs={{0,6},{1,7},{2,4},{3,5},{4,2},{5,3},{6,0},{7,1},{8,14},{9,15},{10,... | collective-permute-start | bytes 208904 | tf_op jit(solution)/shard_map/ppermute | solution.py:25
  128.4 6.7 %collective-permute-start.17 = (bf16[1040,128]{1,0:T(8,128)(2,1)}, bf16[1040,128]{1,0:T(8,128)(2,1)S(1)}, u32[]{:S(2)}, u32[]{:S(2)}) collective-permute-start(bf16[1040,128]{1,0:T(8,128)(2,1)} %get-tuple-element.83), channel_id=1, source_target_pairs={{0,1},{1,0},{2,3},{3,2},{4,5},{5,4},{6,7},{7,6},{8,9},{9,8},{10,11... | collective-permute-start | bytes 798728 | tf_op jit(solution)/shard_map/ppermute | solution.py:25
  129.0 12.7 %collective-permute-start.21 = (bf16[512,128]{1,0:T(8,128)(2,1)}, bf16[512,128]{1,0:T(8,128)(2,1)S(1)}, u32[]{:S(2)}, u32[]{:S(2)}) collective-permute-start(bf16[512,128]{1,0:T(8,128)(2,1)} %get-tuple-element.89), channel_id=1, source_target_pairs={{0,6},{1,7},{2,4},{3,5},{4,2},{5,3},{6,0},{7,1},{8,14},{9,15},{10,... | collective-permute-start | bytes 393224 | tf_op jit(solution)/shard_map/ppermute | solution.py:25
  132.5 9.5 %collective-permute-start.22 = (bf16[512,128]{1,0:T(8,128)(2,1)}, bf16[512,128]{1,0:T(8,128)(2,1)S(1)}, u32[]{:S(2)}, u32[]{:S(2)}) collective-permute-start(bf16[512,128]{1,0:T(8,128)(2,1)} %get-tuple-element.90), channel_id=1, source_target_pairs={{0,4},{1,5},{2,6},{3,7},{4,0},{5,1},{6,2},{7,3},{8,12},{9,13},{10,... | collective-permute-start | bytes 393224 | tf_op jit(solution)/shard_map/ppermute | solution.py:25
  132.5 9.5 %collective-permute-start.23 = (bf16[512,128]{1,0:T(8,128)(2,1)}, bf16[512,128]{1,0:T(8,128)(2,1)S(1)}, u32[]{:S(2)}, u32[]{:S(2)}) collective-permute-start(bf16[512,128]{1,0:T(8,128)(2,1)} %get-tuple-element.91), channel_id=1, source_target_pairs={{0,2},{1,3},{2,0},{3,1},{4,6},{5,7},{6,4},{7,5},{8,10},{9,11},{10,... | collective-permute-start | bytes 393224 | tf_op jit(solution)/shard_map/ppermute | solution.py:25
  137.6 11.4 %collective-permute-start.18 = (bf16[272,128]{1,0:T(8,128)(2,1)}, bf16[272,128]{1,0:T(8,128)(2,1)S(1)}, u32[]{:S(2)}, u32[]{:S(2)}) collective-permute-start(bf16[272,128]{1,0:T(8,128)(2,1)} %get-tuple-element.85), channel_id=1, source_target_pairs={{0,2},{1,3},{2,0},{3,1},{4,6},{5,7},{6,4},{7,5},{8,10},{9,11},{10,... | collective-permute-start | bytes 208904 | tf_op jit(solution)/shard_map/ppermute | solution.py:25
  138.0 11.1 %collective-permute-start.19 = (bf16[272,128]{1,0:T(8,128)(2,1)}, bf16[272,128]{1,0:T(8,128)(2,1)S(1)}, u32[]{:S(2)}, u32[]{:S(2)}) collective-permute-start(bf16[272,128]{1,0:T(8,128)(2,1)} %get-tuple-element.86), channel_id=1, source_target_pairs={{0,4},{1,5},{2,6},{3,7},{4,0},{5,1},{6,2},{7,3},{8,12},{9,13},{10,... | collective-permute-start | bytes 208904 | tf_op jit(solution)/shard_map/ppermute | solution.py:25
  141.7 7.3 %collective-permute-start.20 = (bf16[272,128]{1,0:T(8,128)(2,1)}, bf16[272,128]{1,0:T(8,128)(2,1)S(1)}, u32[]{:S(2)}, u32[]{:S(2)}) collective-permute-start(bf16[272,128]{1,0:T(8,128)(2,1)} %get-tuple-element.87), channel_id=1, source_target_pairs={{0,6},{1,7},{2,4},{3,5},{4,2},{5,3},{6,0},{7,1},{8,14},{9,15},{10,... | collective-permute-start | bytes 208904 | tf_op jit(solution)/shard_map/ppermute | solution.py:25
  160.3 4.5 %collective-permute-start.27 = (f32[8,128]{1,0:T(8,128)S(1)}, f32[8,128]{1,0:T(8,128)S(1)}, u32[]{:S(2)}, u32[]{:S(2)}) collective-permute-start(f32[8,128]{1,0:T(8,128)S(1)} %add.61), channel_id=1, source_target_pairs={{0,4},{1,5},{2,6},{3,7},{4,0},{5,1},{6,2},{7,3},{8,12},{9,13},{10,... | collective-permute-start | bytes 12296 | tf_op jit(solution)/shard_map/ppermute | solution.py:25
  (28 other events, 32.4 us)

commit v2 on v1

v2 whole, which is shorter than its diff:
```python
import functools

import jax
import jax.numpy as jnp
from jax import lax
from jax.experimental import pallas as pl
from jax.experimental.pallas import tpu as pltpu
from jax.sharding import PartitionSpec as P

epsilon = 1e-06
F32 = jnp.float32
BF16 = jnp.bfloat16
PAD = 16
VMEM = pltpu.VMEM
SMEM = pltpu.SMEM


def passed_along(block, axis, distance):
    devices = range(lax.axis_size(axis))
    route = [(i - distance, i) for i in devices if i - distance in devices]
    return lax.ppermute(block, axis, route)


def swapped(block, mask):
    return lax.ppermute(block, "blk", [(i, i ^ mask) for i in range(lax.axis_size("blk"))])


class Plan:
    def __init__(self, tiles, channels, tile, blk):
        self.T, self.W, self.D, self.B = tiles, channels, tile, blk
        self.Z = blk // 2
        self.entries = float(tiles * blk * tile * tile)
        self.n = tiles * blk
        self.part = tiles * tile
        self.half = self.Z * self.part

    def slots(self, feeds, me):
        device = feeds // self.T
        zr = (device // 2) ^ (me // 2)
        yr = (device % 2) ^ (me % 2)
        slot = (yr * self.Z + zr) * self.T + feeds % self.T
        return jnp.where(feeds >= self.n, self.n, slot).astype(jnp.int32)


def packed_row(scalars, tile):
    lane = lax.broadcasted_iota(jnp.int32, (1, tile), 1)
    row = jnp.zeros((1, tile), F32)
    for index, value in enumerate(scalars):
        row = row + jnp.where(lane == index, value, 0.0)
    return split_row(row, tile)


def split_row(row, tile):
    high = row.astype(BF16).astype(F32)
    middle = (row - high).astype(BF16).astype(F32)
    low = row - high - middle
    at = lax.broadcasted_iota(jnp.int32, (PAD, tile), 0)
    rows = jnp.where(at == 0, high, jnp.where(at == 1, middle, jnp.where(at == 2, low, 0.0)))
    return rows.astype(BF16)


def joined_row(rows):
    rows = rows.astype(F32)
    return rows[0:1] + rows[1:2] + rows[2:3]


def total(value):
    return jnp.sum(value, keepdims=True).reshape(1, 1)


def live_mask(plan, sizes, k):
    down = lax.broadcasted_iota(jnp.int32, (plan.D, plan.D), 0)
    across = lax.broadcasted_iota(jnp.int32, (plan.D, plan.D), 1)
    return jnp.logical_and(down < sizes[k], across < sizes[plan.T + k])


def received_sums(plan, parts):
    def tile(k):
        at = pl.ds(k * plan.D, plan.D)
        return functools.reduce(lambda x, y: x + y, [p[at, :].astype(F32) for p in parts])

    level = [joined_row(p[pl.ds(plan.part, PAD), :]) for p in parts]
    while len(level) > 1:
        level = [level[i] + level[i + 1] for i in range(0, len(level), 2)]
    return tile, level[0]


def lane(row, index):
    return row[:, index : index + 1]


def shift_of(plan, a, b, d, e):
    alpha = a / plan.entries
    m = jnp.maximum(b - 2.0 * alpha * d + alpha * alpha * e, 0.0) / plan.entries
    return alpha, m


def update_first(plan, ins, outs, send):
    (start, sizes, energy), (x_out,) = ins, outs
    norm = jnp.zeros((1, 1), F32)
    for k in range(plan.T):
        at = pl.ds(k * plan.D, plan.D)
        x = jnp.where(live_mask(plan, sizes, k), start[at, :].astype(F32), 0.0)
        x_out[at, :] = x
        send(k, x)
        norm = norm + total(x * x)
    return [norm]


def update_second(plan, ins, outs, send):
    (x_in, sizes, energy), arrived = ins[:3], ins[3:]
    q_out, h_out, known_out = outs
    tile, row = received_sums(plan, arrived)
    square = lane(row, 0)
    scale = lax.rsqrt(square / plan.entries + epsilon)
    known_out[...] = jnp.broadcast_to(scale * scale * square, known_out.shape)
    a = b = jnp.zeros((1, 1), F32)
    for k in range(plan.T):
        at = pl.ds(k * plan.D, plan.D)
        x = x_in[at, :]
        image = jnp.where(live_mask(plan, sizes, k), tile(k), 0.0) + energy[k] * x
        q = scale * x
        h = scale * image
        q_out[at, :] = q
        h_out[at, :] = h
        send(k, h)
        a = a + total(q * h)
        b = b + total(h * h)
    return [a, b]


def update_third(plan, ins, outs, send):
    (q_in, h_in, known, sizes, energy), arrived = ins[:5], ins[5:]
    q_out, h_out, z_out, coef_out = outs
    tile, row = received_sums(plan, arrived)
    a, b = lane(row, 0), lane(row, 1)
    alpha, m = shift_of(plan, a, b, a, known[0:1, 0:1])
    beta, scale = jnp.sqrt(m), lax.rsqrt(m + epsilon)
    coef_out[0:1, :] = jnp.broadcast_to(alpha, (1, plan.D))
    coef_out[1:2, :] = jnp.broadcast_to(beta, (1, plan.D))
    sums = [jnp.zeros((1, 1), F32)] * 4
    for k in range(plan.T):
        at = pl.ds(k * plan.D, plan.D)
        q0, h0 = q_in[at, :], h_in[at, :]
        image = jnp.where(live_mask(plan, sizes, k), tile(k), 0.0) + energy[k] * h0
        q = scale * (h0 - alpha * q0)
        h = scale * (image - alpha * h0)
        z = h - beta * q0
        q_out[at, :] = q
        h_out[at, :] = h
        z_out[at, :] = z
        send(k, z)
        sums = [s + total(p) for s, p in zip(sums, (q * h, z * z, z * q, q * q))]
    return sums


def update_last(plan, ins, outs, send):
    (q_in, h_in, z_in, sizes, energy), arrived = ins[:5], ins[5:]
    q_out, z_out, coef_out = outs
    tile, row = received_sums(plan, arrived)
    alpha, m = shift_of(plan, *[lane(row, i) for i in range(4)])
    beta, scale = jnp.sqrt(m), lax.rsqrt(m + epsilon)
    coef_out[0:1, :] = jnp.broadcast_to(alpha, (1, plan.D))
    coef_out[1:2, :] = jnp.broadcast_to(beta, (1, plan.D))
    sums = [jnp.zeros((1, 1), F32)] * 4
    for k in range(plan.T):
        at = pl.ds(k * plan.D, plan.D)
        q1, h1, z1 = q_in[at, :], h_in[at, :], z_in[at, :]
        image = jnp.where(live_mask(plan, sizes, k), tile(k), 0.0) + energy[k] * z1
        q = scale * (z1 - alpha * q1)
        h = scale * (image - alpha * h1)
        z = h - beta * q1
        q_out[at, :] = q
        z_out[at, :] = z
        sums = [s + total(p) for s, p in zip(sums, (q * h, z * z, z * q, q * q))]
    return sums


def on_chip(name, body, ins, outs, scratch=()):
    spaces = [SMEM if len(x.shape) == 1 else VMEM for x in ins]
    return pl.pallas_call(
        body,
        in_specs=[pl.BlockSpec(memory_space=s) for s in spaces],
        out_specs=[pl.BlockSpec(memory_space=VMEM)] * len(outs),
        out_shape=list(outs),
        scratch_shapes=list(scratch),
        compiler_params=pltpu.CompilerParams(vmem_limit_bytes=16 * 2**20),
        name=name,
    )(*ins)


def operator_step(plan, name, update, ins, state_shapes, left, right):
    D, T, W = plan.D, plan.T, plan.W
    pairs = T // 2
    message = jax.ShapeDtypeStruct((plan.half + PAD, D), BF16)
    n_in, n_state = len(ins), len(state_shapes)
    group = next(c for c in range(max(1, W // 2), 0, -1) if W % c == 0)

    def body(*refs):
        in_refs = refs[:n_in]
        left_ref, right_ref = refs[n_in : n_in + 2]
        state_refs = refs[n_in + 2 : n_in + 2 + n_state]
        keep_ref, send_ref, low_ref, half_ref, sum_ref = refs[n_in + 2 + n_state :]
        sizes = next(r for r in in_refs if len(r.shape) == 1 and r.dtype == jnp.int32)

        def send(k, value):
            low_ref[pl.ds(k * D, D), :] = value.astype(BF16)

        row = packed_row(update(plan, in_refs, state_refs, send), D)
        for ref in (keep_ref, send_ref):
            ref[pl.ds(plan.half, PAD), :] = row
        sum_ref[...] = jnp.zeros(sum_ref.shape, F32)
        none = jnp.zeros((D, D), BF16)

        def several(step, carry):
            for h in range(pairs):
                blocks = (h, h + pairs)
                v = [low_ref[pl.ds(k * D, D), :] for k in blocks]
                both = jnp.concatenate(
                    [jnp.concatenate([v[0], none], 1), jnp.concatenate([none, v[1]], 1)], 0
                )
                firsts = [k * W + step * group for k in blocks]
                tiles = [
                    left_ref[pl.ds(pl.multiple_of(f * D, D), group * D), :] for f in firsts
                ]
                half_ref[...] = jnp.dot(
                    jnp.concatenate(tiles, 1), both, preferred_element_type=F32
                ).astype(BF16)
                for w in range(group):
                    for side, f in enumerate(firsts):
                        product = jnp.dot(
                            half_ref[pl.ds(w * D, D), pl.ds(side * D, D)],
                            right_ref[pl.ds(pl.multiple_of((f + w) * D, D), D), :],
                            preferred_element_type=F32,
                        )
                        slot = sizes[2 * T + f + w]
                        at = pl.ds(pl.multiple_of(slot * D, D), D)
                        sum_ref[at, :] += product
            return carry

        lax.fori_loop(0, W // group, several, 0)
        for first, ref in ((0, keep_ref), (plan.half, send_ref)):
            ref[pl.ds(0, plan.half), :] = sum_ref[pl.ds(first, plan.half), :].astype(BF16)

    results = on_chip(
        name,
        body,
        list(ins) + [left, right],
        list(state_shapes) + [message] * 2,
        [
            VMEM((T * D, D), BF16),
            VMEM((group * D, 2 * D), BF16),
            VMEM(((plan.n + 1) * D, D), F32),
        ],
    )
    return results[:n_state], results[n_state:]


def row_of(plan, values):
    across = lax.broadcasted_iota(jnp.int32, (8, plan.D), 1)
    row = jnp.zeros((8, plan.D), F32)
    for index, value in enumerate(values):
        row = row + jnp.where(across == index, value, 0.0)
    return row


def last_step(plan, ins, state_shapes):
    n_in = len(ins)

    def body(*refs):
        sums = update_last(plan, refs[:n_in], refs[n_in:-1], None)
        refs[-1][...] = row_of(plan, sums)

    row = jax.ShapeDtypeStruct((8, plan.D), F32)
    return on_chip("last_step", body, ins, list(state_shapes) + [row])


def outcome(plan, q, z, first, second, *sums):
    def body(q_ref, z_ref, first_ref, second_ref, *refs):
        added = functools.reduce(lambda x, y: x + y, [r[0:1, :] for r in refs[:-2]])
        residual_ref, coef_ref = refs[-2:]
        alpha, m = shift_of(plan, *[lane(added, i) for i in range(4)])
        residual_ref[...] = z_ref[...] - alpha * q_ref[...]
        values = [first_ref[0:1, 0:1], second_ref[0:1, 0:1], alpha]
        values += [first_ref[1:2, 0:1], second_ref[1:2, 0:1], jnp.sqrt(m)]
        coef_ref[...] = row_of(plan, values)

    row = jax.ShapeDtypeStruct((8, plan.D), F32)
    return on_chip("outcome", body, [q, z, first, second, *sums], [q, row])


def middle(plan, keep, got):
    def body(keep_ref, got_ref, *outs):
        end = pl.ds(plan.half, PAD)
        scalars = split_row(joined_row(keep_ref[end, :]) + joined_row(got_ref[end, :]), plan.D)
        for z, out in enumerate(outs):
            at = pl.ds(z * plan.part, plan.part)
            added = keep_ref[at, :].astype(F32) + got_ref[at, :].astype(F32)
            out[pl.ds(0, plan.part), :] = added.astype(BF16)
            out[pl.ds(plan.part, PAD), :] = scalars

    shape = jax.ShapeDtypeStruct((plan.part + PAD, plan.D), BF16)
    return on_chip("middle", body, [keep, got], [shape] * plan.Z)


def exchanged(plan, messages):
    keep, send = messages
    parts = middle(plan, keep, swapped(send, 1))
    last = [swapped(parts[z], 2 * z) for z in range(plan.Z - 1, 0, -1)]
    return [parts[0]] + last[::-1]


def local(
    start_vector,
    left_environment,
    right_environment,
    block_energy,
    sector_rows,
    sector_cols,
    feed_block,
):
    T, W, D = left_environment.shape[1:4]
    plan = Plan(T, W, D, lax.axis_size("blk"))
    left = passed_along(left_environment, "seg", 1).reshape(T * W * D, D)
    right = right_environment.reshape(T * W * D, D)
    slots = plan.slots(feed_block.reshape(T * W), lax.axis_index("blk"))
    sizes = jnp.concatenate([sector_rows[0], sector_cols[0], slots])
    energy = block_energy[0]
    vector = jax.ShapeDtypeStruct((T * D, D), F32)
    row = jax.ShapeDtypeStruct((8, D), F32)
    start = start_vector.reshape(T * D, D)

    (x,), messages = operator_step(
        plan, "step_0", update_first, [start, sizes, energy], [vector], left, right
    )
    arrived = exchanged(plan, messages)
    (q0, h0, known), messages = operator_step(
        plan, "step_1", update_second, [x, sizes, energy] + arrived, [vector, vector, row], left, right
    )
    arrived = exchanged(plan, messages)
    (q1, h1, z1, first), messages = operator_step(
        plan,
        "step_2",
        update_third,
        [q0, h0, known, sizes, energy] + arrived,
        [vector, vector, vector, row],
        left,
        right,
    )
    arrived = exchanged(plan, messages)
    q2, z2, second, sums = last_step(
        plan, [q1, h1, z1, sizes, energy] + arrived, [vector, vector, row]
    )
    mask = 1
    while 2 * mask < plan.B:
        sums = sums + swapped(sums, mask)
        mask *= 2
    residual, coefficients = outcome(plan, q2, z2, first, second, sums, swapped(sums, mask))
    return (coefficients[:1, :6], residual.reshape(1, T, D, D))


def solution(mesh):
    return jax.shard_map(
        local,
        mesh=mesh,
        in_specs=(
            P("seg", "blk", None, None),
            P("seg", "blk", None, None, None),
            P("seg", "blk", None, None, None),
            P("seg", "blk"),
            P("seg", "blk"),
            P("seg", "blk"),
            P("seg", "blk", None),
        ),
        out_specs=(P("seg", None), P("seg", "blk", None, None)),
        check_vma=False,
    )
```

time: 176 us -> 158 us (0.90)
  waiting for transfers between devices: 74.1 us -> 105 us
  Pallas kernels: 44.7 us -> 21 us
  starting transfers between devices: 34.3 us -> 24.9 us
  local copies, waits for them, and re-layouts: 13.5 us -> 5.1 us
  between operations: 5.47 us -> 0.72 us
  other arithmetic: 3.05 us -> 0.78 us
    ppermute x27 -> x15, waiting for transfers between devices: 24.5 us -> 55.3 us  [swapped(): lax.ppermute(block, 'blk', [(i, i ^ mask) for i in range(lax.axis_size('b...]
    pallas_call x10 -> x8, Pallas kernels: 44.7 us -> 21 us  [on_chip(): pl.pallas_call(body, in_specs=[pl.BlockSpec(memory_space=s) for s in spac...]
    ppermute x27 -> x15, starting transfers between devices: 32.4 us -> 23 us  [swapped(): lax.ppermute(block, 'blk', [(i, i ^ mask) for i in range(lax.axis_size('b...]
    another operation x1 -> x0, local copies, waits for them, and re-layouts: 3.17 us -> none  [local(): jnp.stack([first[0, 0], second[0, 0], alpha, first[1, 0], second[1, 0], j...]
    slice x3 -> x1, local copies, waits for them, and re-layouts: 3.28 us -> 0.51 us  [local(): return (coefficients[:1, :6], residual.reshape(1, T, D, D))]
    unnamed x48 -> x10, local copies, waits for them, and re-layouts: 6.24 us -> 3.83 us
    sub x1 -> x0, other arithmetic: 1.76 us -> none  [local(): residual = z2 - alpha * q2]
  transfers between devices with their start and end apart: 28 -> 16, of which waited for: 10 -> 13; matrix products, arithmetic and copies ran while one was open for 2% -> 1% of each run, Pallas kernels for 6% -> 0%
where the time goes in v2:
time: 158 us; the launch traced here: 157 us
  waiting for transfers between devices  105 us (66%)
  starting transfers between devices  24.9 us (16%)
  Pallas kernels  21 us (13%)
  local copies, waits for them, and re-layouts  5.1 us (3%)
    ppermute x15, waiting for transfers between devices, swapped(): lax.ppermute(block, 'blk', [(i, i ^ mask) for i in range(lax.axis_size('b...  55.3 us
    ppermute x1, waiting for transfers between devices, passed_along(): return lax.ppermute(block, axis, route)  49.5 us
    ppermute x15, starting transfers between devices, swapped(): lax.ppermute(block, 'blk', [(i, i ^ mask) for i in range(lax.axis_size('b...  23 us
    pallas_call x8, Pallas kernels, on_chip(): pl.pallas_call(body, in_specs=[pl.BlockSpec(memory_space=s) for s in spac...  21 us
    unnamed x10, local copies, waits for them, and re-layouts  3.83 us
  transfers between devices with their start and end apart: 16, of which 13 were waited for; matrix products, arithmetic and copies ran while one was open for 1% of the time, Pallas kernels for 0%

profile of v2, /device:TPU:6, one launch (start us, length us, event | category | flops | bytes accessed | tf_op | source)
XLA Modules:
  0.0 157.2 jit_solution(12350494843123824637)
XLA Ops:
  0.6 1.9 %collective-permute-start = (bf16[1,4,34,128,128]{4,3,2,1,0:T(8,128)(2,1)}, bf16[1,4,34,128,128]{4,3,2,1,0:T(8,128)(2,1)}, u32[]{:S(2)}, u32[]{:S(2)}) collective-permute-start(bf16[1,4,34,128,128]{4,3,2,1,0:T(8,128)(2,1)} %param.8), channel_id=1, source_target_pairs={{0,8},{8,16},{16,24},{1,9},{9,17},{17,25},{2,10},{10,18},{18,26},{... | collective-permute-start | bytes 13369352 | tf_op jit(solution)/shard_map/ppermute | solution.py:21
  4.1 49.5 %collective-permute-done = bf16[1,4,34,128,128]{4,3,2,1,0:T(8,128)(2,1)} collective-permute-done((bf16[1,4,34,128,128]{4,3,2,1,0:T(8,128)(2,1)}, bf16[1,4,34,128,128]{4,3,2,1,0:T(8,128)(2,1)}, u32[]{:S(2)}, u32[]{:S(2)}) %collective-permute-start) | collective-permute-done | bytes 4456480 | tf_op jit(solution)/shard_map/ppermute | solution.py:21
  53.6 2.3 %copy-done = bf16[1,4,34,128,128]{4,3,2,1,0:T(8,128)(2,1)S(1)} copy-done((bf16[1,4,34,128,128]{4,3,2,1,0:T(8,128)(2,1)S(1)}, bf16[1,4,34,128,128]{4,3,2,1,0:T(8,128)(2,1)}, u32[]{:S(2)}) %copy-start) | copy-done | bytes 4456472
  57.4 6.1 %step_0.1 = (f32[512,128]{1,0:T(8,128)S(1)}, bf16[2064,128]{1,0:T(8,128)(2,1)S(1)}, bf16[2064,128]{1,0:T(8,128)(2,1)S(1)}) custom-call(bf16[512,128]{1,0:T(8,128)(2,1)S(1)} %bitcast.10, s32[144]{0:T(256)S(1)} %pad_add_fusion.refs_1_.refs_3_, f32[4]{0:T(128)S(1)} %bitcast.11, bf16[17408,128]{1,0:T(8,128)(2,1)} %bitcast.4.refs_3_.refs_7_.refs_9_, ...), custom_call_target="tpu_custom_call" | custom-call | tf_op jit(solution)/shard_map/step_0/pallas_call | solution.py:181
  64.1 9.8 %collective-permute-done.1.got_ref = bf16[2064,128]{1,0:T(8,128)(2,1)S(1)} collective-permute-done((bf16[2064,128]{1,0:T(8,128)(2,1)S(1)}, bf16[2064,128]{1,0:T(8,128)(2,1)S(1)}, u32[]{:S(2)}, u32[]{:S(2)}) %collective-permute-start.1) | collective-permute-done | bytes 528416 | tf_op jit(solution)/shard_map/ppermute | solution.py:25
  74.0 1.2 collective-permute-start.2
  75.2 4.1 %collective-permute-start.3 = (bf16[528,128]{1,0:T(8,128)(2,1)S(1)}, bf16[528,128]{1,0:T(8,128)(2,1)S(1)}, u32[]{:S(2)}, u32[]{:S(2)}) collective-permute-start(bf16[528,128]{1,0:T(8,128)(2,1)S(1)} %get-tuple-element.39), channel_id=1, source_target_pairs={{0,4},{1,5},{2,6},{3,7},{4,0},{5,1},{6,2},{7,3},{8,12},{9,13},{10,... | collective-permute-start | bytes 405512 | tf_op jit(solution)/shard_map/ppermute | solution.py:25
  79.3 4.6 %collective-permute-done.3.refs_5_ = bf16[528,128]{1,0:T(8,128)(2,1)S(1)} collective-permute-done((bf16[528,128]{1,0:T(8,128)(2,1)S(1)}, bf16[528,128]{1,0:T(8,128)(2,1)S(1)}, u32[]{:S(2)}, u32[]{:S(2)}) %collective-permute-start.3) | collective-permute-done | bytes 135200 | tf_op jit(solution)/shard_map/ppermute | solution.py:25
  84.0 3.7 %collective-permute-done.4.refs_6_ = bf16[528,128]{1,0:T(8,128)(2,1)S(1)} collective-permute-done((bf16[528,128]{1,0:T(8,128)(2,1)S(1)}, bf16[528,128]{1,0:T(8,128)(2,1)S(1)}, u32[]{:S(2)}, u32[]{:S(2)}) %collective-permute-start.4) | collective-permute-done | bytes 135200 | tf_op jit(solution)/shard_map/ppermute | solution.py:25
  87.7 6.1 %step_1.1 = (f32[512,128]{1,0:T(8,128)S(1)}, f32[512,128]{1,0:T(8,128)S(1)}, f32[8,128]{1,0:T(8,128)S(1)}, bf16[2064,128]{1,0:T(8,128)(2,1)S(1)}, bf16[2064,128]{1,0:T(8,128)(2,1)S(1)}) custom-call(f32[512,128]{1,0:T(8,128)S(1)} %get-tuple-element.34.refs_0_, s32[144]{0:T(256)S(1)} %pad_add_fusion.refs_1_.refs_3_, f32[4]{0:T(128)S(1)} %bitcast.12, ...), custom_call_target="tpu_custom_call" | custom-call | tf_op jit(solution)/shard_map/step_1/pallas_call | solution.py:181
  94.4 8.7 %collective-permute-done.5.got_ref = bf16[2064,128]{1,0:T(8,128)(2,1)S(1)} collective-permute-done((bf16[2064,128]{1,0:T(8,128)(2,1)S(1)}, bf16[2064,128]{1,0:T(8,128)(2,1)S(1)}, u32[]{:S(2)}, u32[]{:S(2)}) %collective-permute-start.5) | collective-permute-done | bytes 528416 | tf_op jit(solution)/shard_map/ppermute | solution.py:25
  103.3 4.2 %collective-permute-start.6 = (bf16[528,128]{1,0:T(8,128)(2,1)S(1)}, bf16[528,128]{1,0:T(8,128)(2,1)S(1)}, u32[]{:S(2)}, u32[]{:S(2)}) collective-permute-start(bf16[528,128]{1,0:T(8,128)(2,1)S(1)} %get-tuple-element.47), channel_id=1, source_target_pairs={{0,2},{1,3},{2,0},{3,1},{4,6},{5,7},{6,4},{7,5},{8,10},{9,11},{10,... | collective-permute-start | bytes 405512 | tf_op jit(solution)/shard_map/ppermute | solution.py:25
  107.8 2.1 %collective-permute-start.8 = (bf16[528,128]{1,0:T(8,128)(2,1)S(1)}, bf16[528,128]{1,0:T(8,128)(2,1)S(1)}, u32[]{:S(2)}, u32[]{:S(2)}) collective-permute-start(bf16[528,128]{1,0:T(8,128)(2,1)S(1)} %get-tuple-element.49), channel_id=1, source_target_pairs={{0,6},{1,7},{2,4},{3,5},{4,2},{5,3},{6,0},{7,1},{8,14},{9,15},{10,... | collective-permute-start | bytes 405512 | tf_op jit(solution)/shard_map/ppermute | solution.py:25
  110.4 5.8 %collective-permute-done.7.refs_7_ = bf16[528,128]{1,0:T(8,128)(2,1)S(1)} collective-permute-done((bf16[528,128]{1,0:T(8,128)(2,1)S(1)}, bf16[528,128]{1,0:T(8,128)(2,1)S(1)}, u32[]{:S(2)}, u32[]{:S(2)}) %collective-permute-start.7) | collective-permute-done | bytes 135200 | tf_op jit(solution)/shard_map/ppermute | solution.py:25
  116.2 6.3 %step_2.1 = (f32[512,128]{1,0:T(8,128)S(1)}, f32[512,128]{1,0:T(8,128)S(1)}, f32[512,128]{1,0:T(8,128)S(1)}, f32[8,128]{1,0:T(8,128)S(1)}, bf16[2064,128]{1,0:T(8,128)(2,1)S(1)}, /*index=5*/bf16[2064,128]{1,0:T(8,128)(2,1)S(1)}) custom-call(f32[512,128]{1,0:T(8,128)S(1)} %get-tuple-element.41.refs_0_, f32[512,128]{1,0:T(8,128)S(1)} %get-tuple-element.42.refs_1_, ...), custom_call_target="tpu_custom_call" | custom-call | tf_op jit(solution)/shard_map/step_2/pallas_call | solution.py:181
  123.1 8.7 %collective-permute-done.9.got_ref = bf16[2064,128]{1,0:T(8,128)(2,1)S(1)} collective-permute-done((bf16[2064,128]{1,0:T(8,128)(2,1)S(1)}, bf16[2064,128]{1,0:T(8,128)(2,1)S(1)}, u32[]{:S(2)}, u32[]{:S(2)}) %collective-permute-start.9) | collective-permute-done | bytes 528416 | tf_op jit(solution)/shard_map/ppermute | solution.py:25
  132.0 2.1 %collective-permute-start.10 = (bf16[528,128]{1,0:T(8,128)(2,1)S(1)}, bf16[528,128]{1,0:T(8,128)(2,1)S(1)}, u32[]{:S(2)}, u32[]{:S(2)}) collective-permute-start(bf16[528,128]{1,0:T(8,128)(2,1)S(1)} %get-tuple-element.56), channel_id=1, source_target_pairs={{0,2},{1,3},{2,0},{3,1},{4,6},{5,7},{6,4},{7,5},{8,10},{9,11},{10,... | collective-permute-start | bytes 405512 | tf_op jit(solution)/shard_map/ppermute | solution.py:25
  134.4 2.1 %collective-permute-start.12 = (bf16[528,128]{1,0:T(8,128)(2,1)S(1)}, bf16[528,128]{1,0:T(8,128)(2,1)S(1)}, u32[]{:S(2)}, u32[]{:S(2)}) collective-permute-start(bf16[528,128]{1,0:T(8,128)(2,1)S(1)} %get-tuple-element.58), channel_id=1, source_target_pairs={{0,6},{1,7},{2,4},{3,5},{4,2},{5,3},{6,0},{7,1},{8,14},{9,15},{10,... | collective-permute-start | bytes 405512 | tf_op jit(solution)/shard_map/ppermute | solution.py:25
  137.1 5.8 %collective-permute-done.11.refs_7_ = bf16[528,128]{1,0:T(8,128)(2,1)S(1)} collective-permute-done((bf16[528,128]{1,0:T(8,128)(2,1)S(1)}, bf16[528,128]{1,0:T(8,128)(2,1)S(1)}, u32[]{:S(2)}, u32[]{:S(2)}) %collective-permute-start.11) | collective-permute-done | bytes 135200 | tf_op jit(solution)/shard_map/ppermute | solution.py:25
  144.6 3.1 %collective-permute-done.13 = f32[8,128]{1,0:T(8,128)S(1)} collective-permute-done((f32[8,128]{1,0:T(8,128)S(1)}, f32[8,128]{1,0:T(8,128)S(1)}, u32[]{:S(2)}, u32[]{:S(2)}) %collective-permute-start.13) | collective-permute-done | bytes 4128 | tf_op jit(solution)/shard_map/ppermute | solution.py:25
  147.7 2.0 %collective-permute-start.14 = (f32[8,128]{1,0:T(8,128)S(1)}, f32[8,128]{1,0:T(8,128)S(1)}, u32[]{:S(2)}, u32[]{:S(2)}) collective-permute-start(f32[8,128]{1,0:T(8,128)S(1)} %add.34), channel_id=1, source_target_pairs={{0,2},{1,3},{2,0},{3,1},{4,6},{5,7},{6,4},{7,5},{8,10},{9,11},{10,... | collective-permute-start | bytes 12296 | tf_op jit(solution)/shard_map/ppermute | solution.py:25
  149.7 1.6 %collective-permute-done.14 = f32[8,128]{1,0:T(8,128)S(1)} collective-permute-done((f32[8,128]{1,0:T(8,128)S(1)}, f32[8,128]{1,0:T(8,128)S(1)}, u32[]{:S(2)}, u32[]{:S(2)}) %collective-permute-start.14) | collective-permute-done | bytes 4128 | tf_op jit(solution)/shard_map/ppermute | solution.py:25
  151.3 2.3 %collective-permute-start.15 = (f32[8,128]{1,0:T(8,128)S(1)}, f32[8,128]{1,0:T(8,128)S(1)}, u32[]{:S(2)}, u32[]{:S(2)}) collective-permute-start(f32[8,128]{1,0:T(8,128)S(1)} %add.35.refs_0_), channel_id=1, source_target_pairs={{0,4},{1,5},{2,6},{3,7},{4,0},{5,1},{6,2},{7,3},{8,12},{9,13},{10,... | collective-permute-start | bytes 12296 | tf_op jit(solution)/shard_map/ppermute | solution.py:25
  153.6 2.2 %collective-permute-done.15.refs_1_ = f32[8,128]{1,0:T(8,128)S(1)} collective-permute-done((f32[8,128]{1,0:T(8,128)S(1)}, f32[8,128]{1,0:T(8,128)S(1)}, u32[]{:S(2)}, u32[]{:S(2)}) %collective-permute-start.15) | collective-permute-done | bytes 4128 | tf_op jit(solution)/shard_map/ppermute | solution.py:25
  (32 shorter events, 10.2 us)
Async XLA Ops:
  0.6 52.9 %collective-permute-start = (bf16[1,4,34,128,128]{4,3,2,1,0:T(8,128)(2,1)}, bf16[1,4,34,128,128]{4,3,2,1,0:T(8,128)(2,1)}, u32[]{:S(2)}, u32[]{:S(2)}) collective-permute-start(bf16[1,4,34,128,128]{4,3,2,1,0:T(8,128)(2,1)} %param.8), channel_id=1, source_target_pairs={{0,8},{8,16},{16,24},{1,9},{9,17},{17,25},{2,10},{10,18},{18,26},{... | collective-permute-start | bytes 13369352 | tf_op jit(solution)/shard_map/ppermute | solution.py:21
  53.6 2.3 %copy-start = (bf16[1,4,34,128,128]{4,3,2,1,0:T(8,128)(2,1)S(1)}, bf16[1,4,34,128,128]{4,3,2,1,0:T(8,128)(2,1)}, u32[]{:S(2)}) copy-start(bf16[1,4,34,128,128]{4,3,2,1,0:T(8,128)(2,1)} %param.9) | copy-start | bytes 13369348
  55.8 0.9 copy-start.2
  56.7 0.7 copy-start.3
  57.4 30.3 %copy-start.1 = (bf16[1,4,34,128,128]{4,3,2,1,0:T(8,128)(2,1)S(1)}, bf16[1,4,34,128,128]{4,3,2,1,0:T(8,128)(2,1)}, u32[]{:S(2)}) copy-start(bf16[1,4,34,128,128]{4,3,2,1,0:T(8,128)(2,1)} %param.9) | copy-start | bytes 13369348
  57.4 30.3 %copy-start.4 = (f32[1,4]{1,0:T(1,128)S(1)}, f32[1,4]{1,0:T(1,128)}, u32[]{:S(2)}) copy-start(f32[1,4]{1,0:T(1,128)} %param.10) | copy-start | bytes 52
  63.5 10.4 %collective-permute-start.1 = (bf16[2064,128]{1,0:T(8,128)(2,1)S(1)}, bf16[2064,128]{1,0:T(8,128)(2,1)S(1)}, u32[]{:S(2)}, u32[]{:S(2)}) collective-permute-start(bf16[2064,128]{1,0:T(8,128)(2,1)S(1)} %get-tuple-element.36), channel_id=1, source_target_pairs={{0,1},{1,0},{2,3},{3,2},{4,5},{5,4},{6,7},{7,6},{8,9},{9,8},{10,11... | collective-permute-start | bytes 1585160 | tf_op jit(solution)/shard_map/ppermute | solution.py:25
  74.0 5.3 %collective-permute-start.2 = (bf16[528,128]{1,0:T(8,128)(2,1)S(1)}, bf16[528,128]{1,0:T(8,128)(2,1)S(1)}, u32[]{:S(2)}, u32[]{:S(2)}) collective-permute-start(bf16[528,128]{1,0:T(8,128)(2,1)S(1)} %get-tuple-element.38), channel_id=1, source_target_pairs={{0,2},{1,3},{2,0},{3,1},{4,6},{5,7},{6,4},{7,5},{8,10},{9,11},{10,... | collective-permute-start | bytes 405512 | tf_op jit(solution)/shard_map/ppermute | solution.py:25
  75.2 8.7 %collective-permute-start.3 = (bf16[528,128]{1,0:T(8,128)(2,1)S(1)}, bf16[528,128]{1,0:T(8,128)(2,1)S(1)}, u32[]{:S(2)}, u32[]{:S(2)}) collective-permute-start(bf16[528,128]{1,0:T(8,128)(2,1)S(1)} %get-tuple-element.39), channel_id=1, source_target_pairs={{0,4},{1,5},{2,6},{3,7},{4,0},{5,1},{6,2},{7,3},{8,12},{9,13},{10,... | collective-permute-start | bytes 405512 | tf_op jit(solution)/shard_map/ppermute | solution.py:25
  79.3 8.4 %collective-permute-start.4 = (bf16[528,128]{1,0:T(8,128)(2,1)S(1)}, bf16[528,128]{1,0:T(8,128)(2,1)S(1)}, u32[]{:S(2)}, u32[]{:S(2)}) collective-permute-start(bf16[528,128]{1,0:T(8,128)(2,1)S(1)} %get-tuple-element.40), channel_id=1, source_target_pairs={{0,6},{1,7},{2,4},{3,5},{4,2},{5,3},{6,0},{7,1},{8,14},{9,15},{10,... | collective-permute-start | bytes 405512 | tf_op jit(solution)/shard_map/ppermute | solution.py:25
  93.8 9.3 %collective-permute-start.5 = (bf16[2064,128]{1,0:T(8,128)(2,1)S(1)}, bf16[2064,128]{1,0:T(8,128)(2,1)S(1)}, u32[]{:S(2)}, u32[]{:S(2)}) collective-permute-start(bf16[2064,128]{1,0:T(8,128)(2,1)S(1)} %get-tuple-element.45), channel_id=1, source_target_pairs={{0,1},{1,0},{2,3},{3,2},{4,5},{5,4},{6,7},{7,6},{8,9},{9,8},{10,11... | collective-permute-start | bytes 1585160 | tf_op jit(solution)/shard_map/ppermute | solution.py:25
  103.3 7.2 %collective-permute-start.6 = (bf16[528,128]{1,0:T(8,128)(2,1)S(1)}, bf16[528,128]{1,0:T(8,128)(2,1)S(1)}, u32[]{:S(2)}, u32[]{:S(2)}) collective-permute-start(bf16[528,128]{1,0:T(8,128)(2,1)S(1)} %get-tuple-element.47), channel_id=1, source_target_pairs={{0,2},{1,3},{2,0},{3,1},{4,6},{5,7},{6,4},{7,5},{8,10},{9,11},{10,... | collective-permute-start | bytes 405512 | tf_op jit(solution)/shard_map/ppermute | solution.py:25
  107.4 8.8 %collective-permute-start.7 = (bf16[528,128]{1,0:T(8,128)(2,1)S(1)}, bf16[528,128]{1,0:T(8,128)(2,1)S(1)}, u32[]{:S(2)}, u32[]{:S(2)}) collective-permute-start(bf16[528,128]{1,0:T(8,128)(2,1)S(1)} %get-tuple-element.48), channel_id=1, source_target_pairs={{0,4},{1,5},{2,6},{3,7},{4,0},{5,1},{6,2},{7,3},{8,12},{9,13},{10,... | collective-permute-start | bytes 405512 | tf_op jit(solution)/shard_map/ppermute | solution.py:25
  107.8 8.5 %collective-permute-start.8 = (bf16[528,128]{1,0:T(8,128)(2,1)S(1)}, bf16[528,128]{1,0:T(8,128)(2,1)S(1)}, u32[]{:S(2)}, u32[]{:S(2)}) collective-permute-start(bf16[528,128]{1,0:T(8,128)(2,1)S(1)} %get-tuple-element.49), channel_id=1, source_target_pairs={{0,6},{1,7},{2,4},{3,5},{4,2},{5,3},{6,0},{7,1},{8,14},{9,15},{10,... | collective-permute-start | bytes 405512 | tf_op jit(solution)/shard_map/ppermute | solution.py:25
  122.6 9.3 %collective-permute-start.9 = (bf16[2064,128]{1,0:T(8,128)(2,1)S(1)}, bf16[2064,128]{1,0:T(8,128)(2,1)S(1)}, u32[]{:S(2)}, u32[]{:S(2)}) collective-permute-start(bf16[2064,128]{1,0:T(8,128)(2,1)S(1)} %get-tuple-element.54), channel_id=1, source_target_pairs={{0,1},{1,0},{2,3},{3,2},{4,5},{5,4},{6,7},{7,6},{8,9},{9,8},{10,11... | collective-permute-start | bytes 1585160 | tf_op jit(solution)/shard_map/ppermute | solution.py:25
  132.0 5.1 %collective-permute-start.10 = (bf16[528,128]{1,0:T(8,128)(2,1)S(1)}, bf16[528,128]{1,0:T(8,128)(2,1)S(1)}, u32[]{:S(2)}, u32[]{:S(2)}) collective-permute-start(bf16[528,128]{1,0:T(8,128)(2,1)S(1)} %get-tuple-element.56), channel_id=1, source_target_pairs={{0,2},{1,3},{2,0},{3,1},{4,6},{5,7},{6,4},{7,5},{8,10},{9,11},{10,... | collective-permute-start | bytes 405512 | tf_op jit(solution)/shard_map/ppermute | solution.py:25
  134.1 8.8 %collective-permute-start.11 = (bf16[528,128]{1,0:T(8,128)(2,1)S(1)}, bf16[528,128]{1,0:T(8,128)(2,1)S(1)}, u32[]{:S(2)}, u32[]{:S(2)}) collective-permute-start(bf16[528,128]{1,0:T(8,128)(2,1)S(1)} %get-tuple-element.57), channel_id=1, source_target_pairs={{0,4},{1,5},{2,6},{3,7},{4,0},{5,1},{6,2},{7,3},{8,12},{9,13},{10,... | collective-permute-start | bytes 405512 | tf_op jit(solution)/shard_map/ppermute | solution.py:25
  134.4 8.5 %collective-permute-start.12 = (bf16[528,128]{1,0:T(8,128)(2,1)S(1)}, bf16[528,128]{1,0:T(8,128)(2,1)S(1)}, u32[]{:S(2)}, u32[]{:S(2)}) collective-permute-start(bf16[528,128]{1,0:T(8,128)(2,1)S(1)} %get-tuple-element.58), channel_id=1, source_target_pairs={{0,6},{1,7},{2,4},{3,5},{4,2},{5,3},{6,0},{7,1},{8,14},{9,15},{10,... | collective-permute-start | bytes 405512 | tf_op jit(solution)/shard_map/ppermute | solution.py:25
  144.0 3.7 %collective-permute-start.13 = (f32[8,128]{1,0:T(8,128)S(1)}, f32[8,128]{1,0:T(8,128)S(1)}, u32[]{:S(2)}, u32[]{:S(2)}) collective-permute-start(f32[8,128]{1,0:T(8,128)S(1)} %get-tuple-element.63), channel_id=1, source_target_pairs={{0,1},{1,0},{2,3},{3,2},{4,5},{5,4},{6,7},{7,6},{8,9},{9,8},{10,11... | collective-permute-start | bytes 12296 | tf_op jit(solution)/shard_map/ppermute | solution.py:25
  147.7 3.6 %collective-permute-start.14 = (f32[8,128]{1,0:T(8,128)S(1)}, f32[8,128]{1,0:T(8,128)S(1)}, u32[]{:S(2)}, u32[]{:S(2)}) collective-permute-start(f32[8,128]{1,0:T(8,128)S(1)} %add.34), channel_id=1, source_target_pairs={{0,2},{1,3},{2,0},{3,1},{4,6},{5,7},{6,4},{7,5},{8,10},{9,11},{10,... | collective-permute-start | bytes 12296 | tf_op jit(solution)/shard_map/ppermute | solution.py:25
  151.3 4.5 %collective-permute-start.15 = (f32[8,128]{1,0:T(8,128)S(1)}, f32[8,128]{1,0:T(8,128)S(1)}, u32[]{:S(2)}, u32[]{:S(2)}) collective-permute-start(f32[8,128]{1,0:T(8,128)S(1)} %add.35.refs_0_), channel_id=1, source_target_pairs={{0,4},{1,5},{2,6},{3,7},{4,0},{5,1},{6,2},{7,3},{8,12},{9,13},{10,... | collective-permute-start | bytes 12296 | tf_op jit(solution)/shard_map/ppermute | solution.py:25

commit v3 on v2

--- a/solution.py
+++ b/solution.py
@@ -29,17 +29,26 @@
     def __init__(self, tiles, channels, tile, blk):
         self.T, self.W, self.D, self.B = tiles, channels, tile, blk
         self.Z = blk // 2
+        self.Ta = tiles // 2
+        self.Tb = tiles - self.Ta
         self.entries = float(tiles * blk * tile * tile)
         self.n = tiles * blk
-        self.part = tiles * tile
-        self.half = self.Z * self.part
-
-    def slots(self, feeds, me):
-        device = feeds // self.T
-        zr = (device // 2) ^ (me // 2)
-        yr = (device % 2) ^ (me % 2)
-        slot = (yr * self.Z + zr) * self.T + feeds % self.T
-        return jnp.where(feeds >= self.n, self.n, slot).astype(jnp.int32)
+        self.a_rows = self.Ta * tile
+        self.b_rows = self.Tb * tile
+
+    def slot(self, feed, me):
+        tiles = jnp.int32(self.T)
+        device, tile = lax.div(feed, tiles), lax.rem(feed, tiles)
+        relative = device ^ me
+        zr, yr = relative >> 1, relative & 1
+        a = (yr * self.Z + zr) * self.Ta + tile
+        b = self.B * self.Ta + (zr * 2 + yr) * self.Tb + (tile - self.Ta)
+        return jnp.where(feed >= self.n, self.n, jnp.where(tile < self.Ta, a, b))
+
+    def messages(self):
+        a = jax.ShapeDtypeStruct((self.Z * self.a_rows + PAD, self.D), BF16)
+        b = jax.ShapeDtypeStruct((2 * self.b_rows, self.D), BF16)
+        return [a, a] + [b] * self.Z
 
 
 def packed_row(scalars, tile):
@@ -64,22 +73,29 @@
     return rows[0:1] + rows[1:2] + rows[2:3]
 
 
+def folded(value):
+    return jnp.sum(value.reshape(value.shape[0] // 8, 8, value.shape[1]), axis=0)
+
+
 def total(value):
     return jnp.sum(value, keepdims=True).reshape(1, 1)
 
 
-def live_mask(plan, sizes, k):
+def live_mask(plan, rows, cols, k):
     down = lax.broadcasted_iota(jnp.int32, (plan.D, plan.D), 0)
     across = lax.broadcasted_iota(jnp.int32, (plan.D, plan.D), 1)
-    return jnp.logical_and(down < sizes[k], across < sizes[plan.T + k])
-
-
-def received_sums(plan, parts):
+    return jnp.logical_and(down < rows[k], across < cols[k])
+
+
+def received_sums(plan, arrived):
+    a_parts, b_parts = arrived[: plan.Z], arrived[plan.Z :]
+
     def tile(k):
-        at = pl.ds(k * plan.D, plan.D)
+        parts, i = (a_parts, k) if k < plan.Ta else (b_parts, k - plan.Ta)
+        at = pl.ds(i * plan.D, plan.D)
         return functools.reduce(lambda x, y: x + y, [p[at, :].astype(F32) for p in parts])
 
-    level = [joined_row(p[pl.ds(plan.part, PAD), :]) for p in parts]
+    level = [joined_row(p[pl.ds(plan.a_rows, PAD), :]) for p in a_parts]
     while len(level) > 1:
         level = [level[i] + level[i + 1] for i in range(0, len(level), 2)]
     return tile, level[0]
@@ -96,41 +112,41 @@
 
 
 def update_first(plan, ins, outs, send):
-    (start, sizes, energy), (x_out,) = ins, outs
-    norm = jnp.zeros((1, 1), F32)
+    (start, rows, cols), (x_out,) = ins, outs
+    norm = jnp.zeros((8, plan.D), F32)
     for k in range(plan.T):
         at = pl.ds(k * plan.D, plan.D)
-        x = jnp.where(live_mask(plan, sizes, k), start[at, :].astype(F32), 0.0)
+        x = jnp.where(live_mask(plan, rows, cols, k), start[at, :].astype(F32), 0.0)
         x_out[at, :] = x
         send(k, x)
-        norm = norm + total(x * x)
-    return [norm]
+        norm = norm + folded(x * x)
+    return [total(norm)]
 
 
 def update_second(plan, ins, outs, send):
-    (x_in, sizes, energy), arrived = ins[:3], ins[3:]
+    (x_in, rows, cols, energy), arrived = ins[:4], ins[4:]
     q_out, h_out, known_out = outs
     tile, row = received_sums(plan, arrived)
     square = lane(row, 0)
     scale = lax.rsqrt(square / plan.entries + epsilon)
     known_out[...] = jnp.broadcast_to(scale * scale * square, known_out.shape)
-    a = b = jnp.zeros((1, 1), F32)
+    a = b = jnp.zeros((8, plan.D), F32)
     for k in range(plan.T):
         at = pl.ds(k * plan.D, plan.D)
         x = x_in[at, :]
-        image = jnp.where(live_mask(plan, sizes, k), tile(k), 0.0) + energy[k] * x
+        image = jnp.where(live_mask(plan, rows, cols, k), tile(k), 0.0) + energy[k] * x
         q = scale * x
         h = scale * image
         q_out[at, :] = q
         h_out[at, :] = h
         send(k, h)
-        a = a + total(q * h)
-        b = b + total(h * h)
-    return [a, b]
+        a = a + folded(q * h)
+        b = b + folded(h * h)
+    return [total(a), total(b)]
 
 
 def update_third(plan, ins, outs, send):
-    (q_in, h_in, known, sizes, energy), arrived = ins[:5], ins[5:]
+    (q_in, h_in, known, rows, cols, energy), arrived = ins[:6], ins[6:]
     q_out, h_out, z_out, coef_out = outs
     tile, row = received_sums(plan, arrived)
     a, b = lane(row, 0), lane(row, 1)
@@ -138,11 +154,11 @@
     beta, scale = jnp.sqrt(m), lax.rsqrt(m + epsilon)
     coef_out[0:1, :] = jnp.broadcast_to(alpha, (1, plan.D))
     coef_out[1:2, :] = jnp.broadcast_to(beta, (1, plan.D))
-    sums = [jnp.zeros((1, 1), F32)] * 4
+    sums = [jnp.zeros((8, plan.D), F32)] * 4
     for k in range(plan.T):
         at = pl.ds(k * plan.D, plan.D)
         q0, h0 = q_in[at, :], h_in[at, :]
-        image = jnp.where(live_mask(plan, sizes, k), tile(k), 0.0) + energy[k] * h0
+        image = jnp.where(live_mask(plan, rows, cols, k), tile(k), 0.0) + energy[k] * h0
         q = scale * (h0 - alpha * q0)
         h = scale * (image - alpha * h0)
         z = h - beta * q0
@@ -150,30 +166,30 @@
         h_out[at, :] = h
         z_out[at, :] = z
         send(k, z)
-        sums = [s + total(p) for s, p in zip(sums, (q * h, z * z, z * q, q * q))]
-    return sums
+        sums = [s + folded(p) for s, p in zip(sums, (q * h, z * z, z * q, q * q))]
+    return [total(s) for s in sums]
 
 
 def update_last(plan, ins, outs, send):
-    (q_in, h_in, z_in, sizes, energy), arrived = ins[:5], ins[5:]
+    (q_in, h_in, z_in, rows, cols, energy), arrived = ins[:6], ins[6:]
     q_out, z_out, coef_out = outs
     tile, row = received_sums(plan, arrived)
     alpha, m = shift_of(plan, *[lane(row, i) for i in range(4)])
     beta, scale = jnp.sqrt(m), lax.rsqrt(m + epsilon)
     coef_out[0:1, :] = jnp.broadcast_to(alpha, (1, plan.D))
     coef_out[1:2, :] = jnp.broadcast_to(beta, (1, plan.D))
-    sums = [jnp.zeros((1, 1), F32)] * 4
+    sums = [jnp.zeros((8, plan.D), F32)] * 4
     for k in range(plan.T):
         at = pl.ds(k * plan.D, plan.D)
         q1, h1, z1 = q_in[at, :], h_in[at, :], z_in[at, :]
-        image = jnp.where(live_mask(plan, sizes, k), tile(k), 0.0) + energy[k] * z1
+        image = jnp.where(live_mask(plan, rows, cols, k), tile(k), 0.0) + energy[k] * z1
         q = scale * (z1 - alpha * q1)
         h = scale * (image - alpha * h1)
         z = h - beta * q1
         q_out[at, :] = q
         z_out[at, :] = z
-        sums = [s + total(p) for s, p in zip(sums, (q * h, z * z, z * q, q * q))]
-    return sums
+        sums = [s + folded(p) for s, p in zip(sums, (q * h, z * z, z * q, q * q))]
+    return [total(s) for s in sums]
 
 
 def on_chip(name, body, ins, outs, scratch=()):
@@ -189,26 +205,27 @@
     )(*ins)
 
 
-def operator_step(plan, name, update, ins, state_shapes, left, right):
+def operator_step(plan, name, update, ins, state_shapes, left, right, slots):
     D, T, W = plan.D, plan.T, plan.W
     pairs = T // 2
-    message = jax.ShapeDtypeStruct((plan.half + PAD, D), BF16)
     n_in, n_state = len(ins), len(state_shapes)
     group = next(c for c in range(max(1, W // 2), 0, -1) if W % c == 0)
 
     def body(*refs):
         in_refs = refs[:n_in]
-        left_ref, right_ref = refs[n_in : n_in + 2]
-        state_refs = refs[n_in + 2 : n_in + 2 + n_state]
-        keep_ref, send_ref, low_ref, half_ref, sum_ref = refs[n_in + 2 + n_state :]
-        sizes = next(r for r in in_refs if len(r.shape) == 1 and r.dtype == jnp.int32)
+        left_ref, right_ref, slot_ref = refs[n_in : n_in + 3]
+        state_refs = refs[n_in + 3 : n_in + 3 + n_state]
+        message_refs = refs[n_in + 3 + n_state : -3]
+        low_ref, half_ref, sum_ref = refs[-3:]
 
         def send(k, value):
             low_ref[pl.ds(k * D, D), :] = value.astype(BF16)
 
-        row = packed_row(update(plan, in_refs, state_refs, send), D)
-        for ref in (keep_ref, send_ref):
-            ref[pl.ds(plan.half, PAD), :] = row
+        row = update(plan, in_refs, state_refs, send)
+        if isinstance(row, list):
+            row = packed_row(row, D)
+        for ref in message_refs[:2]:
+            ref[pl.ds(plan.Z * plan.a_rows, PAD), :] = row
         sum_ref[...] = jnp.zeros(sum_ref.shape, F32)
         none = jnp.zeros((D, D), BF16)
 
@@ -233,20 +250,23 @@
                             right_ref[pl.ds(pl.multiple_of((f + w) * D, D), D), :],
                             preferred_element_type=F32,
                         )
-                        slot = sizes[2 * T + f + w]
+                        slot = slot_ref[f + w]
                         at = pl.ds(pl.multiple_of(slot * D, D), D)
                         sum_ref[at, :] += product
             return carry
 
         lax.fori_loop(0, W // group, several, 0)
-        for first, ref in ((0, keep_ref), (plan.half, send_ref)):
-            ref[pl.ds(0, plan.half), :] = sum_ref[pl.ds(first, plan.half), :].astype(BF16)
+        first = 0
+        for ref in message_refs:
+            rows = ref.shape[0] // D * D
+            ref[pl.ds(0, rows), :] = sum_ref[pl.ds(first, rows), :].astype(BF16)
+            first += rows
 
     results = on_chip(
         name,
         body,
-        list(ins) + [left, right],
-        list(state_shapes) + [message] * 2,
+        list(ins) + [left, right, slots],
+        list(state_shapes) + plan.messages(),
         [
             VMEM((T * D, D), BF16),
             VMEM((group * D, 2 * D), BF16),
@@ -289,25 +309,91 @@
     return on_chip("outcome", body, [q, z, first, second, *sums], [q, row])
 
 
-def middle(plan, keep, got):
+def middle_a(plan, keep, got):
+    rows = plan.a_rows
+
     def body(keep_ref, got_ref, *outs):
-        end = pl.ds(plan.half, PAD)
+        end = pl.ds(plan.Z * rows, PAD)
         scalars = split_row(joined_row(keep_ref[end, :]) + joined_row(got_ref[end, :]), plan.D)
         for z, out in enumerate(outs):
-            at = pl.ds(z * plan.part, plan.part)
+            at = pl.ds(z * rows, rows)
             added = keep_ref[at, :].astype(F32) + got_ref[at, :].astype(F32)
-            out[pl.ds(0, plan.part), :] = added.astype(BF16)
-            out[pl.ds(plan.part, PAD), :] = scalars
-
-    shape = jax.ShapeDtypeStruct((plan.part + PAD, plan.D), BF16)
-    return on_chip("middle", body, [keep, got], [shape] * plan.Z)
+            out[pl.ds(0, rows), :] = added.astype(BF16)
+            out[pl.ds(rows, PAD), :] = scalars
+
+    shape = jax.ShapeDtypeStruct((rows + PAD, plan.D), BF16)
+    return on_chip("middle_a", body, [keep, got], [shape] * plan.Z)
+
+
+def middle_b(plan, parts):
+    rows = plan.b_rows
+
+    def body(*refs):
+        for y, out in enumerate(refs[plan.Z :]):
+            at = pl.ds(y * rows, rows)
+            tiles = [p[at, :].astype(F32) for p in refs[: plan.Z]]
+            out[...] = functools.reduce(lambda u, v: u + v, tiles).astype(out.dtype)
+
+    shapes = [jax.ShapeDtypeStruct((rows, plan.D), d) for d in (F32, BF16)]
+    return on_chip("middle_b", body, parts, shapes)
 
 
 def exchanged(plan, messages):
-    keep, send = messages
-    parts = middle(plan, keep, swapped(send, 1))
-    last = [swapped(parts[z], 2 * z) for z in range(plan.Z - 1, 0, -1)]
-    return [parts[0]] + last[::-1]
+    keep, send, b_parts = messages[0], messages[1], messages[2:]
+    others = range(plan.Z - 1, 0, -1)
+    got = swapped(send, 1)
+    b_got = [swapped(b_parts[z], 2 * z) for z in others]
+    a_parts = middle_a(plan, keep, got)
+    a_last = [swapped(a_parts[z], 2 * z) for z in others]
+    b_keep, b_send = middle_b(plan, [b_parts[0]] + b_got)
+    return [a_parts[0]] + a_last[::-1] + [b_keep, swapped(b_send, 1)]
+
+
+def prepared(plan, start, rows, cols, feeds, right):
+    def body(start_ref, rows_ref, cols_ref, feed_ref, right_ref, *outs):
+        x_ref, low_ref, row_ref, slot_ref, held_ref, done = outs
+        copy = pltpu.make_async_copy(right_ref, held_ref, done)
+        copy.start()
+        me = lax.axis_index("blk")
+
+        def several(w, carry):
+            for k in range(plan.T):
+                slot_ref[k * plan.W + w] = plan.slot(feed_ref[k, w], me)
+            return carry
+
+        lax.fori_loop(0, plan.W, several, 0)
+
+        def send(k, value):
+            low_ref[pl.ds(k * plan.D, plan.D), :] = value.astype(BF16)
+
+        sums = update_first(plan, (start_ref, rows_ref, cols_ref), (x_ref,), send)
+        row_ref[...] = packed_row(sums, plan.D)
+        copy.wait()
+
+    chip = pl.BlockSpec(memory_space=VMEM)
+    scalar = pl.BlockSpec(memory_space=SMEM)
+    return pl.pallas_call(
+        body,
+        in_specs=[chip, scalar, scalar, scalar, pl.BlockSpec(memory_space=pltpu.HBM)],
+        out_specs=[chip, chip, chip, scalar, chip],
+        out_shape=[
+            jax.ShapeDtypeStruct(start.shape, F32),
+            jax.ShapeDtypeStruct(start.shape, BF16),
+            jax.ShapeDtypeStruct((PAD, plan.D), BF16),
+            jax.ShapeDtypeStruct((plan.T * plan.W,), jnp.int32),
+            right,
+        ],
+        scratch_shapes=[pltpu.SemaphoreType.DMA(())],
+        compiler_params=pltpu.CompilerParams(vmem_limit_bytes=16 * 2**20),
+        name="prepared",
+    )(start, rows, cols, feeds, right)
+
+
+def update_none(plan, ins, outs, send):
+    low, row = ins
+    for k in range(plan.T):
+        send(k, low[pl.ds(k * plan.D, plan.D), :])
+    return row[...]
 
 
 def local(
@@ -323,33 +409,40 @@
     plan = Plan(T, W, D, lax.axis_size("blk"))
     left = passed_along(left_environment, "seg", 1).reshape(T * W * D, D)
     right = right_environment.reshape(T * W * D, D)
-    slots = plan.slots(feed_block.reshape(T * W), lax.axis_index("blk"))
-    sizes = jnp.concatenate([sector_rows[0], sector_cols[0], slots])
-    energy = block_energy[0]
+    rows, cols, energy = sector_rows[0], sector_cols[0], block_energy[0]
     vector = jax.ShapeDtypeStruct((T * D, D), F32)
     row = jax.ShapeDtypeStruct((8, D), F32)
     start = start_vector.reshape(T * D, D)
 
-    (x,), messages = operator_step(
-        plan, "step_0", update_first, [start, sizes, energy], [vector], left, right
+    x, low, square, slots, right = prepared(plan, start, rows, cols, feed_block[0], right)
+    _, messages = operator_step(
+        plan, "step_0", update_none, [low, square], [], left, right, slots
     )
     arrived = exchanged(plan, messages)
     (q0, h0, known), messages = operator_step(
-        plan, "step_1", update_second, [x, sizes, energy] + arrived, [vector, vector, row], left, right
+        plan,
+        "step_1",
+        update_second,
+        [x, rows, cols, energy] + arrived,
+        [vector, vector, row],
+        left,
+        right,
+        slots,
     )
     arrived = exchanged(plan, messages)
     (q1, h1, z1, first), messages = operator_step(
         plan,
         "step_2",
         update_third,
-        [q0, h0, known, sizes, energy] + arrived,
+        [q0, h0, known, rows, cols, energy] + arrived,
         [vector, vector, vector, row],
         left,
         right,
+        slots,
     )
     arrived = exchanged(plan, messages)
     q2, z2, second, sums = last_step(
-        plan, [q1, h1, z1, sizes, energy] + arrived, [vector, vector, row]
+        plan, [q1, h1, z1, rows, cols, energy] + arrived, [vector, vector, row]
     )
     mask = 1
     while 2 * mask < plan.B:

time: 158 us -> 129 us (0.82)
  waiting for transfers between devices: 105 us -> 69.2 us
  starting transfers between devices: 24.9 us -> 35.1 us
  Pallas kernels: 21 us -> 18.1 us
    ppermute x15 -> x27, waiting for transfers between devices: 55.3 us -> 26.5 us  [swapped(): lax.ppermute(block, 'blk', [(i, i ^ mask) for i in range(lax.axis_size('b...]
    ppermute x15 -> x27, starting transfers between devices: 23 us -> 33.1 us  [swapped(): lax.ppermute(block, 'blk', [(i, i ^ mask) for i in range(lax.axis_size('b...]
    ppermute x1, waiting for transfers between devices: 49.5 us -> 42.8 us  [passed_along(): return lax.ppermute(block, axis, route)]
    pallas_call x8 -> x11, Pallas kernels: 21 us -> 15.1 us  [on_chip(): pl.pallas_call(body, in_specs=[pl.BlockSpec(memory_space=s) for s in spac...]
    pallas_call x0 -> x1, Pallas kernels: none -> 2.99 us  [prepared(): pl.pallas_call(body, in_specs=[chip, scalar, scalar, scalar, pl.BlockSpec...]
    unnamed x10 -> x16, local copies, waits for them, and re-layouts: 3.83 us -> 5.16 us
  transfers between devices with their start and end apart: 16 -> 28, of which waited for: 13 -> 11; matrix products, arithmetic and copies ran while one was open for 1% -> 0% of each run, Pallas kernels for 0% -> 3%
where the time goes in v3:
time: 129 us
  waiting for transfers between devices  69.2 us (54%)
  starting transfers between devices  35.1 us (27%)
  Pallas kernels  18.1 us (14%)
  local copies, waits for them, and re-layouts  5.67 us (4%)
    ppermute x1, waiting for transfers between devices, passed_along(): return lax.ppermute(block, axis, route)  42.8 us
    ppermute x27, starting transfers between devices, swapped(): lax.ppermute(block, 'blk', [(i, i ^ mask) for i in range(lax.axis_size('b...  33.1 us
    ppermute x27, waiting for transfers between devices, swapped(): lax.ppermute(block, 'blk', [(i, i ^ mask) for i in range(lax.axis_size('b...  26.5 us
    pallas_call x11, Pallas kernels, on_chip(): pl.pallas_call(body, in_specs=[pl.BlockSpec(memory_space=s) for s in spac...  15.1 us
    unnamed x16, local copies, waits for them, and re-layouts  5.16 us
    pallas_call x1, Pallas kernels, prepared(): pl.pallas_call(body, in_specs=[chip, scalar, scalar, scalar, pl.BlockSpec...  2.99 us
  transfers between devices with their start and end apart: 28, of which 11 were waited for; matrix products, arithmetic and copies ran while one was open for 0% of the time, Pallas kernels for 3%

profile of v3, /device:TPU:6, one launch (start us, length us, event | category | flops | bytes accessed | tf_op | source)
XLA Modules:
  0.0 128.9 jit_solution(16662494585466223854)
XLA Ops:
  0.6 1.9 %collective-permute-start = (bf16[1,4,34,128,128]{4,3,2,1,0:T(8,128)(2,1)}, bf16[1,4,34,128,128]{4,3,2,1,0:T(8,128)(2,1)S(1)}, u32[]{:S(2)}, u32[]{:S(2)}) collective-permute-start(bf16[1,4,34,128,128]{4,3,2,1,0:T(8,128)(2,1)} %param.8), channel_id=1, source_target_pairs={{0,8},{8,16},{16,24},{1,9},{9,17},{17,25},{2,10},{10,18},{18,26},{... | collective-permute-start | bytes 13369352 | tf_op jit(solution)/shard_map/ppermute | solution.py:21
  2.6 2.3 %copy-done = bf16[1,4,34,128,128]{4,3,2,1,0:T(8,128)(2,1)S(1)} copy-done((bf16[1,4,34,128,128]{4,3,2,1,0:T(8,128)(2,1)S(1)}, bf16[1,4,34,128,128]{4,3,2,1,0:T(8,128)(2,1)}, u32[]{:S(2)}) %copy-start) | copy-done | bytes 4456472
  7.7 3.0 %prepared.1 = (f32[512,128]{1,0:T(8,128)S(1)}, bf16[512,128]{1,0:T(8,128)(2,1)S(1)}, bf16[16,128]{1,0:T(8,128)(2,1)S(1)}, s32[136]{0:T(256)S(1)}, bf16[17408,128]{1,0:T(8,128)(2,1)S(1)}) custom-call(bf16[512,128]{1,0:T(8,128)(2,1)S(1)} %bitcast.12, s32[4]{0:T(128)S(1)} %bitcast.13, s32[4]{0:T(128)S(1)} %bitcast.17, s32[4,34]{1,0:T(4,128)S(1)} %bitcast.24, ...), custom_call_target="tpu_custom_call" | custom-call | tf_op jit(solution)/shard_map/prepared/pallas_call | solution.py:375
  10.7 42.8 %collective-permute-done = bf16[1,4,34,128,128]{4,3,2,1,0:T(8,128)(2,1)S(1)} collective-permute-done((bf16[1,4,34,128,128]{4,3,2,1,0:T(8,128)(2,1)}, bf16[1,4,34,128,128]{4,3,2,1,0:T(8,128)(2,1)S(1)}, u32[]{:S(2)}, u32[]{:S(2)}) %collective-permute-start) | collective-permute-done | bytes 4456480 | tf_op jit(solution)/shard_map/ppermute | solution.py:21
  53.5 4.0 %step_0.1 = (bf16[1040,128]{1,0:T(8,128)(2,1)S(1)}, bf16[1040,128]{1,0:T(8,128)(2,1)S(1)}, bf16[512,128]{1,0:T(8,128)(2,1)S(1)}, bf16[512,128]{1,0:T(8,128)(2,1)...) custom-call(bf16[512,128]{1,0:T(8,128)(2,1)S(1)} %get-tuple-element.57.refs_0_, ...), custom_call_target="tpu_custom_call" | custom-call | tf_op jit(solution)/shard_map/step_0/pallas_call | solution.py:197
  58.1 3.6 %collective-permute-start.5 = (bf16[512,128]{1,0:T(8,128)(2,1)S(1)}, bf16[512,128]{1,0:T(8,128)(2,1)S(1)}, u32[]{:S(2)}, u32[]{:S(2)}) collective-permute-start(bf16[512,128]{1,0:T(8,128)(2,1)S(1)} %get-tuple-element.68), channel_id=1, source_target_pairs={{0,6},{1,7},{2,4},{3,5},{4,2},{5,3},{6,0},{7,1},{8,14},{9,15},{10,... | collective-permute-start | bytes 393224 | tf_op jit(solution)/shard_map/ppermute | solution.py:25
  62.5 2.2 %collective-permute-done.1.got_ref = bf16[1040,128]{1,0:T(8,128)(2,1)S(1)} collective-permute-done((bf16[1040,128]{1,0:T(8,128)(2,1)S(1)}, bf16[1040,128]{1,0:T(8,128)(2,1)S(1)}, u32[]{:S(2)}, u32[]{:S(2)}) %collective-permute-start.1) | collective-permute-done | bytes 266272 | tf_op jit(solution)/shard_map/ppermute | solution.py:25
  66.3 2.4 %collective-permute-start.3 = (bf16[272,128]{1,0:T(8,128)(2,1)S(1)}, bf16[272,128]{1,0:T(8,128)(2,1)S(1)}, u32[]{:S(2)}, u32[]{:S(2)}) collective-permute-start(bf16[272,128]{1,0:T(8,128)(2,1)S(1)} %get-tuple-element.65), channel_id=1, source_target_pairs={{0,4},{1,5},{2,6},{3,7},{4,0},{5,1},{6,2},{7,3},{8,12},{9,13},{10,... | collective-permute-start | bytes 208904 | tf_op jit(solution)/shard_map/ppermute | solution.py:25
  70.3 3.3 %collective-permute-done.8.refs_9_ = bf16[256,128]{1,0:T(8,128)(2,1)S(1)} collective-permute-done((bf16[256,128]{1,0:T(8,128)(2,1)S(1)}, bf16[256,128]{1,0:T(8,128)(2,1)S(1)}, u32[]{:S(2)}, u32[]{:S(2)}) %collective-permute-start.8) | collective-permute-done | bytes 65568 | tf_op jit(solution)/shard_map/ppermute | solution.py:25
  74.9 4.3 %step_1.1 = (f32[512,128]{1,0:T(8,128)S(1)}, f32[512,128]{1,0:T(8,128)S(1)}, f32[8,128]{1,0:T(8,128)S(1)}, bf16[1040,128]{1,0:T(8,128)(2,1)S(1)}, bf16[1040,128]...) custom-call(f32[512,128]{1,0:T(8,128)S(1)} %get-tuple-element.56.ref, ...), custom_call_target="tpu_custom_call" | custom-call | tf_op jit(solution)/shard_map/step_1/pallas_call | solution.py:197
  80.0 2.1 %collective-permute-start.13 = (bf16[512,128]{1,0:T(8,128)(2,1)S(1)}, bf16[512,128]{1,0:T(8,128)(2,1)S(1)}, u32[]{:S(2)}, u32[]{:S(2)}) collective-permute-start(bf16[512,128]{1,0:T(8,128)(2,1)S(1)} %get-tuple-element.83), channel_id=1, source_target_pairs={{0,6},{1,7},{2,4},{3,5},{4,2},{5,3},{6,0},{7,1},{8,14},{9,15},{10,... | collective-permute-start | bytes 393224 | tf_op jit(solution)/shard_map/ppermute | solution.py:25
  82.1 2.3 %collective-permute-start.15 = (bf16[512,128]{1,0:T(8,128)(2,1)S(1)}, bf16[512,128]{1,0:T(8,128)(2,1)S(1)}, u32[]{:S(2)}, u32[]{:S(2)}) collective-permute-start(bf16[512,128]{1,0:T(8,128)(2,1)S(1)} %get-tuple-element.85), channel_id=1, source_target_pairs={{0,2},{1,3},{2,0},{3,1},{4,6},{5,7},{6,4},{7,5},{8,10},{9,11},{10,... | collective-permute-start | bytes 393224 | tf_op jit(solution)/shard_map/ppermute | solution.py:25
  85.8 2.7 %collective-permute-start.11 = (bf16[272,128]{1,0:T(8,128)(2,1)S(1)}, bf16[272,128]{1,0:T(8,128)(2,1)S(1)}, u32[]{:S(2)}, u32[]{:S(2)}) collective-permute-start(bf16[272,128]{1,0:T(8,128)(2,1)S(1)} %get-tuple-element.80), channel_id=1, source_target_pairs={{0,4},{1,5},{2,6},{3,7},{4,0},{5,1},{6,2},{7,3},{8,12},{9,13},{10,... | collective-permute-start | bytes 208904 | tf_op jit(solution)/shard_map/ppermute | solution.py:25
  88.5 1.7 %collective-permute-start.12 = (bf16[272,128]{1,0:T(8,128)(2,1)S(1)}, bf16[272,128]{1,0:T(8,128)(2,1)S(1)}, u32[]{:S(2)}, u32[]{:S(2)}) collective-permute-start(bf16[272,128]{1,0:T(8,128)(2,1)S(1)} %get-tuple-element.81), channel_id=1, source_target_pairs={{0,6},{1,7},{2,4},{3,5},{4,2},{5,3},{6,0},{7,1},{8,14},{9,15},{10,... | collective-permute-start | bytes 208904 | tf_op jit(solution)/shard_map/ppermute | solution.py:25
  91.1 3.5 %collective-permute-done.16.refs_11_ = bf16[256,128]{1,0:T(8,128)(2,1)S(1)} collective-permute-done((bf16[256,128]{1,0:T(8,128)(2,1)S(1)}, bf16[256,128]{1,0:T(8,128)(2,1)S(1)}, u32[]{:S(2)}, u32[]{:S(2)}) %collective-permute-start.16) | collective-permute-done | bytes 65568 | tf_op jit(solution)/shard_map/ppermute | solution.py:25
  94.6 4.5 %step_2.1 = (f32[512,128]{1,0:T(8,128)S(1)}, f32[512,128]{1,0:T(8,128)S(1)}, f32[512,128]{1,0:T(8,128)S(1)}, f32[8,128]{1,0:T(8,128)S(1)}, bf16[1040,128]{1,0:T(...) custom-call(f32[512,128]{1,0:T(8,128)S(1)} %get-tuple-element.73.ref, ...), custom_call_target="tpu_custom_call" | custom-call | tf_op jit(solution)/shard_map/step_2/pallas_call | solution.py:197
  100.0 2.1 %collective-permute-start.21 = (bf16[512,128]{1,0:T(8,128)(2,1)S(1)}, bf16[512,128]{1,0:T(8,128)(2,1)S(1)}, u32[]{:S(2)}, u32[]{:S(2)}) collective-permute-start(bf16[512,128]{1,0:T(8,128)(2,1)S(1)} %get-tuple-element.98), channel_id=1, source_target_pairs={{0,6},{1,7},{2,4},{3,5},{4,2},{5,3},{6,0},{7,1},{8,14},{9,15},{10,... | collective-permute-start | bytes 393224 | tf_op jit(solution)/shard_map/ppermute | solution.py:25
  102.0 2.3 %collective-permute-start.23 = (bf16[512,128]{1,0:T(8,128)(2,1)S(1)}, bf16[512,128]{1,0:T(8,128)(2,1)S(1)}, u32[]{:S(2)}, u32[]{:S(2)}) collective-permute-start(bf16[512,128]{1,0:T(8,128)(2,1)S(1)} %get-tuple-element.100), channel_id=1, source_target_pairs={{0,2},{1,3},{2,0},{3,1},{4,6},{5,7},{6,4},{7,5},{8,10},{9,11},{10,... | collective-permute-start | bytes 393224 | tf_op jit(solution)/shard_map/ppermute | solution.py:25
  105.7 2.7 %collective-permute-start.19 = (bf16[272,128]{1,0:T(8,128)(2,1)S(1)}, bf16[272,128]{1,0:T(8,128)(2,1)S(1)}, u32[]{:S(2)}, u32[]{:S(2)}) collective-permute-start(bf16[272,128]{1,0:T(8,128)(2,1)S(1)} %get-tuple-element.95), channel_id=1, source_target_pairs={{0,4},{1,5},{2,6},{3,7},{4,0},{5,1},{6,2},{7,3},{8,12},{9,13},{10,... | collective-permute-start | bytes 208904 | tf_op jit(solution)/shard_map/ppermute | solution.py:25
  108.4 1.7 %collective-permute-start.20 = (bf16[272,128]{1,0:T(8,128)(2,1)S(1)}, bf16[272,128]{1,0:T(8,128)(2,1)S(1)}, u32[]{:S(2)}, u32[]{:S(2)}) collective-permute-start(bf16[272,128]{1,0:T(8,128)(2,1)S(1)} %get-tuple-element.96), channel_id=1, source_target_pairs={{0,6},{1,7},{2,4},{3,5},{4,2},{5,3},{6,0},{7,1},{8,14},{9,15},{10,... | collective-permute-start | bytes 208904 | tf_op jit(solution)/shard_map/ppermute | solution.py:25
  111.0 3.5 %collective-permute-done.24.refs_11_ = bf16[256,128]{1,0:T(8,128)(2,1)S(1)} collective-permute-done((bf16[256,128]{1,0:T(8,128)(2,1)S(1)}, bf16[256,128]{1,0:T(8,128)(2,1)S(1)}, u32[]{:S(2)}, u32[]{:S(2)}) %collective-permute-start.24) | collective-permute-done | bytes 65568 | tf_op jit(solution)/shard_map/ppermute | solution.py:25
  116.5 2.8 %collective-permute-done.25 = f32[8,128]{1,0:T(8,128)S(1)} collective-permute-done((f32[8,128]{1,0:T(8,128)S(1)}, f32[8,128]{1,0:T(8,128)S(1)}, u32[]{:S(2)}, u32[]{:S(2)}) %collective-permute-start.25) | collective-permute-done | bytes 4128 | tf_op jit(solution)/shard_map/ppermute | solution.py:25
  119.4 3.6 %collective-permute-done.26 = f32[8,128]{1,0:T(8,128)S(1)} collective-permute-done((f32[8,128]{1,0:T(8,128)S(1)}, f32[8,128]{1,0:T(8,128)S(1)}, u32[]{:S(2)}, u32[]{:S(2)}) %collective-permute-start.26) | collective-permute-done | bytes 4128 | tf_op jit(solution)/shard_map/ppermute | solution.py:25
  123.6 3.8 %collective-permute-done.27.refs_1_ = f32[8,128]{1,0:T(8,128)S(1)} collective-permute-done((f32[8,128]{1,0:T(8,128)S(1)}, f32[8,128]{1,0:T(8,128)S(1)}, u32[]{:S(2)}, u32[]{:S(2)}) %collective-permute-start.27) | collective-permute-done | bytes 4128 | tf_op jit(solution)/shard_map/ppermute | solution.py:25
  (63 shorter events, 19.2 us)
Async XLA Ops:
  0.6 52.8 %collective-permute-start = (bf16[1,4,34,128,128]{4,3,2,1,0:T(8,128)(2,1)}, bf16[1,4,34,128,128]{4,3,2,1,0:T(8,128)(2,1)S(1)}, u32[]{:S(2)}, u32[]{:S(2)}) collective-permute-start(bf16[1,4,34,128,128]{4,3,2,1,0:T(8,128)(2,1)} %param.8), channel_id=1, source_target_pairs={{0,8},{8,16},{16,24},{1,9},{9,17},{17,25},{2,10},{10,18},{18,26},{... | collective-permute-start | bytes 13369352 | tf_op jit(solution)/shard_map/ppermute | solution.py:21
  57.5 7.2 %collective-permute-start.1 = (bf16[1040,128]{1,0:T(8,128)(2,1)S(1)}, bf16[1040,128]{1,0:T(8,128)(2,1)S(1)}, u32[]{:S(2)}, u32[]{:S(2)}) collective-permute-start(bf16[1040,128]{1,0:T(8,128)(2,1)S(1)} %get-tuple-element.62), channel_id=1, source_target_pairs={{0,1},{1,0},{2,3},{3,2},{4,5},{5,4},{6,7},{7,6},{8,9},{9,8},{10,11... | collective-permute-start | bytes 798728 | tf_op jit(solution)/shard_map/ppermute | solution.py:25
  58.1 10.7 %collective-permute-start.5 = (bf16[512,128]{1,0:T(8,128)(2,1)S(1)}, bf16[512,128]{1,0:T(8,128)(2,1)S(1)}, u32[]{:S(2)}, u32[]{:S(2)}) collective-permute-start(bf16[512,128]{1,0:T(8,128)(2,1)S(1)} %get-tuple-element.68), channel_id=1, source_target_pairs={{0,6},{1,7},{2,4},{3,5},{4,2},{5,3},{6,0},{7,1},{8,14},{9,15},{10,... | collective-permute-start | bytes 393224 | tf_op jit(solution)/shard_map/ppermute | solution.py:25
  61.7 7.5 %collective-permute-start.6 = (bf16[512,128]{1,0:T(8,128)(2,1)S(1)}, bf16[512,128]{1,0:T(8,128)(2,1)S(1)}, u32[]{:S(2)}, u32[]{:S(2)}) collective-permute-start(bf16[512,128]{1,0:T(8,128)(2,1)S(1)} %get-tuple-element.69), channel_id=1, source_target_pairs={{0,4},{1,5},{2,6},{3,7},{4,0},{5,1},{6,2},{7,3},{8,12},{9,13},{10,... | collective-permute-start | bytes 393224 | tf_op jit(solution)/shard_map/ppermute | solution.py:25
  61.7 7.5 %collective-permute-start.7 = (bf16[512,128]{1,0:T(8,128)(2,1)S(1)}, bf16[512,128]{1,0:T(8,128)(2,1)S(1)}, u32[]{:S(2)}, u32[]{:S(2)}) collective-permute-start(bf16[512,128]{1,0:T(8,128)(2,1)S(1)} %get-tuple-element.70), channel_id=1, source_target_pairs={{0,2},{1,3},{2,0},{3,1},{4,6},{5,7},{6,4},{7,5},{8,10},{9,11},{10,... | collective-permute-start | bytes 393224 | tf_op jit(solution)/shard_map/ppermute | solution.py:25
  64.8 8.9 %collective-permute-start.2 = (bf16[272,128]{1,0:T(8,128)(2,1)S(1)}, bf16[272,128]{1,0:T(8,128)(2,1)S(1)}, u32[]{:S(2)}, u32[]{:S(2)}) collective-permute-start(bf16[272,128]{1,0:T(8,128)(2,1)S(1)} %get-tuple-element.64), channel_id=1, source_target_pairs={{0,2},{1,3},{2,0},{3,1},{4,6},{5,7},{6,4},{7,5},{8,10},{9,11},{10,... | collective-permute-start | bytes 208904 | tf_op jit(solution)/shard_map/ppermute | solution.py:25
  66.3 7.3 %collective-permute-start.3 = (bf16[272,128]{1,0:T(8,128)(2,1)S(1)}, bf16[272,128]{1,0:T(8,128)(2,1)S(1)}, u32[]{:S(2)}, u32[]{:S(2)}) collective-permute-start(bf16[272,128]{1,0:T(8,128)(2,1)S(1)} %get-tuple-element.65), channel_id=1, source_target_pairs={{0,4},{1,5},{2,6},{3,7},{4,0},{5,1},{6,2},{7,3},{8,12},{9,13},{10,... | collective-permute-start | bytes 208904 | tf_op jit(solution)/shard_map/ppermute | solution.py:25
  68.8 6.1 %collective-permute-start.4 = (bf16[272,128]{1,0:T(8,128)(2,1)S(1)}, bf16[272,128]{1,0:T(8,128)(2,1)S(1)}, u32[]{:S(2)}, u32[]{:S(2)}) collective-permute-start(bf16[272,128]{1,0:T(8,128)(2,1)S(1)} %get-tuple-element.66), channel_id=1, source_target_pairs={{0,6},{1,7},{2,4},{3,5},{4,2},{5,3},{6,0},{7,1},{8,14},{9,15},{10,... | collective-permute-start | bytes 208904 | tf_op jit(solution)/shard_map/ppermute | solution.py:25
  69.3 4.3 %collective-permute-start.8 = (bf16[256,128]{1,0:T(8,128)(2,1)S(1)}, bf16[256,128]{1,0:T(8,128)(2,1)S(1)}, u32[]{:S(2)}, u32[]{:S(2)}) collective-permute-start(bf16[256,128]{1,0:T(8,128)(2,1)S(1)} %get-tuple-element.72), channel_id=1, source_target_pairs={{0,1},{1,0},{2,3},{3,2},{4,5},{5,4},{6,7},{7,6},{8,9},{9,8},{10,11... | collective-permute-start | bytes 196616 | tf_op jit(solution)/shard_map/ppermute | solution.py:25
  79.2 6.5 %collective-permute-start.9 = (bf16[1040,128]{1,0:T(8,128)(2,1)S(1)}, bf16[1040,128]{1,0:T(8,128)(2,1)S(1)}, u32[]{:S(2)}, u32[]{:S(2)}) collective-permute-start(bf16[1040,128]{1,0:T(8,128)(2,1)S(1)} %get-tuple-element.77), channel_id=1, source_target_pairs={{0,1},{1,0},{2,3},{3,2},{4,5},{5,4},{6,7},{7,6},{8,9},{9,8},{10,11... | collective-permute-start | bytes 798728 | tf_op jit(solution)/shard_map/ppermute | solution.py:25
  80.0 8.5 %collective-permute-start.13 = (bf16[512,128]{1,0:T(8,128)(2,1)S(1)}, bf16[512,128]{1,0:T(8,128)(2,1)S(1)}, u32[]{:S(2)}, u32[]{:S(2)}) collective-permute-start(bf16[512,128]{1,0:T(8,128)(2,1)S(1)} %get-tuple-element.83), channel_id=1, source_target_pairs={{0,6},{1,7},{2,4},{3,5},{4,2},{5,3},{6,0},{7,1},{8,14},{9,15},{10,... | collective-permute-start | bytes 393224 | tf_op jit(solution)/shard_map/ppermute | solution.py:25
  82.1 8.1 %collective-permute-start.14 = (bf16[512,128]{1,0:T(8,128)(2,1)S(1)}, bf16[512,128]{1,0:T(8,128)(2,1)S(1)}, u32[]{:S(2)}, u32[]{:S(2)}) collective-permute-start(bf16[512,128]{1,0:T(8,128)(2,1)S(1)} %get-tuple-element.84), channel_id=1, source_target_pairs={{0,4},{1,5},{2,6},{3,7},{4,0},{5,1},{6,2},{7,3},{8,12},{9,13},{10,... | collective-permute-start | bytes 393224 | tf_op jit(solution)/shard_map/ppermute | solution.py:25
  82.1 8.1 %collective-permute-start.15 = (bf16[512,128]{1,0:T(8,128)(2,1)S(1)}, bf16[512,128]{1,0:T(8,128)(2,1)S(1)}, u32[]{:S(2)}, u32[]{:S(2)}) collective-permute-start(bf16[512,128]{1,0:T(8,128)(2,1)S(1)} %get-tuple-element.85), channel_id=1, source_target_pairs={{0,2},{1,3},{2,0},{3,1},{4,6},{5,7},{6,4},{7,5},{8,10},{9,11},{10,... | collective-permute-start | bytes 393224 | tf_op jit(solution)/shard_map/ppermute | solution.py:25
  85.7 8.9 %collective-permute-start.10 = (bf16[272,128]{1,0:T(8,128)(2,1)S(1)}, bf16[272,128]{1,0:T(8,128)(2,1)S(1)}, u32[]{:S(2)}, u32[]{:S(2)}) collective-permute-start(bf16[272,128]{1,0:T(8,128)(2,1)S(1)} %get-tuple-element.79), channel_id=1, source_target_pairs={{0,2},{1,3},{2,0},{3,1},{4,6},{5,7},{6,4},{7,5},{8,10},{9,11},{10,... | collective-permute-start | bytes 208904 | tf_op jit(solution)/shard_map/ppermute | solution.py:25
  85.8 8.8 %collective-permute-start.11 = (bf16[272,128]{1,0:T(8,128)(2,1)S(1)}, bf16[272,128]{1,0:T(8,128)(2,1)S(1)}, u32[]{:S(2)}, u32[]{:S(2)}) collective-permute-start(bf16[272,128]{1,0:T(8,128)(2,1)S(1)} %get-tuple-element.80), channel_id=1, source_target_pairs={{0,4},{1,5},{2,6},{3,7},{4,0},{5,1},{6,2},{7,3},{8,12},{9,13},{10,... | collective-permute-start | bytes 208904 | tf_op jit(solution)/shard_map/ppermute | solution.py:25
  88.5 6.1 %collective-permute-start.12 = (bf16[272,128]{1,0:T(8,128)(2,1)S(1)}, bf16[272,128]{1,0:T(8,128)(2,1)S(1)}, u32[]{:S(2)}, u32[]{:S(2)}) collective-permute-start(bf16[272,128]{1,0:T(8,128)(2,1)S(1)} %get-tuple-element.81), channel_id=1, source_target_pairs={{0,6},{1,7},{2,4},{3,5},{4,2},{5,3},{6,0},{7,1},{8,14},{9,15},{10,... | collective-permute-start | bytes 208904 | tf_op jit(solution)/shard_map/ppermute | solution.py:25
  99.1 6.5 %collective-permute-start.17 = (bf16[1040,128]{1,0:T(8,128)(2,1)S(1)}, bf16[1040,128]{1,0:T(8,128)(2,1)S(1)}, u32[]{:S(2)}, u32[]{:S(2)}) collective-permute-start(bf16[1040,128]{1,0:T(8,128)(2,1)S(1)} %get-tuple-element.92), channel_id=1, source_target_pairs={{0,1},{1,0},{2,3},{3,2},{4,5},{5,4},{6,7},{7,6},{8,9},{9,8},{10,11... | collective-permute-start | bytes 798728 | tf_op jit(solution)/shard_map/ppermute | solution.py:25
  100.0 8.5 %collective-permute-start.21 = (bf16[512,128]{1,0:T(8,128)(2,1)S(1)}, bf16[512,128]{1,0:T(8,128)(2,1)S(1)}, u32[]{:S(2)}, u32[]{:S(2)}) collective-permute-start(bf16[512,128]{1,0:T(8,128)(2,1)S(1)} %get-tuple-element.98), channel_id=1, source_target_pairs={{0,6},{1,7},{2,4},{3,5},{4,2},{5,3},{6,0},{7,1},{8,14},{9,15},{10,... | collective-permute-start | bytes 393224 | tf_op jit(solution)/shard_map/ppermute | solution.py:25
  102.0 8.1 %collective-permute-start.22 = (bf16[512,128]{1,0:T(8,128)(2,1)S(1)}, bf16[512,128]{1,0:T(8,128)(2,1)S(1)}, u32[]{:S(2)}, u32[]{:S(2)}) collective-permute-start(bf16[512,128]{1,0:T(8,128)(2,1)S(1)} %get-tuple-element.99), channel_id=1, source_target_pairs={{0,4},{1,5},{2,6},{3,7},{4,0},{5,1},{6,2},{7,3},{8,12},{9,13},{10,... | collective-permute-start | bytes 393224 | tf_op jit(solution)/shard_map/ppermute | solution.py:25
  102.0 8.1 %collective-permute-start.23 = (bf16[512,128]{1,0:T(8,128)(2,1)S(1)}, bf16[512,128]{1,0:T(8,128)(2,1)S(1)}, u32[]{:S(2)}, u32[]{:S(2)}) collective-permute-start(bf16[512,128]{1,0:T(8,128)(2,1)S(1)} %get-tuple-element.100), channel_id=1, source_target_pairs={{0,2},{1,3},{2,0},{3,1},{4,6},{5,7},{6,4},{7,5},{8,10},{9,11},{10,... | collective-permute-start | bytes 393224 | tf_op jit(solution)/shard_map/ppermute | solution.py:25
  105.6 8.9 %collective-permute-start.18 = (bf16[272,128]{1,0:T(8,128)(2,1)S(1)}, bf16[272,128]{1,0:T(8,128)(2,1)S(1)}, u32[]{:S(2)}, u32[]{:S(2)}) collective-permute-start(bf16[272,128]{1,0:T(8,128)(2,1)S(1)} %get-tuple-element.94), channel_id=1, source_target_pairs={{0,2},{1,3},{2,0},{3,1},{4,6},{5,7},{6,4},{7,5},{8,10},{9,11},{10,... | collective-permute-start | bytes 208904 | tf_op jit(solution)/shard_map/ppermute | solution.py:25
  105.7 8.8 %collective-permute-start.19 = (bf16[272,128]{1,0:T(8,128)(2,1)S(1)}, bf16[272,128]{1,0:T(8,128)(2,1)S(1)}, u32[]{:S(2)}, u32[]{:S(2)}) collective-permute-start(bf16[272,128]{1,0:T(8,128)(2,1)S(1)} %get-tuple-element.95), channel_id=1, source_target_pairs={{0,4},{1,5},{2,6},{3,7},{4,0},{5,1},{6,2},{7,3},{8,12},{9,13},{10,... | collective-permute-start | bytes 208904 | tf_op jit(solution)/shard_map/ppermute | solution.py:25
  108.4 6.1 %collective-permute-start.20 = (bf16[272,128]{1,0:T(8,128)(2,1)S(1)}, bf16[272,128]{1,0:T(8,128)(2,1)S(1)}, u32[]{:S(2)}, u32[]{:S(2)}) collective-permute-start(bf16[272,128]{1,0:T(8,128)(2,1)S(1)} %get-tuple-element.96), channel_id=1, source_target_pairs={{0,6},{1,7},{2,4},{3,5},{4,2},{5,3},{6,0},{7,1},{8,14},{9,15},{10,... | collective-permute-start | bytes 208904 | tf_op jit(solution)/shard_map/ppermute | solution.py:25
  123.0 4.5 %collective-permute-start.27 = (f32[8,128]{1,0:T(8,128)S(1)}, f32[8,128]{1,0:T(8,128)S(1)}, u32[]{:S(2)}, u32[]{:S(2)}) collective-permute-start(f32[8,128]{1,0:T(8,128)S(1)} %add.7.refs_0_), channel_id=1, source_target_pairs={{0,4},{1,5},{2,6},{3,7},{4,0},{5,1},{6,2},{7,3},{8,12},{9,13},{10,... | collective-permute-start | bytes 12296 | tf_op jit(solution)/shard_map/ppermute | solution.py:25
  (12 other events, 85.3 us)

commit v4 on v3

--- a/solution.py
+++ b/solution.py
@@ -7,6 +7,7 @@
 from jax.experimental.pallas import tpu as pltpu
 from jax.sharding import PartitionSpec as P
 
+
 epsilon = 1e-06
 F32 = jnp.float32
 BF16 = jnp.bfloat16
@@ -15,14 +16,14 @@
 SMEM = pltpu.SMEM
 
 
-def passed_along(block, axis, distance):
-    devices = range(lax.axis_size(axis))
-    route = [(i - distance, i) for i in devices if i - distance in devices]
-    return lax.ppermute(block, axis, route)
-
-
-def swapped(block, mask):
-    return lax.ppermute(block, "blk", [(i, i ^ mask) for i in range(lax.axis_size("blk"))])
+def handed(block, targets, distance):
+    return lax.ppermute(block, "seg", [(s - distance, s) for s in targets])
+
+
+def swapped(block, mask, segments):
+    blk = lax.axis_size("blk")
+    route = [(s * blk + i, s * blk + (i ^ mask)) for s in segments for i in range(blk)]
+    return lax.ppermute(block, ("seg", "blk"), route)
 
 
 class Plan:
@@ -35,6 +36,10 @@
         self.n = tiles * blk
         self.a_rows = self.Ta * tile
         self.b_rows = self.Tb * tile
+        self.H = tiles // 2
+        self.group = next(
+            c for c in range(max(1, channels // 2), 0, -1) if channels % c == 0
+        )
 
     def slot(self, feed, me):
         tiles = jnp.int32(self.T)
@@ -124,9 +129,16 @@
 
 
 def update_second(plan, ins, outs, send):
-    (x_in, rows, cols, energy), arrived = ins[:4], ins[4:]
+    (x_in, rows, cols, energy, own, own_row, helped), arrived = ins[:7], ins[7:]
     q_out, h_out, known_out = outs
-    tile, row = received_sums(plan, arrived)
+    odd = in_odd_segment()
+    half_tile, half_row = received_sums(plan, arrived)
+    row = jnp.where(odd, own_row[0:1, :], half_row)
+
+    def tile(k):
+        at = pl.ds(k * plan.D, plan.D)
+        return jnp.where(odd, own[at, :], half_tile(k) + helped[at, :].astype(F32))
+
     square = lane(row, 0)
     scale = lax.rsqrt(square / plan.entries + epsilon)
     known_out[...] = jnp.broadcast_to(scale * scale * square, known_out.shape)
@@ -170,7 +182,7 @@
     return [total(s) for s in sums]
 
 
-def update_last(plan, ins, outs, send):
+def update_last(plan, ins, outs):
     (q_in, h_in, z_in, rows, cols, energy), arrived = ins[:6], ins[6:]
     q_out, z_out, coef_out = outs
     tile, row = received_sums(plan, arrived)
@@ -192,7 +204,7 @@
     return [total(s) for s in sums]
 
 
-def on_chip(name, body, ins, outs, scratch=()):
+def on_chip(body, ins, outs, scratch=()):
     spaces = [SMEM if len(x.shape) == 1 else VMEM for x in ins]
     return pl.pallas_call(
         body,
@@ -201,77 +213,153 @@
         out_shape=list(outs),
         scratch_shapes=list(scratch),
         compiler_params=pltpu.CompilerParams(vmem_limit_bytes=16 * 2**20),
-        name=name,
     )(*ins)
 
 
-def operator_step(plan, name, update, ins, state_shapes, left, right, slots):
-    D, T, W = plan.D, plan.T, plan.W
-    pairs = T // 2
+def in_odd_segment():
+    return lax.axis_index("seg") % 2 == 1
+
+
+class Block:
+    def __init__(self, left, right, low, slots):
+        self.left, self.right, self.low, self.slots = left, right, low, slots
+
+
+def multiply(plan, pairs, half_ref, sum_ref):
+    D, W, group = plan.D, plan.W, plan.group
+    none = jnp.zeros((D, D), BF16)
+
+    def rows(place, first, count):
+        ref, block = place
+        return ref[pl.ds(pl.multiple_of((block * W + first) * D, D), count * D), :]
+
+    def several(step, carry):
+        first = step * group
+        for pair in pairs:
+            v = [b.low[0][pl.ds(b.low[1] * D, D), :] for b in pair]
+            both = jnp.concatenate(
+                [jnp.concatenate([v[0], none], 1), jnp.concatenate([none, v[1]], 1)], 0
+            )
+            tiles = [rows(b.left, first, group) for b in pair]
+            half_ref[...] = jnp.dot(
+                jnp.concatenate(tiles, 1), both, preferred_element_type=F32
+            ).astype(BF16)
+            for w in range(group):
+                for side, b in enumerate(pair):
+                    product = jnp.dot(
+                        half_ref[pl.ds(w * D, D), pl.ds(side * D, D)],
+                        rows(b.right, first + w, 1),
+                        preferred_element_type=F32,
+                    )
+                    ref, block = b.slots
+                    slot = ref[block * W + first + w]
+                    sum_ref[pl.ds(pl.multiple_of(slot * D, D), D), :] += product
+        return carry
+
+    lax.fori_loop(0, W // group, several, 0)
+
+
+def flush(plan, row, sum_ref, message_refs):
+    first = 0
+    for ref in message_refs:
+        rows = ref.shape[0] // plan.D * plan.D
+        ref[pl.ds(0, rows), :] = sum_ref[pl.ds(first, rows), :].astype(BF16)
+        first += rows
+    for ref in message_refs[:2]:
+        ref[pl.ds(plan.Z * plan.a_rows, PAD), :] = row
+
+
+def work_space(plan):
+    return [
+        VMEM((plan.group * plan.D, 2 * plan.D), BF16),
+        VMEM(((plan.n + 1) * plan.D, plan.D), F32),
+    ]
+
+
+def first_own(plan, low, row, slots, left, right):
+    def body(low_ref, row_ref, slot_ref, left_ref, right_ref, *refs):
+        message_refs, (half_ref, sum_ref) = refs[:-2], refs[-2:]
+
+        @pl.when(in_odd_segment())
+        def _():
+            def at(k):
+                return Block((left_ref, k), (right_ref, k), (low_ref, k), (slot_ref, k))
+
+            sum_ref[...] = jnp.zeros(sum_ref.shape, F32)
+            pairs = [(at(k), at(k + plan.H)) for k in range(plan.H)]
+            multiply(plan, pairs, half_ref, sum_ref)
+            flush(plan, row_ref[...], sum_ref, message_refs)
+
+    ins = [low, row, slots, left, right]
+    return on_chip(body, ins, plan.messages(), work_space(plan))
+
+
+def first_half(plan, low, row, slots, left, right, other_low, other_slots, held, other_right):
+    def body(*refs):
+        low_ref, row_ref, slot_ref, left_ref, right_ref = refs[:5]
+        other_low_ref, other_slot_ref, held_ref, other_right_ref = refs[5:9]
+        message_refs, (half_ref, sum_ref) = refs[9:-2], refs[-2:]
+        odd = in_odd_segment()
+
+        def all_of(places):
+            def at(k):
+                return Block(*[(p, k) for p in places])
+
+            sum_ref[...] = jnp.zeros(sum_ref.shape, F32)
+            pairs = [(at(k), at(k + plan.H // 2)) for k in range(plan.H // 2)]
+            multiply(plan, pairs, half_ref, sum_ref)
+            flush(plan, row_ref[...], sum_ref, message_refs)
+
+        @pl.when(odd)
+        def _():
+            all_of((held_ref, other_right_ref, other_low_ref, other_slot_ref))
+
+        @pl.when(jnp.logical_not(odd))
+        def _():
+            all_of((left_ref, right_ref, low_ref, slot_ref))
+
+    ins = [low, row, slots, left, right, other_low, other_slots, held, other_right]
+    return on_chip(body, ins, plan.messages(), work_space(plan))
+
+
+def operator_step(plan, update, ins, state_shapes, lefts, right, slots):
     n_in, n_state = len(ins), len(state_shapes)
-    group = next(c for c in range(max(1, W // 2), 0, -1) if W % c == 0)
 
     def body(*refs):
-        in_refs = refs[:n_in]
-        left_ref, right_ref, slot_ref = refs[n_in : n_in + 3]
-        state_refs = refs[n_in + 3 : n_in + 3 + n_state]
-        message_refs = refs[n_in + 3 + n_state : -3]
+        own_ref, first_ref, last_ref, right_ref, slot_ref = refs[n_in : n_in + 5]
+        state_refs = refs[n_in + 5 : n_in + 5 + n_state]
+        message_refs = refs[n_in + 5 + n_state : -3]
         low_ref, half_ref, sum_ref = refs[-3:]
+        odd = in_odd_segment()
 
         def send(k, value):
-            low_ref[pl.ds(k * D, D), :] = value.astype(BF16)
-
-        row = update(plan, in_refs, state_refs, send)
-        if isinstance(row, list):
-            row = packed_row(row, D)
-        for ref in message_refs[:2]:
-            ref[pl.ds(plan.Z * plan.a_rows, PAD), :] = row
+            low_ref[pl.ds(k * plan.D, plan.D), :] = value.astype(BF16)
+
+        row = packed_row(update(plan, refs[:n_in], state_refs, send), plan.D)
         sum_ref[...] = jnp.zeros(sum_ref.shape, F32)
-        none = jnp.zeros((D, D), BF16)
-
-        def several(step, carry):
-            for h in range(pairs):
-                blocks = (h, h + pairs)
-                v = [low_ref[pl.ds(k * D, D), :] for k in blocks]
-                both = jnp.concatenate(
-                    [jnp.concatenate([v[0], none], 1), jnp.concatenate([none, v[1]], 1)], 0
-                )
-                firsts = [k * W + step * group for k in blocks]
-                tiles = [
-                    left_ref[pl.ds(pl.multiple_of(f * D, D), group * D), :] for f in firsts
-                ]
-                half_ref[...] = jnp.dot(
-                    jnp.concatenate(tiles, 1), both, preferred_element_type=F32
-                ).astype(BF16)
-                for w in range(group):
-                    for side, f in enumerate(firsts):
-                        product = jnp.dot(
-                            half_ref[pl.ds(w * D, D), pl.ds(side * D, D)],
-                            right_ref[pl.ds(pl.multiple_of((f + w) * D, D), D), :],
-                            preferred_element_type=F32,
-                        )
-                        slot = slot_ref[f + w]
-                        at = pl.ds(pl.multiple_of(slot * D, D), D)
-                        sum_ref[at, :] += product
-            return carry
-
-        lax.fori_loop(0, W // group, several, 0)
-        first = 0
-        for ref in message_refs:
-            rows = ref.shape[0] // D * D
-            ref[pl.ds(0, rows), :] = sum_ref[pl.ds(first, rows), :].astype(BF16)
-            first += rows
+
+        def all_of(place):
+            def at(k):
+                return Block(place(k), (right_ref, k), (low_ref, k), (slot_ref, k))
+
+            pairs = [(at(k), at(k + plan.H)) for k in range(plan.H)]
+            multiply(plan, pairs, half_ref, sum_ref)
+
+        @pl.when(odd)
+        def _():
+            all_of(lambda k: (own_ref, k))
+
+        @pl.when(jnp.logical_not(odd))
+        def _():
+            all_of(lambda k: (first_ref, k) if k < plan.H else (last_ref, k - plan.H))
+
+        flush(plan, row, sum_ref, message_refs)
 
     results = on_chip(
-        name,
         body,
-        list(ins) + [left, right, slots],
+        list(ins) + list(lefts) + [right, slots],
         list(state_shapes) + plan.messages(),
-        [
-            VMEM((T * D, D), BF16),
-            VMEM((group * D, 2 * D), BF16),
-            VMEM(((plan.n + 1) * D, D), F32),
-        ],
+        [VMEM((plan.T * plan.D, plan.D), BF16)] + work_space(plan),
     )
     return results[:n_state], results[n_state:]
 
@@ -288,11 +376,11 @@
     n_in = len(ins)
 
     def body(*refs):
-        sums = update_last(plan, refs[:n_in], refs[n_in:-1], None)
+        sums = update_last(plan, refs[:n_in], refs[n_in:-1])
         refs[-1][...] = row_of(plan, sums)
 
     row = jax.ShapeDtypeStruct((8, plan.D), F32)
-    return on_chip("last_step", body, ins, list(state_shapes) + [row])
+    return on_chip(body, ins, list(state_shapes) + [row])
 
 
 def outcome(plan, q, z, first, second, *sums):
@@ -306,7 +394,7 @@
         coef_ref[...] = row_of(plan, values)
 
     row = jax.ShapeDtypeStruct((8, plan.D), F32)
-    return on_chip("outcome", body, [q, z, first, second, *sums], [q, row])
+    return on_chip(body, [q, z, first, second, *sums], [q, row])
 
 
 def middle_a(plan, keep, got):
@@ -322,7 +410,7 @@
             out[pl.ds(rows, PAD), :] = scalars
 
     shape = jax.ShapeDtypeStruct((rows + PAD, plan.D), BF16)
-    return on_chip("middle_a", body, [keep, got], [shape] * plan.Z)
+    return on_chip(body, [keep, got], [shape] * plan.Z)
 
 
 def middle_b(plan, parts):
@@ -335,65 +423,99 @@
             out[...] = functools.reduce(lambda u, v: u + v, tiles).astype(out.dtype)
 
     shapes = [jax.ShapeDtypeStruct((rows, plan.D), d) for d in (F32, BF16)]
-    return on_chip("middle_b", body, parts, shapes)
-
-
-def exchanged(plan, messages):
+    return on_chip(body, parts, shapes)
+
+
+def exchanged(plan, messages, segments):
     keep, send, b_parts = messages[0], messages[1], messages[2:]
     others = range(plan.Z - 1, 0, -1)
-    got = swapped(send, 1)
-    b_got = [swapped(b_parts[z], 2 * z) for z in others]
+    got = swapped(send, 1, segments)
+    b_got = [swapped(b_parts[z], 2 * z, segments) for z in others]
     a_parts = middle_a(plan, keep, got)
-    a_last = [swapped(a_parts[z], 2 * z) for z in others]
+    a_last = [swapped(a_parts[z], 2 * z, segments) for z in others]
     b_keep, b_send = middle_b(plan, [b_parts[0]] + b_got)
-    return [a_parts[0]] + a_last[::-1] + [b_keep, swapped(b_send, 1)]
-
-
-def prepared(plan, start, rows, cols, feeds, right):
-    def body(start_ref, rows_ref, cols_ref, feed_ref, right_ref, *outs):
-        x_ref, low_ref, row_ref, slot_ref, held_ref, done = outs
-        copy = pltpu.make_async_copy(right_ref, held_ref, done)
-        copy.start()
+    return [a_parts[0]] + a_last[::-1] + [b_keep, swapped(b_send, 1, segments)]
+
+
+def gathered(plan, arrived, dtype):
+    def body(*refs):
+        tile, row = received_sums(plan, refs[:-2])
+        for k in range(plan.T):
+            refs[-2][pl.ds(k * plan.D, plan.D), :] = tile(k).astype(dtype)
+        refs[-1][...] = jnp.broadcast_to(row, refs[-1].shape)
+
+    sums = jax.ShapeDtypeStruct((plan.T * plan.D, plan.D), dtype)
+    row = jax.ShapeDtypeStruct((8, plan.D), F32)
+    return on_chip(body, arrived, [sums, row])
+
+
+def copying(sources, slices):
+    def body(*refs):
+        n = len(sources)
+        copies = []
+        for i, (source, first, rows) in enumerate(slices):
+            done = refs[n + len(slices)].at[i]
+            from_ref = refs[source].at[pl.ds(first, rows)]
+            copies.append(pltpu.make_async_copy(from_ref, refs[n + i], done))
+        for copy in copies:
+            copy.start()
+        for copy in copies:
+            copy.wait()
+
+    return pl.pallas_call(
+        body,
+        in_specs=[pl.BlockSpec(memory_space=pl.ANY)] * len(sources),
+        out_specs=[pl.BlockSpec(memory_space=VMEM)] * len(slices),
+        out_shape=[
+            jax.ShapeDtypeStruct((rows, sources[i].shape[1]), sources[i].dtype)
+            for i, _, rows in slices
+        ],
+        scratch_shapes=[pltpu.SemaphoreType.DMA((len(slices),))],
+        compiler_params=pltpu.CompilerParams(vmem_limit_bytes=16 * 2**20),
+    )(*[pltpu.with_memory_space_constraint(x, pltpu.HBM) for x in sources])
+
+
+def prepared(plan, start, rows, cols, feeds):
+    def body(start_ref, rows_ref, cols_ref, feed_ref, *outs):
+        x_ref, low_ref, row_ref, slot_ref, last_low_ref, last_slot_ref = outs
         me = lax.axis_index("blk")
 
         def several(w, carry):
             for k in range(plan.T):
-                slot_ref[k * plan.W + w] = plan.slot(feed_ref[k, w], me)
+                slot = plan.slot(feed_ref[k, w], me)
+                slot_ref[k * plan.W + w] = slot
+                if k >= plan.H:
+                    last_slot_ref[(k - plan.H) * plan.W + w] = slot
             return carry
 
         lax.fori_loop(0, plan.W, several, 0)
 
         def send(k, value):
             low_ref[pl.ds(k * plan.D, plan.D), :] = value.astype(BF16)
+            if k >= plan.H:
+                last_low_ref[pl.ds((k - plan.H) * plan.D, plan.D), :] = value.astype(BF16)
 
         sums = update_first(plan, (start_ref, rows_ref, cols_ref), (x_ref,), send)
         row_ref[...] = packed_row(sums, plan.D)
-        copy.wait()
 
     chip = pl.BlockSpec(memory_space=VMEM)
     scalar = pl.BlockSpec(memory_space=SMEM)
+    last = plan.T - plan.H
     return pl.pallas_call(
         body,
-        in_specs=[chip, scalar, scalar, scalar, pl.BlockSpec(memory_space=pltpu.HBM)],
-        out_specs=[chip, chip, chip, scalar, chip],
+        in_specs=[chip, scalar, scalar, scalar],
+        out_specs=[chip, chip, chip, scalar, chip, scalar],
         out_shape=[
             jax.ShapeDtypeStruct(start.shape, F32),
             jax.ShapeDtypeStruct(start.shape, BF16),
             jax.ShapeDtypeStruct((PAD, plan.D), BF16),
             jax.ShapeDtypeStruct((plan.T * plan.W,), jnp.int32),
-            right,
+            jax.ShapeDtypeStruct((last * plan.D, plan.D), BF16),
+            jax.ShapeDtypeStruct((last * plan.W,), jnp.int32),
         ],
-        scratch_shapes=[pltpu.SemaphoreType.DMA(())],
         compiler_params=pltpu.CompilerParams(vmem_limit_bytes=16 * 2**20),
         name="prepared",
-    )(start, rows, cols, feeds, right)
-
-
-def update_none(plan, ins, outs, send):
-    low, row = ins
-    for k in range(plan.T):
-        send(k, low[pl.ds(k * plan.D, plan.D), :])
-    return row[...]
+    )(start, rows, cols, feeds)
 
 
 def local(
@@ -407,48 +529,81 @@
 ):
     T, W, D = left_environment.shape[1:4]
     plan = Plan(T, W, D, lax.axis_size("blk"))
-    left = passed_along(left_environment, "seg", 1).reshape(T * W * D, D)
+    segments = range(lax.axis_size("seg"))
+    evens = [s for s in segments if s % 2 == 0]
+    odds = [s for s in segments if s % 2 == 1]
+    helped = [s for s in evens if s > 0]
+    helpers = [s - 1 for s in helped]
+
+    left = left_environment.reshape(T * W * D, D)
     right = right_environment.reshape(T * W * D, D)
     rows, cols, energy = sector_rows[0], sector_cols[0], block_energy[0]
     vector = jax.ShapeDtypeStruct((T * D, D), F32)
     row = jax.ShapeDtypeStruct((8, D), F32)
     start = start_vector.reshape(T * D, D)
 
-    x, low, square, slots, right = prepared(plan, start, rows, cols, feed_block[0], right)
-    _, messages = operator_step(
-        plan, "step_0", update_none, [low, square], [], left, right, slots
+    first_rows = plan.H * W * D
+    last_rows = T * W * D - first_rows
+    sent_left, sent_right = copying([left, right], [(0, 0, first_rows), (1, first_rows, last_rows)])
+    left_first = handed(sent_left, helped, 1)
+    right_last = handed(sent_right, helpers, -1)
+    left_own = handed(left_environment, odds, 1).reshape(T * W * D, D)
+    held_left, held_right = copying([left, right], [(0, first_rows, last_rows), (1, 0, T * W * D)])
+    left_last = handed(held_left, helped, 1)
+    x, low, square, slots, last_low, last_slots = prepared(
+        plan, start, rows, cols, feed_block[0]
     )
-    arrived = exchanged(plan, messages)
+    other_low = handed(last_low, helpers, -1)
+    other_slots = handed(last_slots, helpers, -1)
+
+    messages = first_own(plan, low, square, slots, left_own, held_right)
+    arrived = exchanged(plan, messages, odds)
+    own, own_row = gathered(plan, arrived, F32)
+    messages = first_half(
+        plan,
+        low,
+        square,
+        slots,
+        left_first,
+        held_right,
+        other_low,
+        other_slots,
+        held_left,
+        right_last,
+    )
+    half = exchanged(plan, messages, evens + helpers)
+    help_sum, _ = gathered(plan, half, BF16)
+    help_sum = handed(help_sum, helped, 1)
+    lefts = [left_own, left_first, left_last]
     (q0, h0, known), messages = operator_step(
         plan,
-        "step_1",
         update_second,
-        [x, rows, cols, energy] + arrived,
+        [x, rows, cols, energy, own, own_row, help_sum] + half,
         [vector, vector, row],
-        left,
-        right,
+        lefts,
+        held_right,
         slots,
     )
-    arrived = exchanged(plan, messages)
+    arrived = exchanged(plan, messages, segments)
     (q1, h1, z1, first), messages = operator_step(
         plan,
-        "step_2",
         update_third,
         [q0, h0, known, rows, cols, energy] + arrived,
         [vector, vector, vector, row],
-        left,
-        right,
+        lefts,
+        held_right,
         slots,
     )
-    arrived = exchanged(plan, messages)
+    arrived = exchanged(plan, messages, segments)
     q2, z2, second, sums = last_step(
         plan, [q1, h1, z1, rows, cols, energy] + arrived, [vector, vector, row]
     )
     mask = 1
     while 2 * mask < plan.B:
-        sums = sums + swapped(sums, mask)
+        sums = sums + swapped(sums, mask, segments)
         mask *= 2
-    residual, coefficients = outcome(plan, q2, z2, first, second, sums, swapped(sums, mask))
+    last = swapped(sums, mask, segments)
+    residual, coefficients = outcome(plan, q2, z2, first, second, sums, last)
     return (coefficients[:1, :6], residual.reshape(1, T, D, D))
 
 

time: 129 us -> 160 us (1.24); the launches traced: 129 us -> 157 us
  starting transfers between devices: 35.1 us -> 73.9 us
  waiting for transfers between devices: 69.2 us -> 57.8 us
  Pallas kernels: 18.1 us -> 23.7 us
  local copies, waits for them, and re-layouts: 5.67 us -> 0.54 us
    ppermute x28 -> x42, starting transfers between devices: 35.1 us -> 73.9 us  [the longest x35 55.1 us: swapped(): return lax.ppermute(block, ('seg', 'blk'), route)]
    ppermute x28 -> x42, waiting for transfers between devices: 69.2 us -> 57.8 us  [the longest x35 30.5 us: swapped(): return lax.ppermute(block, ('seg', 'blk'), route)]
    unnamed x16 -> x10, local copies, waits for them, and re-layouts: 5.16 us -> 0.03 us
    pallas_call x1 -> x3, Pallas kernels: 2.99 us -> 7.87 us  [the longest x2 5.28 us: copying(): pl.pallas_call(body, in_specs=[pl.BlockSpec(memory_space=pl.ANY)] * len(s...]
    pallas_call x11 -> x16, Pallas kernels: 15.1 us -> 15.8 us  [on_chip(): pl.pallas_call(body, in_specs=[pl.BlockSpec(memory_space=s) for s in spac...]
  transfers between devices with their start and end apart: 28 -> 42, of which waited for: 11 -> 14; matrix products, arithmetic and copies ran while one was open for 0% -> 0% of each run, Pallas kernels for 3% -> 8%
where the time goes in v4:
time: 160 us; the launch traced here: 157 us
  starting transfers between devices  73.9 us (46%)
  waiting for transfers between devices  57.8 us (36%)
  Pallas kernels  23.7 us (15%)
    ppermute x35, starting transfers between devices, swapped(): return lax.ppermute(block, ('seg', 'blk'), route)  55.1 us
    ppermute x35, waiting for transfers between devices, swapped(): return lax.ppermute(block, ('seg', 'blk'), route)  30.5 us
    ppermute x7, waiting for transfers between devices, handed(): return lax.ppermute(block, 'seg', [(s - distance, s) for s in targets])  27.3 us
    ppermute x7, starting transfers between devices, handed(): return lax.ppermute(block, 'seg', [(s - distance, s) for s in targets])  18.8 us
    pallas_call x16, Pallas kernels, on_chip(): pl.pallas_call(body, in_specs=[pl.BlockSpec(memory_space=s) for s in spac...  15.8 us
    pallas_call x2, Pallas kernels, copying(): pl.pallas_call(body, in_specs=[pl.BlockSpec(memory_space=pl.ANY)] * len(s...  5.28 us
  transfers between devices with their start and end apart: 42, of which 14 were waited for; matrix products, arithmetic and copies ran while one was open for 0% of the time, Pallas kernels for 8%

profile of v4, /device:TPU:6, one launch (start us, length us, event | category | flops | bytes accessed | tf_op | source)
XLA Modules:
  0.0 157.1 jit_solution(12819973844784493711)
XLA Ops:
  6.3 4.7 %collective-permute-start.12 = (bf16[8704,128]{1,0:T(8,128)(2,1)S(1)}, bf16[8704,128]{1,0:T(8,128)(2,1)S(1)}, u32[]{:S(2)}, u32[]{:S(2)}) collective-permute-start(bf16[8704,128]{1,0:T(8,128)(2,1)S(1)} %get-tuple-element.99), channel_id=1, source_target_pairs={{16,8},{17,9},{18,10},{19,11},{20,12},{21,13},{22,14},{23,15}} | collective-permute-start | bytes 6684680 | tf_op jit(solution)/shard_map/ppermute | solution.py:20
  11.0 3.0 %shard_map.86 = (bf16[8704,128]{1,0:T(8,128)(2,1)S(1)}, bf16[17408,128]{1,0:T(8,128)(2,1)S(1)}) custom-call(bf16[17408,128]{1,0:T(8,128)(2,1)} %bitcast.28, bf16[17408,128]{1,0:T(8,128)(2,1)} %bitcast.26), custom_call_target="tpu_custom_call" | custom-call | tf_op jit(solution)/shard_map/pallas_call | solution.py:465
  15.3 2.6 %prepared.1 = (f32[512,128]{1,0:T(8,128)S(1)}, bf16[512,128]{1,0:T(8,128)(2,1)S(1)}, bf16[16,128]{1,0:T(8,128)(2,1)S(1)}, s32[136]{0:T(256)S(1)}, bf16[256,128]{1,0:T(8,128)(2,1)S(1)}, /*index=5*/s32[68]{0:T(128)S(1)}) custom-call(bf16[512,128]{1,0:T(8,128)(2,1)S(1)} %bitcast.12, s32[4]{0:T(128)S(1)} %bitcast.13, s32[4]{0:T(128)S(1)} %bitcast.17, ...), custom_call_target="tpu_custom_call" | custom-call | tf_op jit(solution)/shard_map/prepared/pallas_call | solution.py:504
  17.9 4.4 %collective-permute-start.11 = (s32[68]{0:T(128)S(1)}, s32[68]{0:T(128)S(1)}, u32[]{:S(2)}, u32[]{:S(2)}) collective-permute-start(s32[68]{0:T(128)S(1)} %get-tuple-element.97), channel_id=1, source_target_pairs={{16,8},{17,9},{18,10},{19,11},{20,12},{21,13},{22,14},{23,15}} | collective-permute-start | bytes 824 | tf_op jit(solution)/shard_map/ppermute | solution.py:20
  22.3 13.5 %collective-permute-done.11.refs_6_ = s32[68]{0:T(128)S(1)} collective-permute-done((s32[68]{0:T(128)S(1)}, s32[68]{0:T(128)S(1)}, u32[]{:S(2)}, u32[]{:S(2)}) %collective-permute-start.11) | collective-permute-done | bytes 304 | tf_op jit(solution)/shard_map/ppermute | solution.py:20
  35.9 3.9 %collective-permute-start.10 = (bf16[256,128]{1,0:T(8,128)(2,1)S(1)}, bf16[256,128]{1,0:T(8,128)(2,1)S(1)}, u32[]{:S(2)}, u32[]{:S(2)}) collective-permute-start(bf16[256,128]{1,0:T(8,128)(2,1)S(1)} %get-tuple-element.96), channel_id=1, source_target_pairs={{16,8},{17,9},{18,10},{19,11},{20,12},{21,13},{22,14},{23,15}} | collective-permute-start | bytes 196616 | tf_op jit(solution)/shard_map/ppermute | solution.py:20
  41.6 2.9 %shard_map.92 = (bf16[1040,128]{1,0:T(8,128)(2,1)S(1)}, bf16[1040,128]{1,0:T(8,128)(2,1)S(1)}, bf16[512,128]{1,0:T(8,128)(2,1)S(1)}, bf16[512,128]{1,0:T(8,128)(...) custom-call(bf16[512,128]{1,0:T(8,128)(2,1)S(1)} %get-tuple-element.77.low_ref.refs_0_, ...), custom_call_target="tpu_custom_call" | custom-call | tf_op jit(solution)/shard_map/pallas_call | solution.py:209
  44.5 5.5 %collective-permute-start.17 = (bf16[512,128]{1,0:T(8,128)(2,1)S(1)}, bf16[512,128]{1,0:T(8,128)(2,1)S(1)}, u32[]{:S(2)}, u32[]{:S(2)}) collective-permute-start(bf16[512,128]{1,0:T(8,128)(2,1)S(1)} %get-tuple-element.107), channel_id=1, source_target_pairs={{0,6},{1,7},{2,4},{3,5},{4,2},{5,3},{6,0},{7,1},{16,22},{17,23},{1... | collective-permute-start | bytes 393224 | tf_op jit(solution)/shard_map/ppermute | solution.py:26
  54.4 2.7 %collective-permute-start.19 = (bf16[512,128]{1,0:T(8,128)(2,1)S(1)}, bf16[512,128]{1,0:T(8,128)(2,1)S(1)}, u32[]{:S(2)}, u32[]{:S(2)}) collective-permute-start(bf16[512,128]{1,0:T(8,128)(2,1)S(1)} %get-tuple-element.109), channel_id=1, source_target_pairs={{0,2},{1,3},{2,0},{3,1},{4,6},{5,7},{6,4},{7,5},{16,18},{17,19},{1... | collective-permute-start | bytes 393224 | tf_op jit(solution)/shard_map/ppermute | solution.py:26
  57.1 4.0 %collective-permute-done.18.refs_2_ = bf16[512,128]{1,0:T(8,128)(2,1)S(1)} collective-permute-done((bf16[512,128]{1,0:T(8,128)(2,1)S(1)}, bf16[512,128]{1,0:T(8,128)(2,1)S(1)}, u32[]{:S(2)}, u32[]{:S(2)}) %collective-permute-start.18) | collective-permute-done | bytes 131104 | tf_op jit(solution)/shard_map/ppermute | solution.py:26
  62.5 3.1 %collective-permute-start.20 = (bf16[256,128]{1,0:T(8,128)(2,1)S(1)}, bf16[256,128]{1,0:T(8,128)(2,1)S(1)}, u32[]{:S(2)}, u32[]{:S(2)}) collective-permute-start(bf16[256,128]{1,0:T(8,128)(2,1)S(1)} %get-tuple-element.111), channel_id=1, source_target_pairs={{0,1},{1,0},{2,3},{3,2},{4,5},{5,4},{6,7},{7,6},{16,17},{17,16},{1... | collective-permute-start | bytes 196616 | tf_op jit(solution)/shard_map/ppermute | solution.py:26
  72.5 4.8 %collective-permute-start.15 = (bf16[272,128]{1,0:T(8,128)(2,1)S(1)}, bf16[272,128]{1,0:T(8,128)(2,1)S(1)}, u32[]{:S(2)}, u32[]{:S(2)}) collective-permute-start(bf16[272,128]{1,0:T(8,128)(2,1)S(1)} %get-tuple-element.104), channel_id=1, source_target_pairs={{0,4},{1,5},{2,6},{3,7},{4,0},{5,1},{6,2},{7,3},{16,20},{17,21},{1... | collective-permute-start | bytes 208904 | tf_op jit(solution)/shard_map/ppermute | solution.py:26
  77.3 3.4 %collective-permute-start.16 = (bf16[272,128]{1,0:T(8,128)(2,1)S(1)}, bf16[272,128]{1,0:T(8,128)(2,1)S(1)}, u32[]{:S(2)}, u32[]{:S(2)}) collective-permute-start(bf16[272,128]{1,0:T(8,128)(2,1)S(1)} %get-tuple-element.105), channel_id=1, source_target_pairs={{0,6},{1,7},{2,4},{3,5},{4,2},{5,3},{6,0},{7,1},{16,22},{17,23},{1... | collective-permute-start | bytes 208904 | tf_op jit(solution)/shard_map/ppermute | solution.py:26
  81.5 3.9 %collective-permute-done.16.refs_3_.refs_10_ = bf16[272,128]{1,0:T(8,128)(2,1)S(1)} collective-permute-done((bf16[272,128]{1,0:T(8,128)(2,1)S(1)}, bf16[272,128]{1,0:T(8,128)(2,1)S(1)}, u32[]{:S(2)}, u32[]{:S(2)}) %collective-permute-start.16) | collective-permute-done | bytes 69664 | tf_op jit(solution)/shard_map/ppermute | solution.py:26
  89.5 11.9 %collective-permute-done.21.refs_6_ = bf16[512,128]{1,0:T(8,128)(2,1)S(1)} collective-permute-done((bf16[512,128]{1,0:T(8,128)(2,1)S(1)}, bf16[512,128]{1,0:T(8,128)(2,1)S(1)}, u32[]{:S(2)}, u32[]{:S(2)}) %collective-permute-start.21) | collective-permute-done | bytes 131104 | tf_op jit(solution)/shard_map/ppermute | solution.py:20
  101.4 4.5 %shard_map.96 = (f32[512,128]{1,0:T(8,128)S(1)}, f32[512,128]{1,0:T(8,128)S(1)}, f32[8,128]{1,0:T(8,128)S(1)}, bf16[1040,128]{1,0:T(8,128)(2,1)S(1)}, bf16[1040,...) custom-call(f32[512,128]{1,0:T(8,128)S(1)} %get-tuple-element.76.ref, ...), custom_call_target="tpu_custom_call" | custom-call | tf_op jit(solution)/shard_map/pallas_call | solution.py:209
  108.0 3.3 %collective-permute-start.28 = (bf16[512,128]{1,0:T(8,128)(2,1)S(1)}, bf16[512,128]{1,0:T(8,128)(2,1)S(1)}, u32[]{:S(2)}, u32[]{:S(2)}) collective-permute-start(bf16[512,128]{1,0:T(8,128)(2,1)S(1)} %get-tuple-element.124), channel_id=1, source_target_pairs={{0,4},{1,5},{2,6},{3,7},{4,0},{5,1},{6,2},{7,3},{8,12},{9,13},{10,... | collective-permute-start | bytes 393224 | tf_op jit(solution)/shard_map/ppermute | solution.py:26
  112.5 3.4 %collective-permute-start.24 = (bf16[272,128]{1,0:T(8,128)(2,1)S(1)}, bf16[272,128]{1,0:T(8,128)(2,1)S(1)}, u32[]{:S(2)}, u32[]{:S(2)}) collective-permute-start(bf16[272,128]{1,0:T(8,128)(2,1)S(1)} %get-tuple-element.119), channel_id=1, source_target_pairs={{0,2},{1,3},{2,0},{3,1},{4,6},{5,7},{6,4},{7,5},{8,10},{9,11},{10,... | collective-permute-start | bytes 208904 | tf_op jit(solution)/shard_map/ppermute | solution.py:26
  119.4 3.4 %collective-permute-done.30.refs_11_ = bf16[256,128]{1,0:T(8,128)(2,1)S(1)} collective-permute-done((bf16[256,128]{1,0:T(8,128)(2,1)S(1)}, bf16[256,128]{1,0:T(8,128)(2,1)S(1)}, u32[]{:S(2)}, u32[]{:S(2)}) %collective-permute-start.30) | collective-permute-done | bytes 65568 | tf_op jit(solution)/shard_map/ppermute | solution.py:26
  122.8 4.6 %shard_map.99 = (f32[512,128]{1,0:T(8,128)S(1)}, f32[512,128]{1,0:T(8,128)S(1)}, f32[512,128]{1,0:T(8,128)S(1)}, f32[8,128]{1,0:T(8,128)S(1)}, bf16[1040,128]{1,...) custom-call(f32[512,128]{1,0:T(8,128)S(1)} %get-tuple-element.113.re, ...), custom_call_target="tpu_custom_call" | custom-call | tf_op jit(solution)/shard_map/pallas_call | solution.py:209
  139.4 3.4 %collective-permute-done.38.refs_11_ = bf16[256,128]{1,0:T(8,128)(2,1)S(1)} collective-permute-done((bf16[256,128]{1,0:T(8,128)(2,1)S(1)}, bf16[256,128]{1,0:T(8,128)(2,1)S(1)}, u32[]{:S(2)}, u32[]{:S(2)}) %collective-permute-start.38) | collective-permute-done | bytes 65568 | tf_op jit(solution)/shard_map/ppermute | solution.py:26
  144.9 2.7 %collective-permute-done.39 = f32[8,128]{1,0:T(8,128)S(1)} collective-permute-done((f32[8,128]{1,0:T(8,128)S(1)}, f32[8,128]{1,0:T(8,128)S(1)}, u32[]{:S(2)}, u32[]{:S(2)}) %collective-permute-start.39) | collective-permute-done | bytes 4128 | tf_op jit(solution)/shard_map/ppermute | solution.py:26
  147.8 3.5 %collective-permute-done.40 = f32[8,128]{1,0:T(8,128)S(1)} collective-permute-done((f32[8,128]{1,0:T(8,128)S(1)}, f32[8,128]{1,0:T(8,128)S(1)}, u32[]{:S(2)}, u32[]{:S(2)}) %collective-permute-start.40) | collective-permute-done | bytes 4128 | tf_op jit(solution)/shard_map/ppermute | solution.py:26
  151.5 4.2 %collective-permute-done.41.refs_1_ = f32[8,128]{1,0:T(8,128)S(1)} collective-permute-done((f32[8,128]{1,0:T(8,128)S(1)}, f32[8,128]{1,0:T(8,128)S(1)}, u32[]{:S(2)}, u32[]{:S(2)}) %collective-permute-start.41) | collective-permute-done | bytes 4128 | tf_op jit(solution)/shard_map/ppermute | solution.py:26
  (92 shorter events, 48.8 us)
Async XLA Ops:
  0.6 64.9 %collective-permute-start = (bf16[1,4,34,128,128]{4,3,2,1,0:T(8,128)(2,1)}, bf16[1,4,34,128,128]{4,3,2,1,0:T(8,128)(2,1)S(1)}, u32[]{:S(2)}, u32[]{:S(2)}) collective-permute-start(bf16[1,4,34,128,128]{4,3,2,1,0:T(8,128)(2,1)} %param.8), channel_id=1, source_target_pairs={{0,8},{16,24},{1,9},{17,25},{2,10},{18,26},{3,11},{19,27},{4,12},{... | collective-permute-start | bytes 13369352 | tf_op jit(solution)/shard_map/ppermute | solution.py:20
  5.0 36.6 %collective-permute-start.9 = (bf16[8704,128]{1,0:T(8,128)(2,1)S(1)}, bf16[8704,128]{1,0:T(8,128)(2,1)S(1)}, u32[]{:S(2)}, u32[]{:S(2)}) collective-permute-start(bf16[8704,128]{1,0:T(8,128)(2,1)S(1)} %get-tuple-element.95), channel_id=1, source_target_pairs={{8,16},{9,17},{10,18},{11,19},{12,20},{13,21},{14,22},{15,23}} | collective-permute-start | bytes 6684680 | tf_op jit(solution)/shard_map/ppermute | solution.py:20
  6.3 35.3 %collective-permute-start.12 = (bf16[8704,128]{1,0:T(8,128)(2,1)S(1)}, bf16[8704,128]{1,0:T(8,128)(2,1)S(1)}, u32[]{:S(2)}, u32[]{:S(2)}) collective-permute-start(bf16[8704,128]{1,0:T(8,128)(2,1)S(1)} %get-tuple-element.99), channel_id=1, source_target_pairs={{16,8},{17,9},{18,10},{19,11},{20,12},{21,13},{22,14},{23,15}} | collective-permute-start | bytes 6684680 | tf_op jit(solution)/shard_map/ppermute | solution.py:20
  14.0 75.5 %collective-permute-start.22 = (bf16[8704,128]{1,0:T(8,128)(2,1)S(1)}, bf16[8704,128]{1,0:T(8,128)(2,1)S(1)}, u32[]{:S(2)}, u32[]{:S(2)}) collective-permute-start(bf16[8704,128]{1,0:T(8,128)(2,1)S(1)} %get-tuple-element.98.refs_7_), channel_id=1, source_target_pairs={{8,16},{9,17},{10,18},{11,19},{12,20},{13,21},{14,22},{15,23}} | collective-permute-start | bytes 6684680 | tf_op jit(solution)/shard_map/ppermute | solution.py:20
  17.9 17.9 %collective-permute-start.11 = (s32[68]{0:T(128)S(1)}, s32[68]{0:T(128)S(1)}, u32[]{:S(2)}, u32[]{:S(2)}) collective-permute-start(s32[68]{0:T(128)S(1)} %get-tuple-element.97), channel_id=1, source_target_pairs={{16,8},{17,9},{18,10},{19,11},{20,12},{21,13},{22,14},{23,15}} | collective-permute-start | bytes 824 | tf_op jit(solution)/shard_map/ppermute | solution.py:20
  44.5 9.9 %collective-permute-start.17 = (bf16[512,128]{1,0:T(8,128)(2,1)S(1)}, bf16[512,128]{1,0:T(8,128)(2,1)S(1)}, u32[]{:S(2)}, u32[]{:S(2)}) collective-permute-start(bf16[512,128]{1,0:T(8,128)(2,1)S(1)} %get-tuple-element.107), channel_id=1, source_target_pairs={{0,6},{1,7},{2,4},{3,5},{4,2},{5,3},{6,0},{7,1},{16,22},{17,23},{1... | collective-permute-start | bytes 393224 | tf_op jit(solution)/shard_map/ppermute | solution.py:26
  50.0 19.7 %collective-permute-start.13 = (bf16[1040,128]{1,0:T(8,128)(2,1)S(1)}, bf16[1040,128]{1,0:T(8,128)(2,1)S(1)}, u32[]{:S(2)}, u32[]{:S(2)}) collective-permute-start(bf16[1040,128]{1,0:T(8,128)(2,1)S(1)} %get-tuple-element.101), channel_id=1, source_target_pairs={{0,1},{1,0},{2,3},{3,2},{4,5},{5,4},{6,7},{7,6},{16,17},{17,16},{1... | collective-permute-start | bytes 798728 | tf_op jit(solution)/shard_map/ppermute | solution.py:26
  52.5 8.6 %collective-permute-start.18 = (bf16[512,128]{1,0:T(8,128)(2,1)S(1)}, bf16[512,128]{1,0:T(8,128)(2,1)S(1)}, u32[]{:S(2)}, u32[]{:S(2)}) collective-permute-start(bf16[512,128]{1,0:T(8,128)(2,1)S(1)} %get-tuple-element.108), channel_id=1, source_target_pairs={{0,4},{1,5},{2,6},{3,7},{4,0},{5,1},{6,2},{7,3},{16,20},{17,21},{1... | collective-permute-start | bytes 393224 | tf_op jit(solution)/shard_map/ppermute | solution.py:26
  54.4 8.0 %collective-permute-start.19 = (bf16[512,128]{1,0:T(8,128)(2,1)S(1)}, bf16[512,128]{1,0:T(8,128)(2,1)S(1)}, u32[]{:S(2)}, u32[]{:S(2)}) collective-permute-start(bf16[512,128]{1,0:T(8,128)(2,1)S(1)} %get-tuple-element.109), channel_id=1, source_target_pairs={{0,2},{1,3},{2,0},{3,1},{4,6},{5,7},{6,4},{7,5},{16,18},{17,19},{1... | collective-permute-start | bytes 393224 | tf_op jit(solution)/shard_map/ppermute | solution.py:26
  66.1 21.1 %collective-permute-start.1 = (bf16[1040,128]{1,0:T(8,128)(2,1)S(1)}, bf16[1040,128]{1,0:T(8,128)(2,1)S(1)}, u32[]{:S(2)}, u32[]{:S(2)}) collective-permute-start(bf16[1040,128]{1,0:T(8,128)(2,1)S(1)} %get-tuple-element.82), channel_id=1, source_target_pairs={{8,9},{9,8},{10,11},{11,10},{12,13},{13,12},{14,15},{15,14},{24,25... | collective-permute-start | bytes 798728 | tf_op jit(solution)/shard_map/ppermute | solution.py:26
  69.8 7.5 %collective-permute-start.7 = (bf16[512,128]{1,0:T(8,128)(2,1)S(1)}, bf16[512,128]{1,0:T(8,128)(2,1)S(1)}, u32[]{:S(2)}, u32[]{:S(2)}) collective-permute-start(bf16[512,128]{1,0:T(8,128)(2,1)S(1)} %get-tuple-element.90), channel_id=1, source_target_pairs={{8,10},{9,11},{10,8},{11,9},{12,14},{13,15},{14,12},{15,13},{24,26... | collective-permute-start | bytes 393224 | tf_op jit(solution)/shard_map/ppermute | solution.py:26
  70.5 10.2 %collective-permute-start.14 = (bf16[272,128]{1,0:T(8,128)(2,1)S(1)}, bf16[272,128]{1,0:T(8,128)(2,1)S(1)}, u32[]{:S(2)}, u32[]{:S(2)}) collective-permute-start(bf16[272,128]{1,0:T(8,128)(2,1)S(1)} %get-tuple-element.103), channel_id=1, source_target_pairs={{0,2},{1,3},{2,0},{3,1},{4,6},{5,7},{6,4},{7,5},{16,18},{17,19},{1... | collective-permute-start | bytes 208904 | tf_op jit(solution)/shard_map/ppermute | solution.py:26
  72.5 9.0 %collective-permute-start.15 = (bf16[272,128]{1,0:T(8,128)(2,1)S(1)}, bf16[272,128]{1,0:T(8,128)(2,1)S(1)}, u32[]{:S(2)}, u32[]{:S(2)}) collective-permute-start(bf16[272,128]{1,0:T(8,128)(2,1)S(1)} %get-tuple-element.104), channel_id=1, source_target_pairs={{0,4},{1,5},{2,6},{3,7},{4,0},{5,1},{6,2},{7,3},{16,20},{17,21},{1... | collective-permute-start | bytes 208904 | tf_op jit(solution)/shard_map/ppermute | solution.py:26
  77.3 8.1 %collective-permute-start.16 = (bf16[272,128]{1,0:T(8,128)(2,1)S(1)}, bf16[272,128]{1,0:T(8,128)(2,1)S(1)}, u32[]{:S(2)}, u32[]{:S(2)}) collective-permute-start(bf16[272,128]{1,0:T(8,128)(2,1)S(1)} %get-tuple-element.105), channel_id=1, source_target_pairs={{0,6},{1,7},{2,4},{3,5},{4,2},{5,3},{6,0},{7,1},{16,22},{17,23},{1... | collective-permute-start | bytes 208904 | tf_op jit(solution)/shard_map/ppermute | solution.py:26
  80.8 7.9 %collective-permute-start.8 = (bf16[256,128]{1,0:T(8,128)(2,1)S(1)}, bf16[256,128]{1,0:T(8,128)(2,1)S(1)}, u32[]{:S(2)}, u32[]{:S(2)}) collective-permute-start(bf16[256,128]{1,0:T(8,128)(2,1)S(1)} %get-tuple-element.92), channel_id=1, source_target_pairs={{8,9},{9,8},{10,11},{11,10},{12,13},{13,12},{14,15},{15,14},{24,25... | collective-permute-start | bytes 196616 | tf_op jit(solution)/shard_map/ppermute | solution.py:26
  86.0 15.4 %collective-permute-start.21 = (bf16[512,128]{1,0:T(8,128)(2,1)S(1)}, bf16[512,128]{1,0:T(8,128)(2,1)S(1)}, u32[]{:S(2)}, u32[]{:S(2)}) collective-permute-start(bf16[512,128]{1,0:T(8,128)(2,1)S(1)} %get-tuple-element.112), channel_id=1, source_target_pairs={{8,16},{9,17},{10,18},{11,19},{12,20},{13,21},{14,22},{15,23}} | collective-permute-start | bytes 393224 | tf_op jit(solution)/shard_map/ppermute | solution.py:20
  106.1 9.8 %collective-permute-start.27 = (bf16[512,128]{1,0:T(8,128)(2,1)S(1)}, bf16[512,128]{1,0:T(8,128)(2,1)S(1)}, u32[]{:S(2)}, u32[]{:S(2)}) collective-permute-start(bf16[512,128]{1,0:T(8,128)(2,1)S(1)} %get-tuple-element.123), channel_id=1, source_target_pairs={{0,6},{1,7},{2,4},{3,5},{4,2},{5,3},{6,0},{7,1},{8,14},{9,15},{10,... | collective-permute-start | bytes 393224 | tf_op jit(solution)/shard_map/ppermute | solution.py:26
  108.0 10.4 %collective-permute-start.28 = (bf16[512,128]{1,0:T(8,128)(2,1)S(1)}, bf16[512,128]{1,0:T(8,128)(2,1)S(1)}, u32[]{:S(2)}, u32[]{:S(2)}) collective-permute-start(bf16[512,128]{1,0:T(8,128)(2,1)S(1)} %get-tuple-element.124), channel_id=1, source_target_pairs={{0,4},{1,5},{2,6},{3,7},{4,0},{5,1},{6,2},{7,3},{8,12},{9,13},{10,... | collective-permute-start | bytes 393224 | tf_op jit(solution)/shard_map/ppermute | solution.py:26
  112.5 10.2 %collective-permute-start.24 = (bf16[272,128]{1,0:T(8,128)(2,1)S(1)}, bf16[272,128]{1,0:T(8,128)(2,1)S(1)}, u32[]{:S(2)}, u32[]{:S(2)}) collective-permute-start(bf16[272,128]{1,0:T(8,128)(2,1)S(1)} %get-tuple-element.119), channel_id=1, source_target_pairs={{0,2},{1,3},{2,0},{3,1},{4,6},{5,7},{6,4},{7,5},{8,10},{9,11},{10,... | collective-permute-start | bytes 208904 | tf_op jit(solution)/shard_map/ppermute | solution.py:26
  128.3 8.0 %collective-permute-start.35 = (bf16[512,128]{1,0:T(8,128)(2,1)S(1)}, bf16[512,128]{1,0:T(8,128)(2,1)S(1)}, u32[]{:S(2)}, u32[]{:S(2)}) collective-permute-start(bf16[512,128]{1,0:T(8,128)(2,1)S(1)} %get-tuple-element.138), channel_id=1, source_target_pairs={{0,6},{1,7},{2,4},{3,5},{4,2},{5,3},{6,0},{7,1},{8,14},{9,15},{10,... | collective-permute-start | bytes 393224 | tf_op jit(solution)/shard_map/ppermute | solution.py:26
  129.6 8.8 %collective-permute-start.36 = (bf16[512,128]{1,0:T(8,128)(2,1)S(1)}, bf16[512,128]{1,0:T(8,128)(2,1)S(1)}, u32[]{:S(2)}, u32[]{:S(2)}) collective-permute-start(bf16[512,128]{1,0:T(8,128)(2,1)S(1)} %get-tuple-element.139), channel_id=1, source_target_pairs={{0,4},{1,5},{2,6},{3,7},{4,0},{5,1},{6,2},{7,3},{8,12},{9,13},{10,... | collective-permute-start | bytes 393224 | tf_op jit(solution)/shard_map/ppermute | solution.py:26
  130.3 8.0 %collective-permute-start.37 = (bf16[512,128]{1,0:T(8,128)(2,1)S(1)}, bf16[512,128]{1,0:T(8,128)(2,1)S(1)}, u32[]{:S(2)}, u32[]{:S(2)}) collective-permute-start(bf16[512,128]{1,0:T(8,128)(2,1)S(1)} %get-tuple-element.140), channel_id=1, source_target_pairs={{0,2},{1,3},{2,0},{3,1},{4,6},{5,7},{6,4},{7,5},{8,10},{9,11},{10,... | collective-permute-start | bytes 393224 | tf_op jit(solution)/shard_map/ppermute | solution.py:26
  133.9 8.9 %collective-permute-start.32 = (bf16[272,128]{1,0:T(8,128)(2,1)S(1)}, bf16[272,128]{1,0:T(8,128)(2,1)S(1)}, u32[]{:S(2)}, u32[]{:S(2)}) collective-permute-start(bf16[272,128]{1,0:T(8,128)(2,1)S(1)} %get-tuple-element.134), channel_id=1, source_target_pairs={{0,2},{1,3},{2,0},{3,1},{4,6},{5,7},{6,4},{7,5},{8,10},{9,11},{10,... | collective-permute-start | bytes 208904 | tf_op jit(solution)/shard_map/ppermute | solution.py:26
  135.0 7.8 %collective-permute-start.33 = (bf16[272,128]{1,0:T(8,128)(2,1)S(1)}, bf16[272,128]{1,0:T(8,128)(2,1)S(1)}, u32[]{:S(2)}, u32[]{:S(2)}) collective-permute-start(bf16[272,128]{1,0:T(8,128)(2,1)S(1)} %get-tuple-element.135), channel_id=1, source_target_pairs={{0,4},{1,5},{2,6},{3,7},{4,0},{5,1},{6,2},{7,3},{8,12},{9,13},{10,... | collective-permute-start | bytes 208904 | tf_op jit(solution)/shard_map/ppermute | solution.py:26
  (23 other events, 155.6 us)

commit v5 on v4

--- a/solution.py
+++ b/solution.py
@@ -20,10 +20,8 @@
     return lax.ppermute(block, "seg", [(s - distance, s) for s in targets])
 
 
-def swapped(block, mask, segments):
-    blk = lax.axis_size("blk")
-    route = [(s * blk + i, s * blk + (i ^ mask)) for s in segments for i in range(blk)]
-    return lax.ppermute(block, ("seg", "blk"), route)
+def swapped(block, mask, axis="blk"):
+    return lax.ppermute(block, axis, [(i, i ^ mask) for i in range(lax.axis_size(axis))])
 
 
 class Plan:
@@ -259,14 +257,17 @@
     lax.fori_loop(0, W // group, several, 0)
 
 
-def flush(plan, row, sum_ref, message_refs):
+def scalars(plan, row, message_refs):
+    for ref in message_refs[:2]:
+        ref[pl.ds(plan.Z * plan.a_rows, PAD), :] = row
+
+
+def flush(plan, sum_ref, message_refs):
     first = 0
     for ref in message_refs:
         rows = ref.shape[0] // plan.D * plan.D
         ref[pl.ds(0, rows), :] = sum_ref[pl.ds(first, rows), :].astype(BF16)
         first += rows
-    for ref in message_refs[:2]:
-        ref[pl.ds(plan.Z * plan.a_rows, PAD), :] = row
 
 
 def work_space(plan):
@@ -276,11 +277,11 @@
     ]
 
 
-def first_own(plan, low, row, slots, left, right):
-    def body(low_ref, row_ref, slot_ref, left_ref, right_ref, *refs):
+def first_next(plan, row, left, right, low, slots):
+    def body(row_ref, left_ref, right_ref, low_ref, slot_ref, *refs):
         message_refs, (half_ref, sum_ref) = refs[:-2], refs[-2:]
 
-        @pl.when(in_odd_segment())
+        @pl.when(jnp.logical_not(in_odd_segment()))
         def _():
             def at(k):
                 return Block((left_ref, k), (right_ref, k), (low_ref, k), (slot_ref, k))
@@ -288,17 +289,21 @@
             sum_ref[...] = jnp.zeros(sum_ref.shape, F32)
             pairs = [(at(k), at(k + plan.H)) for k in range(plan.H)]
             multiply(plan, pairs, half_ref, sum_ref)
-            flush(plan, row_ref[...], sum_ref, message_refs)
-
-    ins = [low, row, slots, left, right]
+            flush(plan, sum_ref, message_refs)
+
+        scalars(plan, row_ref[...], message_refs)
+
+    ins = [row, left, right, low, slots]
     return on_chip(body, ins, plan.messages(), work_space(plan))
 
 
-def first_half(plan, low, row, slots, left, right, other_low, other_slots, held, other_right):
-    def body(*refs):
-        low_ref, row_ref, slot_ref, left_ref, right_ref = refs[:5]
-        other_low_ref, other_slot_ref, held_ref, other_right_ref = refs[5:9]
-        message_refs, (half_ref, sum_ref) = refs[9:-2], refs[-2:]
+def first_half(plan, row, crossed, own, other):
+    n_own = len(own)
+
+    def body(row_ref, crossed_ref, *refs):
+        right_ref, low_ref, slot_ref = refs[:n_own]
+        held_ref, other_low_ref, other_slot_ref = refs[n_own : n_own + 3]
+        message_refs, (half_ref, sum_ref) = refs[n_own + 3 : -2], refs[-2:]
         odd = in_odd_segment()
 
         def all_of(places):
@@ -308,17 +313,19 @@
             sum_ref[...] = jnp.zeros(sum_ref.shape, F32)
             pairs = [(at(k), at(k + plan.H // 2)) for k in range(plan.H // 2)]
             multiply(plan, pairs, half_ref, sum_ref)
-            flush(plan, row_ref[...], sum_ref, message_refs)
+            flush(plan, sum_ref, message_refs)
 
         @pl.when(odd)
         def _():
-            all_of((held_ref, other_right_ref, other_low_ref, other_slot_ref))
+            all_of((held_ref, crossed_ref, other_low_ref, other_slot_ref))
 
         @pl.when(jnp.logical_not(odd))
         def _():
-            all_of((left_ref, right_ref, low_ref, slot_ref))
-
-    ins = [low, row, slots, left, right, other_low, other_slots, held, other_right]
+            all_of((crossed_ref, right_ref, low_ref, slot_ref))
+
+        scalars(plan, row_ref[...], message_refs)
+
+    ins = [row, crossed] + own + other
     return on_chip(body, ins, plan.messages(), work_space(plan))
 
 
@@ -353,7 +360,8 @@
         def _():
             all_of(lambda k: (first_ref, k) if k < plan.H else (last_ref, k - plan.H))
 
-        flush(plan, row, sum_ref, message_refs)
+        flush(plan, sum_ref, message_refs)
+        scalars(plan, row, message_refs)
 
     results = on_chip(
         body,
@@ -402,12 +410,12 @@
 
     def body(keep_ref, got_ref, *outs):
         end = pl.ds(plan.Z * rows, PAD)
-        scalars = split_row(joined_row(keep_ref[end, :]) + joined_row(got_ref[end, :]), plan.D)
+        row = split_row(joined_row(keep_ref[end, :]) + joined_row(got_ref[end, :]), plan.D)
         for z, out in enumerate(outs):
             at = pl.ds(z * rows, rows)
             added = keep_ref[at, :].astype(F32) + got_ref[at, :].astype(F32)
             out[pl.ds(0, rows), :] = added.astype(BF16)
-            out[pl.ds(rows, PAD), :] = scalars
+            out[pl.ds(rows, PAD), :] = row
 
     shape = jax.ShapeDtypeStruct((rows + PAD, plan.D), BF16)
     return on_chip(body, [keep, got], [shape] * plan.Z)
@@ -426,15 +434,15 @@
     return on_chip(body, parts, shapes)
 
 
-def exchanged(plan, messages, segments):
+def exchanged(plan, messages):
     keep, send, b_parts = messages[0], messages[1], messages[2:]
     others = range(plan.Z - 1, 0, -1)
-    got = swapped(send, 1, segments)
-    b_got = [swapped(b_parts[z], 2 * z, segments) for z in others]
+    got = swapped(send, 1)
+    b_got = [swapped(b_parts[z], 2 * z) for z in others]
     a_parts = middle_a(plan, keep, got)
-    a_last = [swapped(a_parts[z], 2 * z, segments) for z in others]
+    a_last = [swapped(a_parts[z], 2 * z) for z in others]
     b_keep, b_send = middle_b(plan, [b_parts[0]] + b_got)
-    return [a_parts[0]] + a_last[::-1] + [b_keep, swapped(b_send, 1, segments)]
+    return [a_parts[0]] + a_last[::-1] + [b_keep, swapped(b_send, 1)]
 
 
 def gathered(plan, arrived, dtype):
@@ -450,27 +458,34 @@
 
 
 def copying(sources, slices):
+    n, m = len(sources), len(slices)
+
     def body(*refs):
-        n = len(sources)
-        copies = []
-        for i, (source, first, rows) in enumerate(slices):
-            done = refs[n + len(slices)].at[i]
-            from_ref = refs[source].at[pl.ds(first, rows)]
-            copies.append(pltpu.make_async_copy(from_ref, refs[n + i], done))
-        for copy in copies:
-            copy.start()
-        for copy in copies:
-            copy.wait()
+        odd = in_odd_segment()
+
+        def all_of(side):
+            copies = []
+            for i, choice in enumerate(slices):
+                source, first = choice[side]
+                from_ref = refs[source].at[pl.ds(first, choice[2])]
+                copies.append(pltpu.make_async_copy(from_ref, refs[n + i], refs[n + m].at[i]))
+            for copy in copies:
+                copy.start()
+            for copy in copies:
+                copy.wait()
+
+        pl.when(jnp.logical_not(odd))(lambda: all_of(0))
+        pl.when(odd)(lambda: all_of(1))
 
     return pl.pallas_call(
         body,
-        in_specs=[pl.BlockSpec(memory_space=pl.ANY)] * len(sources),
-        out_specs=[pl.BlockSpec(memory_space=VMEM)] * len(slices),
+        in_specs=[pl.BlockSpec(memory_space=pl.ANY)] * n,
+        out_specs=[pl.BlockSpec(memory_space=VMEM)] * m,
         out_shape=[
-            jax.ShapeDtypeStruct((rows, sources[i].shape[1]), sources[i].dtype)
-            for i, _, rows in slices
+            jax.ShapeDtypeStruct((c[2], sources[c[0][0]].shape[1]), sources[c[0][0]].dtype)
+            for c in slices
         ],
-        scratch_shapes=[pltpu.SemaphoreType.DMA((len(slices),))],
+        scratch_shapes=[pltpu.SemaphoreType.DMA((m,))],
         compiler_params=pltpu.CompilerParams(vmem_limit_bytes=16 * 2**20),
     )(*[pltpu.with_memory_space_constraint(x, pltpu.HBM) for x in sources])
 
@@ -529,10 +544,7 @@
 ):
     T, W, D = left_environment.shape[1:4]
     plan = Plan(T, W, D, lax.axis_size("blk"))
-    segments = range(lax.axis_size("seg"))
-    evens = [s for s in segments if s % 2 == 0]
-    odds = [s for s in segments if s % 2 == 1]
-    helped = [s for s in evens if s > 0]
+    helped = [s for s in range(1, lax.axis_size("seg")) if s % 2 == 0]
     helpers = [s - 1 for s in helped]
 
     left = left_environment.reshape(T * W * D, D)
@@ -541,40 +553,41 @@
     vector = jax.ShapeDtypeStruct((T * D, D), F32)
     row = jax.ShapeDtypeStruct((8, D), F32)
     start = start_vector.reshape(T * D, D)
-
-    first_rows = plan.H * W * D
-    last_rows = T * W * D - first_rows
-    sent_left, sent_right = copying([left, right], [(0, 0, first_rows), (1, first_rows, last_rows)])
-    left_first = handed(sent_left, helped, 1)
-    right_last = handed(sent_right, helpers, -1)
-    left_own = handed(left_environment, odds, 1).reshape(T * W * D, D)
-    held_left, held_right = copying([left, right], [(0, first_rows, last_rows), (1, 0, T * W * D)])
-    left_last = handed(held_left, helped, 1)
+    every = T * W * D
+    half_rows = every // 2
+
+    (sent,) = copying([left, right], [((1, half_rows), (0, 0), half_rows)])
+    pairs = list(zip(helpers, helped)) + list(zip(helped, helpers))
+    crossed = lax.ppermute(sent, "seg", pairs)
+    (own_side,) = copying([left, right], [((0, 0), (1, 0), every)])
+    partner = swapped(own_side, 1, "seg")
+    held_left, held_right = copying(
+        [left, right], [((0, half_rows), (0, half_rows), half_rows), ((1, 0), (1, 0), every)]
+    )
     x, low, square, slots, last_low, last_slots = prepared(
         plan, start, rows, cols, feed_block[0]
     )
+    partner_low = swapped(low, 1, "seg")
+    partner_slots = swapped(slots, 1, "seg")
     other_low = handed(last_low, helpers, -1)
     other_slots = handed(last_slots, helpers, -1)
 
-    messages = first_own(plan, low, square, slots, left_own, held_right)
-    arrived = exchanged(plan, messages, odds)
+    messages = first_next(plan, square, own_side, partner, partner_low, partner_slots)
+    arrived = exchanged(plan, messages)
     own, own_row = gathered(plan, arrived, F32)
+    own = swapped(own, 1, "seg")
+    left_last = handed(held_left, helped, 1)
     messages = first_half(
         plan,
-        low,
         square,
-        slots,
-        left_first,
-        held_right,
-        other_low,
-        other_slots,
-        held_left,
-        right_last,
-    )
-    half = exchanged(plan, messages, evens + helpers)
+        crossed,
+        [held_right, low, slots],
+        [held_left, other_low, other_slots],
+    )
+    half = exchanged(plan, messages)
     help_sum, _ = gathered(plan, half, BF16)
     help_sum = handed(help_sum, helped, 1)
-    lefts = [left_own, left_first, left_last]
+    lefts = [partner, crossed, left_last]
     (q0, h0, known), messages = operator_step(
         plan,
         update_second,
@@ -584,7 +597,7 @@
         held_right,
         slots,
     )
-    arrived = exchanged(plan, messages, segments)
+    arrived = exchanged(plan, messages)
     (q1, h1, z1, first), messages = operator_step(
         plan,
         update_third,
@@ -594,15 +607,15 @@
         held_right,
         slots,
     )
-    arrived = exchanged(plan, messages, segments)
+    arrived = exchanged(plan, messages)
     q2, z2, second, sums = last_step(
         plan, [q1, h1, z1, rows, cols, energy] + arrived, [vector, vector, row]
     )
     mask = 1
     while 2 * mask < plan.B:
-        sums = sums + swapped(sums, mask, segments)
+        sums = sums + swapped(sums, mask)
         mask *= 2
-    last = swapped(sums, mask, segments)
+    last = swapped(sums, mask)
     residual, coefficients = outcome(plan, q2, z2, first, second, sums, last)
     return (coefficients[:1, :6], residual.reshape(1, T, D, D))
 

time: 160 us -> 160 us (level)
  the two profiles are of different devices: /device:TPU:6 before, /device:TPU:0 now
where the time goes in v5:
time: 160 us
  starting transfers between devices  78.2 us (49%)
  waiting for transfers between devices  51.4 us (32%)
  Pallas kernels  28.6 us (18%)
    ppermute x39, starting transfers between devices, swapped(): lax.ppermute(block, axis, [(i, i ^ mask) for i in range(lax.axis_size(axi...  74.5 us
    ppermute x39, waiting for transfers between devices, swapped(): lax.ppermute(block, axis, [(i, i ^ mask) for i in range(lax.axis_size(axi...  51.4 us
    pallas_call x16, Pallas kernels, on_chip(): pl.pallas_call(body, in_specs=[pl.BlockSpec(memory_space=s) for s in spac...  19.1 us
    pallas_call x3, Pallas kernels, copying(): pl.pallas_call(body, in_specs=[pl.BlockSpec(memory_space=pl.ANY)] * n, ou...  6.89 us
  transfers between devices with their start and end apart: 44, of which 18 were waited for; matrix products, arithmetic and copies ran while one was open for 0% of the time, Pallas kernels for 10%

profile of v5, /device:TPU:0, one launch (start us, length us, event | category | flops | bytes accessed | tf_op | source)
XLA Modules:
  0.0 159.8 jit_solution(12487963672825718328)
XLA Ops:
  6.1 3.0 %shard_map.92 = (bf16[8704,128]{1,0:T(8,128)(2,1)S(1)}, bf16[17408,128]{1,0:T(8,128)(2,1)S(1)}) custom-call(bf16[17408,128]{1,0:T(8,128)(2,1)} %bitcast.23, bf16[17408,128]{1,0:T(8,128)(2,1)} %bitcast.26), custom_call_target="tpu_custom_call" | custom-call | tf_op jit(solution)/shard_map/pallas_call | solution.py:480
  9.9 2.6 %prepared.1 = (f32[512,128]{1,0:T(8,128)S(1)}, bf16[512,128]{1,0:T(8,128)(2,1)S(1)}, bf16[16,128]{1,0:T(8,128)(2,1)S(1)}, s32[136]{0:T(256)S(1)}, bf16[256,128]{1,0:T(8,128)(2,1)S(1)}, /*index=5*/s32[68]{0:T(128)S(1)}) custom-call(bf16[512,128]{1,0:T(8,128)(2,1)S(1)} %bitcast.8, s32[4]{0:T(128)S(1)} %bitcast.9, s32[4]{0:T(128)S(1)} %bitcast.13, ...), custom_call_target="tpu_custom_call" | custom-call | tf_op jit(solution)/shard_map/prepared/pallas_call | solution.py:519
  12.5 5.0 %collective-permute-start.1 = (bf16[512,128]{1,0:T(8,128)(2,1)S(1)}, bf16[512,128]{1,0:T(8,128)(2,1)S(1)}, u32[]{:S(2)}, u32[]{:S(2)}) collective-permute-start(bf16[512,128]{1,0:T(8,128)(2,1)S(1)} %get-tuple-element.76.refs_1_), channel_id=1, source_target_pairs={{0,8},{8,0},{16,24},{24,16},{1,9},{9,1},{17,25},{25,17},{2,10},{10... | collective-permute-start | bytes 393224 | tf_op jit(solution)/shard_map/ppermute | solution.py:24
  18.9 2.9 %shard_map.93 = (bf16[1040,128]{1,0:T(8,128)(2,1)S(1)}, bf16[1040,128]{1,0:T(8,128)(2,1)S(1)}, bf16[512,128]{1,0:T(8,128)(2,1)S(1)}, bf16[512,128]{1,0:T(8,128)(...) custom-call(bf16[16,128]{1,0:T(8,128)(2,1)S(1)} %get-tuple-element.75.row_ref, ...), custom_call_target="tpu_custom_call" | custom-call | tf_op jit(solution)/shard_map/pallas_call | solution.py:207
  21.9 4.3 %collective-permute-start.19 = (bf16[512,128]{1,0:T(8,128)(2,1)S(1)}, bf16[512,128]{1,0:T(8,128)(2,1)S(1)}, u32[]{:S(2)}, u32[]{:S(2)}) collective-permute-start(bf16[512,128]{1,0:T(8,128)(2,1)S(1)} %get-tuple-element.103), channel_id=1, source_target_pairs={{0,6},{1,7},{2,4},{3,5},{4,2},{5,3},{6,0},{7,1},{8,14},{9,15},{10,... | collective-permute-start | bytes 393224 | tf_op jit(solution)/shard_map/ppermute | solution.py:24
  26.1 21.4 %collective-permute-start.2 = (s32[136]{0:T(256)S(1)}, s32[136]{0:T(256)S(1)}, u32[]{:S(2)}, u32[]{:S(2)}) collective-permute-start(s32[136]{0:T(256)S(1)} %get-tuple-element.77.refs_2_.refs_17_.refs_16_), channel_id=1, source_target_pairs={{0,8},{8,0},{16,24},{24,16},{1,9},{9,1},{17,25},{25,17},{2,10},{10... | collective-permute-start | bytes 1640 | tf_op jit(solution)/shard_map/ppermute | solution.py:24
  48.4 4.1 %shard_map.87 = (bf16[1040,128]{1,0:T(8,128)(2,1)S(1)}, bf16[1040,128]{1,0:T(8,128)(2,1)S(1)}, bf16[512,128]{1,0:T(8,128)(2,1)S(1)}, bf16[512,128]{1,0:T(8,128)(...) custom-call(bf16[16,128]{1,0:T(8,128)(2,1)S(1)} %get-tuple-element.75.row_ref, ...), custom_call_target="tpu_custom_call" | custom-call | tf_op jit(solution)/shard_map/pallas_call | solution.py:207
  55.1 3.4 %collective-permute-start.9 = (bf16[512,128]{1,0:T(8,128)(2,1)S(1)}, bf16[512,128]{1,0:T(8,128)(2,1)S(1)}, u32[]{:S(2)}, u32[]{:S(2)}) collective-permute-start(bf16[512,128]{1,0:T(8,128)(2,1)S(1)} %get-tuple-element.87), channel_id=1, source_target_pairs={{0,2},{1,3},{2,0},{3,1},{4,6},{5,7},{6,4},{7,5},{8,10},{9,11},{10,... | collective-permute-start | bytes 393224 | tf_op jit(solution)/shard_map/ppermute | solution.py:24
  58.5 2.6 %collective-permute-done.7.refs_1_ = bf16[512,128]{1,0:T(8,128)(2,1)S(1)} collective-permute-done((bf16[512,128]{1,0:T(8,128)(2,1)S(1)}, bf16[512,128]{1,0:T(8,128)(2,1)S(1)}, u32[]{:S(2)}, u32[]{:S(2)}) %collective-permute-start.7) | collective-permute-done | bytes 131104 | tf_op jit(solution)/shard_map/ppermute | solution.py:24
  61.6 5.4 %collective-permute-done.8.refs_2_ = bf16[512,128]{1,0:T(8,128)(2,1)S(1)} collective-permute-done((bf16[512,128]{1,0:T(8,128)(2,1)S(1)}, bf16[512,128]{1,0:T(8,128)(2,1)S(1)}, u32[]{:S(2)}, u32[]{:S(2)}) %collective-permute-start.8) | collective-permute-done | bytes 131104 | tf_op jit(solution)/shard_map/ppermute | solution.py:24
  68.6 6.5 %collective-permute-done.20.refs_2_ = bf16[512,128]{1,0:T(8,128)(2,1)S(1)} collective-permute-done((bf16[512,128]{1,0:T(8,128)(2,1)S(1)}, bf16[512,128]{1,0:T(8,128)(2,1)S(1)}, u32[]{:S(2)}, u32[]{:S(2)}) %collective-permute-start.20) | collective-permute-done | bytes 131104 | tf_op jit(solution)/shard_map/ppermute | solution.py:24
  75.4 4.1 %collective-permute-start.6 = (bf16[272,128]{1,0:T(8,128)(2,1)S(1)}, bf16[272,128]{1,0:T(8,128)(2,1)S(1)}, u32[]{:S(2)}, u32[]{:S(2)}) collective-permute-start(bf16[272,128]{1,0:T(8,128)(2,1)S(1)} %get-tuple-element.83), channel_id=1, source_target_pairs={{0,6},{1,7},{2,4},{3,5},{4,2},{5,3},{6,0},{7,1},{8,14},{9,15},{10,... | collective-permute-start | bytes 208904 | tf_op jit(solution)/shard_map/ppermute | solution.py:24
  82.9 3.6 %collective-permute-start.17 = (bf16[272,128]{1,0:T(8,128)(2,1)S(1)}, bf16[272,128]{1,0:T(8,128)(2,1)S(1)}, u32[]{:S(2)}, u32[]{:S(2)}) collective-permute-start(bf16[272,128]{1,0:T(8,128)(2,1)S(1)} %get-tuple-element.100), channel_id=1, source_target_pairs={{0,4},{1,5},{2,6},{3,7},{4,0},{5,1},{6,2},{7,3},{8,12},{9,13},{10,... | collective-permute-start | bytes 208904 | tf_op jit(solution)/shard_map/ppermute | solution.py:24
  87.4 3.4 %collective-permute-done.17.refs_2_.refs_9_ = bf16[272,128]{1,0:T(8,128)(2,1)S(1)} collective-permute-done((bf16[272,128]{1,0:T(8,128)(2,1)S(1)}, bf16[272,128]{1,0:T(8,128)(2,1)S(1)}, u32[]{:S(2)}, u32[]{:S(2)}) %collective-permute-start.17) | collective-permute-done | bytes 69664 | tf_op jit(solution)/shard_map/ppermute | solution.py:24
  93.9 4.3 %shard_map.97 = (f32[512,128]{1,0:T(8,128)S(1)}, f32[512,128]{1,0:T(8,128)S(1)}, f32[8,128]{1,0:T(8,128)S(1)}, bf16[1040,128]{1,0:T(8,128)(2,1)S(1)}, bf16[1040,...) custom-call(f32[512,128]{1,0:T(8,128)S(1)} %get-tuple-element.74.ref, ...), custom_call_target="tpu_custom_call" | custom-call | tf_op jit(solution)/shard_map/pallas_call | solution.py:207
  98.3 2.4 %collective-permute-start.29 = (bf16[512,128]{1,0:T(8,128)(2,1)S(1)}, bf16[512,128]{1,0:T(8,128)(2,1)S(1)}, u32[]{:S(2)}, u32[]{:S(2)}) collective-permute-start(bf16[512,128]{1,0:T(8,128)(2,1)S(1)} %get-tuple-element.119), channel_id=1, source_target_pairs={{0,6},{1,7},{2,4},{3,5},{4,2},{5,3},{6,0},{7,1},{8,14},{9,15},{10,... | collective-permute-start | bytes 393224 | tf_op jit(solution)/shard_map/ppermute | solution.py:24
  109.2 4.9 %collective-permute-done.30.refs_2_ = bf16[512,128]{1,0:T(8,128)(2,1)S(1)} collective-permute-done((bf16[512,128]{1,0:T(8,128)(2,1)S(1)}, bf16[512,128]{1,0:T(8,128)(2,1)S(1)}, u32[]{:S(2)}, u32[]{:S(2)}) %collective-permute-start.30) | collective-permute-done | bytes 131104 | tf_op jit(solution)/shard_map/ppermute | solution.py:24
  118.8 4.6 %shard_map.100 = (f32[512,128]{1,0:T(8,128)S(1)}, f32[512,128]{1,0:T(8,128)S(1)}, f32[512,128]{1,0:T(8,128)S(1)}, f32[8,128]{1,0:T(8,128)S(1)}, bf16[1040,128]{1...) custom-call(f32[512,128]{1,0:T(8,128)S(1)} %get-tuple-element.109.re, ...), custom_call_target="tpu_custom_call" | custom-call | tf_op jit(solution)/shard_map/pallas_call | solution.py:207
  125.5 2.7 %collective-permute-start.37 = (bf16[512,128]{1,0:T(8,128)(2,1)S(1)}, bf16[512,128]{1,0:T(8,128)(2,1)S(1)}, u32[]{:S(2)}, u32[]{:S(2)}) collective-permute-start(bf16[512,128]{1,0:T(8,128)(2,1)S(1)} %get-tuple-element.134), channel_id=1, source_target_pairs={{0,6},{1,7},{2,4},{3,5},{4,2},{5,3},{6,0},{7,1},{8,14},{9,15},{10,... | collective-permute-start | bytes 393224 | tf_op jit(solution)/shard_map/ppermute | solution.py:24
  136.2 4.3 %collective-permute-done.38.refs_2_ = bf16[512,128]{1,0:T(8,128)(2,1)S(1)} collective-permute-done((bf16[512,128]{1,0:T(8,128)(2,1)S(1)}, bf16[512,128]{1,0:T(8,128)(2,1)S(1)}, u32[]{:S(2)}, u32[]{:S(2)}) %collective-permute-start.38) | collective-permute-done | bytes 131104 | tf_op jit(solution)/shard_map/ppermute | solution.py:24
  140.6 4.8 %collective-permute-done.40.refs_11_ = bf16[256,128]{1,0:T(8,128)(2,1)S(1)} collective-permute-done((bf16[256,128]{1,0:T(8,128)(2,1)S(1)}, bf16[256,128]{1,0:T(8,128)(2,1)S(1)}, u32[]{:S(2)}, u32[]{:S(2)}) %collective-permute-start.40) | collective-permute-done | bytes 65568 | tf_op jit(solution)/shard_map/ppermute | solution.py:24
  146.7 3.6 %collective-permute-done.41 = f32[8,128]{1,0:T(8,128)S(1)} collective-permute-done((f32[8,128]{1,0:T(8,128)S(1)}, f32[8,128]{1,0:T(8,128)S(1)}, u32[]{:S(2)}, u32[]{:S(2)}) %collective-permute-start.41) | collective-permute-done | bytes 4128 | tf_op jit(solution)/shard_map/ppermute | solution.py:24
  151.5 2.4 %collective-permute-done.42 = f32[8,128]{1,0:T(8,128)S(1)} collective-permute-done((f32[8,128]{1,0:T(8,128)S(1)}, f32[8,128]{1,0:T(8,128)S(1)}, u32[]{:S(2)}, u32[]{:S(2)}) %collective-permute-start.42) | collective-permute-done | bytes 4128 | tf_op jit(solution)/shard_map/ppermute | solution.py:24
  156.1 2.4 %collective-permute-done.43.refs_1_ = f32[8,128]{1,0:T(8,128)S(1)} collective-permute-done((f32[8,128]{1,0:T(8,128)S(1)}, f32[8,128]{1,0:T(8,128)S(1)}, u32[]{:S(2)}, u32[]{:S(2)}) %collective-permute-start.43) | collective-permute-done | bytes 4128 | tf_op jit(solution)/shard_map/ppermute | solution.py:24
  (97 shorter events, 50.1 us)
Async XLA Ops:
  2.9 45.4 %collective-permute-start = (bf16[17408,128]{1,0:T(8,128)(2,1)S(1)}, bf16[17408,128]{1,0:T(8,128)(2,1)S(1)}, u32[]{:S(2)}, u32[]{:S(2)}) collective-permute-start(bf16[17408,128]{1,0:T(8,128)(2,1)S(1)} %shard_map.86.left_ref), channel_id=1, source_target_pairs={{0,8},{8,0},{16,24},{24,16},{1,9},{9,1},{17,25},{25,17},{2,10},{10... | collective-permute-start | bytes 13369352 | tf_op jit(solution)/shard_map/ppermute | solution.py:24
  5.2 13.8 %collective-permute-start.12 = (bf16[8704,128]{1,0:T(8,128)(2,1)S(1)}, bf16[8704,128]{1,0:T(8,128)(2,1)S(1)}, u32[]{:S(2)}, u32[]{:S(2)}) collective-permute-start(bf16[8704,128]{1,0:T(8,128)(2,1)S(1)} %shard_map.91), channel_id=1, source_target_pairs={{8,16},{16,8},{9,17},{17,9},{10,18},{18,10},{11,19},{19,11},{12,20... | collective-permute-start | bytes 6684680 | tf_op jit(solution)/shard_map/ppermute | solution.py:561
  9.1 84.8 %collective-permute-start.24 = (bf16[8704,128]{1,0:T(8,128)(2,1)S(1)}, bf16[8704,128]{1,0:T(8,128)(2,1)S(1)}, u32[]{:S(2)}, u32[]{:S(2)}) collective-permute-start(bf16[8704,128]{1,0:T(8,128)(2,1)S(1)} %get-tuple-element.93.refs_3_), channel_id=1, source_target_pairs={{8,16},{9,17},{10,18},{11,19},{12,20},{13,21},{14,22},{15,23}} | collective-permute-start | bytes 6684680 | tf_op jit(solution)/shard_map/ppermute | solution.py:20
  12.5 35.8 %collective-permute-start.1 = (bf16[512,128]{1,0:T(8,128)(2,1)S(1)}, bf16[512,128]{1,0:T(8,128)(2,1)S(1)}, u32[]{:S(2)}, u32[]{:S(2)}) collective-permute-start(bf16[512,128]{1,0:T(8,128)(2,1)S(1)} %get-tuple-element.76.refs_1_), channel_id=1, source_target_pairs={{0,8},{8,0},{16,24},{24,16},{1,9},{9,1},{17,25},{25,17},{2,10},{10... | collective-permute-start | bytes 393224 | tf_op jit(solution)/shard_map/ppermute | solution.py:24
  21.9 33.2 %collective-permute-start.19 = (bf16[512,128]{1,0:T(8,128)(2,1)S(1)}, bf16[512,128]{1,0:T(8,128)(2,1)S(1)}, u32[]{:S(2)}, u32[]{:S(2)}) collective-permute-start(bf16[512,128]{1,0:T(8,128)(2,1)S(1)} %get-tuple-element.103), channel_id=1, source_target_pairs={{0,6},{1,7},{2,4},{3,5},{4,2},{5,3},{6,0},{7,1},{8,14},{9,15},{10,... | collective-permute-start | bytes 393224 | tf_op jit(solution)/shard_map/ppermute | solution.py:24
  26.1 22.2 %collective-permute-start.2 = (s32[136]{0:T(256)S(1)}, s32[136]{0:T(256)S(1)}, u32[]{:S(2)}, u32[]{:S(2)}) collective-permute-start(s32[136]{0:T(256)S(1)} %get-tuple-element.77.refs_2_.refs_17_.refs_16_), channel_id=1, source_target_pairs={{0,8},{8,0},{16,24},{24,16},{1,9},{9,1},{17,25},{25,17},{2,10},{10... | collective-permute-start | bytes 1640 | tf_op jit(solution)/shard_map/ppermute | solution.py:24
  52.5 14.7 %collective-permute-start.3 = (bf16[1040,128]{1,0:T(8,128)(2,1)S(1)}, bf16[1040,128]{1,0:T(8,128)(2,1)S(1)}, u32[]{:S(2)}, u32[]{:S(2)}) collective-permute-start(bf16[1040,128]{1,0:T(8,128)(2,1)S(1)} %get-tuple-element.79), channel_id=1, source_target_pairs={{0,1},{1,0},{2,3},{3,2},{4,5},{5,4},{6,7},{7,6},{8,9},{9,8},{10,11... | collective-permute-start | bytes 798728 | tf_op jit(solution)/shard_map/ppermute | solution.py:24
  54.4 12.5 %collective-permute-start.8 = (bf16[512,128]{1,0:T(8,128)(2,1)S(1)}, bf16[512,128]{1,0:T(8,128)(2,1)S(1)}, u32[]{:S(2)}, u32[]{:S(2)}) collective-permute-start(bf16[512,128]{1,0:T(8,128)(2,1)S(1)} %get-tuple-element.86), channel_id=1, source_target_pairs={{0,4},{1,5},{2,6},{3,7},{4,0},{5,1},{6,2},{7,3},{8,12},{9,13},{10,... | collective-permute-start | bytes 393224 | tf_op jit(solution)/shard_map/ppermute | solution.py:24
  55.1 11.8 %collective-permute-start.9 = (bf16[512,128]{1,0:T(8,128)(2,1)S(1)}, bf16[512,128]{1,0:T(8,128)(2,1)S(1)}, u32[]{:S(2)}, u32[]{:S(2)}) collective-permute-start(bf16[512,128]{1,0:T(8,128)(2,1)S(1)} %get-tuple-element.87), channel_id=1, source_target_pairs={{0,2},{1,3},{2,0},{3,1},{4,6},{5,7},{6,4},{7,5},{8,10},{9,11},{10,... | collective-permute-start | bytes 393224 | tf_op jit(solution)/shard_map/ppermute | solution.py:24
  61.0 21.7 %collective-permute-start.15 = (bf16[1040,128]{1,0:T(8,128)(2,1)S(1)}, bf16[1040,128]{1,0:T(8,128)(2,1)S(1)}, u32[]{:S(2)}, u32[]{:S(2)}) collective-permute-start(bf16[1040,128]{1,0:T(8,128)(2,1)S(1)} %get-tuple-element.97), channel_id=1, source_target_pairs={{0,1},{1,0},{2,3},{3,2},{4,5},{5,4},{6,7},{7,6},{8,9},{9,8},{10,11... | collective-permute-start | bytes 798728 | tf_op jit(solution)/shard_map/ppermute | solution.py:24
  66.9 8.2 %collective-permute-start.20 = (bf16[512,128]{1,0:T(8,128)(2,1)S(1)}, bf16[512,128]{1,0:T(8,128)(2,1)S(1)}, u32[]{:S(2)}, u32[]{:S(2)}) collective-permute-start(bf16[512,128]{1,0:T(8,128)(2,1)S(1)} %get-tuple-element.104), channel_id=1, source_target_pairs={{0,4},{1,5},{2,6},{3,7},{4,0},{5,1},{6,2},{7,3},{8,12},{9,13},{10,... | collective-permute-start | bytes 393224 | tf_op jit(solution)/shard_map/ppermute | solution.py:24
  82.6 11.3 %collective-permute-start.11 = (f32[512,128]{1,0:T(8,128)S(1)}, f32[512,128]{1,0:T(8,128)S(1)}, u32[]{:S(2)}, u32[]{:S(2)}) collective-permute-start(f32[512,128]{1,0:T(8,128)S(1)} %get-tuple-element.90), channel_id=1, source_target_pairs={{0,8},{8,0},{16,24},{24,16},{1,9},{9,1},{17,25},{25,17},{2,10},{10... | collective-permute-start | bytes 786440 | tf_op jit(solution)/shard_map/ppermute | solution.py:24
  98.3 9.5 %collective-permute-start.29 = (bf16[512,128]{1,0:T(8,128)(2,1)S(1)}, bf16[512,128]{1,0:T(8,128)(2,1)S(1)}, u32[]{:S(2)}, u32[]{:S(2)}) collective-permute-start(bf16[512,128]{1,0:T(8,128)(2,1)S(1)} %get-tuple-element.119), channel_id=1, source_target_pairs={{0,6},{1,7},{2,4},{3,5},{4,2},{5,3},{6,0},{7,1},{8,14},{9,15},{10,... | collective-permute-start | bytes 393224 | tf_op jit(solution)/shard_map/ppermute | solution.py:24
  100.7 13.4 %collective-permute-start.30 = (bf16[512,128]{1,0:T(8,128)(2,1)S(1)}, bf16[512,128]{1,0:T(8,128)(2,1)S(1)}, u32[]{:S(2)}, u32[]{:S(2)}) collective-permute-start(bf16[512,128]{1,0:T(8,128)(2,1)S(1)} %get-tuple-element.120), channel_id=1, source_target_pairs={{0,4},{1,5},{2,6},{3,7},{4,0},{5,1},{6,2},{7,3},{8,12},{9,13},{10,... | collective-permute-start | bytes 393224 | tf_op jit(solution)/shard_map/ppermute | solution.py:24
  101.3 12.9 %collective-permute-start.31 = (bf16[512,128]{1,0:T(8,128)(2,1)S(1)}, bf16[512,128]{1,0:T(8,128)(2,1)S(1)}, u32[]{:S(2)}, u32[]{:S(2)}) collective-permute-start(bf16[512,128]{1,0:T(8,128)(2,1)S(1)} %get-tuple-element.121), channel_id=1, source_target_pairs={{0,2},{1,3},{2,0},{3,1},{4,6},{5,7},{6,4},{7,5},{8,10},{9,11},{10,... | collective-permute-start | bytes 393224 | tf_op jit(solution)/shard_map/ppermute | solution.py:24
  104.7 14.0 %collective-permute-start.26 = (bf16[272,128]{1,0:T(8,128)(2,1)S(1)}, bf16[272,128]{1,0:T(8,128)(2,1)S(1)}, u32[]{:S(2)}, u32[]{:S(2)}) collective-permute-start(bf16[272,128]{1,0:T(8,128)(2,1)S(1)} %get-tuple-element.115), channel_id=1, source_target_pairs={{0,2},{1,3},{2,0},{3,1},{4,6},{5,7},{6,4},{7,5},{8,10},{9,11},{10,... | collective-permute-start | bytes 208904 | tf_op jit(solution)/shard_map/ppermute | solution.py:24
  106.3 12.5 %collective-permute-start.27 = (bf16[272,128]{1,0:T(8,128)(2,1)S(1)}, bf16[272,128]{1,0:T(8,128)(2,1)S(1)}, u32[]{:S(2)}, u32[]{:S(2)}) collective-permute-start(bf16[272,128]{1,0:T(8,128)(2,1)S(1)} %get-tuple-element.116), channel_id=1, source_target_pairs={{0,4},{1,5},{2,6},{3,7},{4,0},{5,1},{6,2},{7,3},{8,12},{9,13},{10,... | collective-permute-start | bytes 208904 | tf_op jit(solution)/shard_map/ppermute | solution.py:24
  107.7 11.0 %collective-permute-start.28 = (bf16[272,128]{1,0:T(8,128)(2,1)S(1)}, bf16[272,128]{1,0:T(8,128)(2,1)S(1)}, u32[]{:S(2)}, u32[]{:S(2)}) collective-permute-start(bf16[272,128]{1,0:T(8,128)(2,1)S(1)} %get-tuple-element.117), channel_id=1, source_target_pairs={{0,6},{1,7},{2,4},{3,5},{4,2},{5,3},{6,0},{7,1},{8,14},{9,15},{10,... | collective-permute-start | bytes 208904 | tf_op jit(solution)/shard_map/ppermute | solution.py:24
  125.5 9.5 %collective-permute-start.37 = (bf16[512,128]{1,0:T(8,128)(2,1)S(1)}, bf16[512,128]{1,0:T(8,128)(2,1)S(1)}, u32[]{:S(2)}, u32[]{:S(2)}) collective-permute-start(bf16[512,128]{1,0:T(8,128)(2,1)S(1)} %get-tuple-element.134), channel_id=1, source_target_pairs={{0,6},{1,7},{2,4},{3,5},{4,2},{5,3},{6,0},{7,1},{8,14},{9,15},{10,... | collective-permute-start | bytes 393224 | tf_op jit(solution)/shard_map/ppermute | solution.py:24
  128.2 12.3 %collective-permute-start.38 = (bf16[512,128]{1,0:T(8,128)(2,1)S(1)}, bf16[512,128]{1,0:T(8,128)(2,1)S(1)}, u32[]{:S(2)}, u32[]{:S(2)}) collective-permute-start(bf16[512,128]{1,0:T(8,128)(2,1)S(1)} %get-tuple-element.135), channel_id=1, source_target_pairs={{0,4},{1,5},{2,6},{3,7},{4,0},{5,1},{6,2},{7,3},{8,12},{9,13},{10,... | collective-permute-start | bytes 393224 | tf_op jit(solution)/shard_map/ppermute | solution.py:24
  128.2 12.3 %collective-permute-start.39 = (bf16[512,128]{1,0:T(8,128)(2,1)S(1)}, bf16[512,128]{1,0:T(8,128)(2,1)S(1)}, u32[]{:S(2)}, u32[]{:S(2)}) collective-permute-start(bf16[512,128]{1,0:T(8,128)(2,1)S(1)} %get-tuple-element.136), channel_id=1, source_target_pairs={{0,2},{1,3},{2,0},{3,1},{4,6},{5,7},{6,4},{7,5},{8,10},{9,11},{10,... | collective-permute-start | bytes 393224 | tf_op jit(solution)/shard_map/ppermute | solution.py:24
  131.2 14.3 %collective-permute-start.34 = (bf16[272,128]{1,0:T(8,128)(2,1)S(1)}, bf16[272,128]{1,0:T(8,128)(2,1)S(1)}, u32[]{:S(2)}, u32[]{:S(2)}) collective-permute-start(bf16[272,128]{1,0:T(8,128)(2,1)S(1)} %get-tuple-element.130), channel_id=1, source_target_pairs={{0,2},{1,3},{2,0},{3,1},{4,6},{5,7},{6,4},{7,5},{8,10},{9,11},{10,... | collective-permute-start | bytes 208904 | tf_op jit(solution)/shard_map/ppermute | solution.py:24
  132.8 12.6 %collective-permute-start.35 = (bf16[272,128]{1,0:T(8,128)(2,1)S(1)}, bf16[272,128]{1,0:T(8,128)(2,1)S(1)}, u32[]{:S(2)}, u32[]{:S(2)}) collective-permute-start(bf16[272,128]{1,0:T(8,128)(2,1)S(1)} %get-tuple-element.131), channel_id=1, source_target_pairs={{0,4},{1,5},{2,6},{3,7},{4,0},{5,1},{6,2},{7,3},{8,12},{9,13},{10,... | collective-permute-start | bytes 208904 | tf_op jit(solution)/shard_map/ppermute | solution.py:24
  135.0 10.5 %collective-permute-start.36 = (bf16[272,128]{1,0:T(8,128)(2,1)S(1)}, bf16[272,128]{1,0:T(8,128)(2,1)S(1)}, u32[]{:S(2)}, u32[]{:S(2)}) collective-permute-start(bf16[272,128]{1,0:T(8,128)(2,1)S(1)} %get-tuple-element.132), channel_id=1, source_target_pairs={{0,6},{1,7},{2,4},{3,5},{4,2},{5,3},{6,0},{7,1},{8,14},{9,15},{10,... | collective-permute-start | bytes 208904 | tf_op jit(solution)/shard_map/ppermute | solution.py:24
  (25 other events, 194.5 us)

commit v6 on v5

--- a/solution.py
+++ b/solution.py
@@ -25,7 +25,7 @@
 
 
 class Plan:
-    def __init__(self, tiles, channels, tile, blk):
+    def __init__(self, tiles, channels, tile, blk, segments):
         self.T, self.W, self.D, self.B = tiles, channels, tile, blk
         self.Z = blk // 2
         self.Ta = tiles // 2
@@ -35,6 +35,8 @@
         self.a_rows = self.Ta * tile
         self.b_rows = self.Tb * tile
         self.H = tiles // 2
+        self.shared = segments == 4
+        self.helped = 2
         self.group = next(
             c for c in range(max(1, channels // 2), 0, -1) if channels % c == 0
         )
@@ -47,6 +49,9 @@
         a = (yr * self.Z + zr) * self.Ta + tile
         b = self.B * self.Ta + (zr * 2 + yr) * self.Tb + (tile - self.Ta)
         return jnp.where(feed >= self.n, self.n, jnp.where(tile < self.Ta, a, b))
+
+    def works_for_next(self):
+        return lax.axis_index("seg") < self.helped
 
     def messages(self):
         a = jax.ShapeDtypeStruct((self.Z * self.a_rows + PAD, self.D), BF16)
@@ -127,15 +132,17 @@
 
 
 def update_second(plan, ins, outs, send):
-    (x_in, rows, cols, energy, own, own_row, helped), arrived = ins[:7], ins[7:]
+    (x_in, rows, cols, energy), arrived = ins[:4], ins[4:]
     q_out, h_out, known_out = outs
-    odd = in_odd_segment()
-    half_tile, half_row = received_sums(plan, arrived)
-    row = jnp.where(odd, own_row[0:1, :], half_row)
+    if plan.shared:
+        handed_on, arrived = arrived[0], arrived[1:]
+    own_tile, row = received_sums(plan, arrived)
 
     def tile(k):
-        at = pl.ds(k * plan.D, plan.D)
-        return jnp.where(odd, own[at, :], half_tile(k) + helped[at, :].astype(F32))
+        if not plan.shared:
+            return own_tile(k)
+        kept = jnp.where(plan.works_for_next(), 0.0, own_tile(k))
+        return kept + handed_on[pl.ds(k * plan.D, plan.D), :].astype(F32)
 
     square = lane(row, 0)
     scale = lax.rsqrt(square / plan.entries + epsilon)
@@ -277,55 +284,35 @@
     ]
 
 
-def first_next(plan, row, left, right, low, slots):
-    def body(row_ref, left_ref, right_ref, low_ref, slot_ref, *refs):
-        message_refs, (half_ref, sum_ref) = refs[:-2], refs[-2:]
-
-        @pl.when(jnp.logical_not(in_odd_segment()))
-        def _():
+def first_step(plan, row, roles):
+    ins, places = [row], []
+    for _, arrays in roles:
+        for array in arrays:
+            if all(array is not known for known in ins):
+                ins.append(array)
+        places.append([next(i for i, a in enumerate(ins) if a is array) for array in arrays])
+
+    def body(*refs):
+        n = len(ins)
+        message_refs, (half_ref, sum_ref) = refs[n:-2], refs[-2:]
+
+        def work(place):
             def at(k):
-                return Block((left_ref, k), (right_ref, k), (low_ref, k), (slot_ref, k))
-
+                return Block(*[(refs[i], k) for i in place])
+
+            blocks = refs[place[0]].shape[0] // (plan.W * plan.D)
             sum_ref[...] = jnp.zeros(sum_ref.shape, F32)
-            pairs = [(at(k), at(k + plan.H)) for k in range(plan.H)]
+            pairs = [(at(k), at(k + blocks // 2)) for k in range(blocks // 2)]
             multiply(plan, pairs, half_ref, sum_ref)
-            flush(plan, sum_ref, message_refs)
-
-        scalars(plan, row_ref[...], message_refs)
-
-    ins = [row, left, right, low, slots]
-    return on_chip(body, ins, plan.messages(), work_space(plan))
-
-
-def first_half(plan, row, crossed, own, other):
-    n_own = len(own)
-
-    def body(row_ref, crossed_ref, *refs):
-        right_ref, low_ref, slot_ref = refs[:n_own]
-        held_ref, other_low_ref, other_slot_ref = refs[n_own : n_own + 3]
-        message_refs, (half_ref, sum_ref) = refs[n_own + 3 : -2], refs[-2:]
-        odd = in_odd_segment()
-
-        def all_of(places):
-            def at(k):
-                return Block(*[(p, k) for p in places])
-
-            sum_ref[...] = jnp.zeros(sum_ref.shape, F32)
-            pairs = [(at(k), at(k + plan.H // 2)) for k in range(plan.H // 2)]
-            multiply(plan, pairs, half_ref, sum_ref)
-            flush(plan, sum_ref, message_refs)
-
-        @pl.when(odd)
-        def _():
-            all_of((held_ref, crossed_ref, other_low_ref, other_slot_ref))
-
-        @pl.when(jnp.logical_not(odd))
-        def _():
-            all_of((crossed_ref, right_ref, low_ref, slot_ref))
-
-        scalars(plan, row_ref[...], message_refs)
-
-    ins = [row, crossed] + own + other
+
+        for (segment, _), place in zip(roles, places):
+            if segment is None:
+                work(place)
+            else:
+                pl.when(lax.axis_index("seg") == segment)(functools.partial(work, place))
+        flush(plan, sum_ref, message_refs)
+        scalars(plan, refs[0][...], message_refs)
+
     return on_chip(body, ins, plan.messages(), work_space(plan))
 
 
@@ -333,9 +320,11 @@
     n_in, n_state = len(ins), len(state_shapes)
 
     def body(*refs):
-        own_ref, first_ref, last_ref, right_ref, slot_ref = refs[n_in : n_in + 5]
-        state_refs = refs[n_in + 5 : n_in + 5 + n_state]
-        message_refs = refs[n_in + 5 + n_state : -3]
+        left_refs = refs[n_in : n_in + len(lefts)]
+        n = n_in + len(lefts)
+        right_ref, slot_ref = refs[n : n + 2]
+        state_refs = refs[n + 2 : n + 2 + n_state]
+        message_refs = refs[n + 2 + n_state : -3]
         low_ref, half_ref, sum_ref = refs[-3:]
         odd = in_odd_segment()
 
@@ -352,13 +341,14 @@
             pairs = [(at(k), at(k + plan.H)) for k in range(plan.H)]
             multiply(plan, pairs, half_ref, sum_ref)
 
-        @pl.when(odd)
-        def _():
-            all_of(lambda k: (own_ref, k))
-
-        @pl.when(jnp.logical_not(odd))
-        def _():
-            all_of(lambda k: (first_ref, k) if k < plan.H else (last_ref, k - plan.H))
+        def in_halves(k):
+            return (left_refs[1], k) if k < plan.H else (left_refs[2], k - plan.H)
+
+        if plan.shared:
+            pl.when(odd)(lambda: all_of(lambda k: (left_refs[0], k)))
+            pl.when(jnp.logical_not(odd))(lambda: all_of(in_halves))
+        else:
+            all_of(lambda k: (left_refs[0], k))
 
         flush(plan, sum_ref, message_refs)
         scalars(plan, row, message_refs)
@@ -447,14 +437,12 @@
 
 def gathered(plan, arrived, dtype):
     def body(*refs):
-        tile, row = received_sums(plan, refs[:-2])
+        tile, _ = received_sums(plan, refs[:-1])
         for k in range(plan.T):
-            refs[-2][pl.ds(k * plan.D, plan.D), :] = tile(k).astype(dtype)
-        refs[-1][...] = jnp.broadcast_to(row, refs[-1].shape)
+            refs[-1][pl.ds(k * plan.D, plan.D), :] = tile(k).astype(dtype)
 
     sums = jax.ShapeDtypeStruct((plan.T * plan.D, plan.D), dtype)
-    row = jax.ShapeDtypeStruct((8, plan.D), F32)
-    return on_chip(body, arrived, [sums, row])
+    return on_chip(body, arrived, [sums])[0]
 
 
 def copying(sources, slices):
@@ -533,6 +521,48 @@
     )(start, rows, cols, feeds)
 
 
+def plain_start(plan, left, right, start, rows, cols, feeds):
+    segments = range(1, lax.axis_size("seg"))
+    left = handed(left, segments, 1)
+    every = right.shape[0]
+    (held_right,) = copying([right], [((0, 0), (0, 0), every)])
+    x, low, square, slots, _, _ = prepared(plan, start, rows, cols, feeds)
+    messages = first_step(plan, square, [(None, [left, held_right, low, slots])])
+    return x, slots, [left], held_right, exchanged(plan, messages)
+
+
+def shared_start(plan, left, right, start, rows, cols, feeds):
+    every = right.shape[0]
+    half = every // 2
+    helped, helper = plan.helped, plan.helped - 1
+
+    (sent,) = copying([left, right], [((1, half), (0, 0), half)])
+    crossed = lax.ppermute(sent, "seg", [(helper, helped), (helped, helper)])
+    (own_side,) = copying([left, right], [((0, 0), (1, 0), every)])
+    partner = swapped(own_side, 1, "seg")
+    x, low, square, slots, last_low, last_slots = prepared(plan, start, rows, cols, feeds)
+    partner_low = swapped(low, 1, "seg")
+    partner_slots = swapped(slots, 1, "seg")
+    other_low = handed(last_low, [helper], -1)
+    other_slots = handed(last_slots, [helper], -1)
+    held_left, held_right = copying(
+        [left, right], [((0, half), (0, half), half), ((1, 0), (1, 0), every)]
+    )
+    left_last = handed(held_left, [helped], 1)
+
+    roles = [
+        (helper - 1, [own_side, partner, partner_low, partner_slots]),
+        (helper, [held_left, crossed, other_low, other_slots]),
+        (helped, [crossed, held_right, low, slots]),
+        (helped + 1, [partner, held_right, low, slots]),
+    ]
+    messages = first_step(plan, square, roles)
+    arrived = exchanged(plan, messages)
+    sums = gathered(plan, arrived, BF16)
+    got = handed(sums, [helper, helped], 1)
+    return x, slots, [partner, crossed, left_last], held_right, [got] + arrived
+
+
 def local(
     start_vector,
     left_environment,
@@ -543,55 +573,21 @@
     feed_block,
 ):
     T, W, D = left_environment.shape[1:4]
-    plan = Plan(T, W, D, lax.axis_size("blk"))
-    helped = [s for s in range(1, lax.axis_size("seg")) if s % 2 == 0]
-    helpers = [s - 1 for s in helped]
-
+    plan = Plan(T, W, D, lax.axis_size("blk"), lax.axis_size("seg"))
     left = left_environment.reshape(T * W * D, D)
     right = right_environment.reshape(T * W * D, D)
     rows, cols, energy = sector_rows[0], sector_cols[0], block_energy[0]
     vector = jax.ShapeDtypeStruct((T * D, D), F32)
     row = jax.ShapeDtypeStruct((8, D), F32)
     start = start_vector.reshape(T * D, D)
-    every = T * W * D
-    half_rows = every // 2
-
-    (sent,) = copying([left, right], [((1, half_rows), (0, 0), half_rows)])
-    pairs = list(zip(helpers, helped)) + list(zip(helped, helpers))
-    crossed = lax.ppermute(sent, "seg", pairs)
-    (own_side,) = copying([left, right], [((0, 0), (1, 0), every)])
-    partner = swapped(own_side, 1, "seg")
-    held_left, held_right = copying(
-        [left, right], [((0, half_rows), (0, half_rows), half_rows), ((1, 0), (1, 0), every)]
+    first = shared_start if plan.shared else plain_start
+    x, slots, lefts, held_right, arrived = first(
+        plan, left, right, start, rows, cols, feed_block[0]
     )
-    x, low, square, slots, last_low, last_slots = prepared(
-        plan, start, rows, cols, feed_block[0]
-    )
-    partner_low = swapped(low, 1, "seg")
-    partner_slots = swapped(slots, 1, "seg")
-    other_low = handed(last_low, helpers, -1)
-    other_slots = handed(last_slots, helpers, -1)
-
-    messages = first_next(plan, square, own_side, partner, partner_low, partner_slots)
-    arrived = exchanged(plan, messages)
-    own, own_row = gathered(plan, arrived, F32)
-    own = swapped(own, 1, "seg")
-    left_last = handed(held_left, helped, 1)
-    messages = first_half(
-        plan,
-        square,
-        crossed,
-        [held_right, low, slots],
-        [held_left, other_low, other_slots],
-    )
-    half = exchanged(plan, messages)
-    help_sum, _ = gathered(plan, half, BF16)
-    help_sum = handed(help_sum, helped, 1)
-    lefts = [partner, crossed, left_last]
     (q0, h0, known), messages = operator_step(
         plan,
         update_second,
-        [x, rows, cols, energy, own, own_row, help_sum] + half,
+        [x, rows, cols, energy] + arrived,
         [vector, vector, row],
         lefts,
         held_right,

time: 160 us -> 136 us (0.85)
  starting transfers between devices: 78.2 us -> 66 us
  waiting for transfers between devices: 51.4 us -> 43.2 us
  Pallas kernels: 28.6 us -> 25.5 us
    ppermute x39 -> x30, starting transfers between devices: 74.5 us -> 58.6 us  [swapped(): lax.ppermute(block, axis, [(i, i ^ mask) for i in range(lax.axis_size(axi...]
    ppermute x39 -> x30, waiting for transfers between devices: 51.4 us -> 42.3 us  [swapped(): lax.ppermute(block, axis, [(i, i ^ mask) for i in range(lax.axis_size(axi...]
    ppermute x4, starting transfers between devices: 2.78 us -> 6.41 us  [handed(): return lax.ppermute(block, 'seg', [(s - distance, s) for s in targets])]
    pallas_call x16 -> x12, Pallas kernels: 19.1 us -> 16 us  [on_chip(): pl.pallas_call(body, in_specs=[pl.BlockSpec(memory_space=s) for s in spac...]
  transfers between devices with their start and end apart: 44 -> 35, of which waited for: 18 -> 15; matrix products, arithmetic and copies ran while one was open for 0% -> 0% of each run, Pallas kernels for 10% -> 9%
where the time goes in v6:
time: 136 us
  starting transfers between devices  66 us (49%)
  waiting for transfers between devices  43.2 us (32%)
  Pallas kernels  25.5 us (19%)
    ppermute x30, starting transfers between devices, swapped(): lax.ppermute(block, axis, [(i, i ^ mask) for i in range(lax.axis_size(axi...  58.6 us
    ppermute x30, waiting for transfers between devices, swapped(): lax.ppermute(block, axis, [(i, i ^ mask) for i in range(lax.axis_size(axi...  42.3 us
    pallas_call x12, Pallas kernels, on_chip(): pl.pallas_call(body, in_specs=[pl.BlockSpec(memory_space=s) for s in spac...  16 us
    pallas_call x3, Pallas kernels, copying(): pl.pallas_call(body, in_specs=[pl.BlockSpec(memory_space=pl.ANY)] * n, ou...  6.89 us
    ppermute x4, starting transfers between devices, handed(): return lax.ppermute(block, 'seg', [(s - distance, s) for s in targets])  6.41 us
  transfers between devices with their start and end apart: 35, of which 15 were waited for; matrix products, arithmetic and copies ran while one was open for 0% of the time, Pallas kernels for 9%

profile of v6, /device:TPU:0, one launch (start us, length us, event | category | flops | bytes accessed | tf_op | source)
XLA Modules:
  0.0 136.1 jit_solution(14473625734383579211)
XLA Ops:
  0.6 2.3 %shard_map.86.refs_1_ = bf16[17408,128]{1,0:T(8,128)(2,1)S(1)} custom-call(bf16[17408,128]{1,0:T(8,128)(2,1)} %bitcast.21, bf16[17408,128]{1,0:T(8,128)(2,1)} %bitcast.24), custom_call_target="tpu_custom_call" | custom-call | tf_op jit(solution)/shard_map/pallas_call | solution.py:468
  6.1 3.0 %shard_map.87 = (bf16[8704,128]{1,0:T(8,128)(2,1)S(1)}, bf16[17408,128]{1,0:T(8,128)(2,1)S(1)}) custom-call(bf16[17408,128]{1,0:T(8,128)(2,1)} %bitcast.23, bf16[17408,128]{1,0:T(8,128)(2,1)} %bitcast.26), custom_call_target="tpu_custom_call" | custom-call | tf_op jit(solution)/shard_map/pallas_call | solution.py:468
  9.9 2.6 %prepared.1 = (f32[512,128]{1,0:T(8,128)S(1)}, bf16[512,128]{1,0:T(8,128)(2,1)S(1)}, bf16[16,128]{1,0:T(8,128)(2,1)S(1)}, s32[136]{0:T(256)S(1)}, bf16[256,128]{1,0:T(8,128)(2,1)S(1)}, /*index=5*/s32[68]{0:T(128)S(1)}) custom-call(bf16[512,128]{1,0:T(8,128)(2,1)S(1)} %bitcast.8, s32[4]{0:T(128)S(1)} %bitcast.9, s32[4]{0:T(128)S(1)} %bitcast.13, ...), custom_call_target="tpu_custom_call" | custom-call | tf_op jit(solution)/shard_map/prepared/pallas_call | solution.py:507
  12.5 5.0 %collective-permute-start.1 = (bf16[512,128]{1,0:T(8,128)(2,1)S(1)}, bf16[512,128]{1,0:T(8,128)(2,1)S(1)}, u32[]{:S(2)}, u32[]{:S(2)}) collective-permute-start(bf16[512,128]{1,0:T(8,128)(2,1)S(1)} %get-tuple-element.61.refs_10_), channel_id=1, source_target_pairs={{0,8},{8,0},{16,24},{24,16},{1,9},{9,1},{17,25},{25,17},{2,10},{10... | collective-permute-start | bytes 393224 | tf_op jit(solution)/shard_map/ppermute | solution.py:24
  18.3 16.8 %collective-permute-start.2 = (s32[136]{0:T(256)S(1)}, s32[136]{0:T(256)S(1)}, u32[]{:S(2)}, u32[]{:S(2)}) collective-permute-start(s32[136]{0:T(256)S(1)} %get-tuple-element.62.refs_11_.refs_15_.refs_16_), channel_id=1, source_target_pairs={{0,8},{8,0},{16,24},{24,16},{1,9},{9,1},{17,25},{25,17},{2,10},{10... | collective-permute-start | bytes 1640 | tf_op jit(solution)/shard_map/ppermute | solution.py:24
  36.6 4.2 %shard_map.89 = (bf16[1040,128]{1,0:T(8,128)(2,1)S(1)}, bf16[1040,128]{1,0:T(8,128)(2,1)S(1)}, bf16[512,128]{1,0:T(8,128)(2,1)S(1)}, bf16[512,128]{1,0:T(8,128)(...) custom-call(bf16[16,128]{1,0:T(8,128)(2,1)S(1)} %get-tuple-element.60.refs_0_, ...), custom_call_target="tpu_custom_call" | custom-call | tf_op jit(solution)/shard_map/pallas_call | solution.py:214
  40.8 2.2 %collective-permute-start.6 = (bf16[1040,128]{1,0:T(8,128)(2,1)S(1)}, bf16[1040,128]{1,0:T(8,128)(2,1)S(1)}, u32[]{:S(2)}, u32[]{:S(2)}) collective-permute-start(bf16[1040,128]{1,0:T(8,128)(2,1)S(1)} %get-tuple-element.68), channel_id=1, source_target_pairs={{0,1},{1,0},{2,3},{3,2},{4,5},{5,4},{6,7},{7,6},{8,9},{9,8},{10,11... | collective-permute-start | bytes 798728 | tf_op jit(solution)/shard_map/ppermute | solution.py:24
  43.0 3.6 %collective-permute-start.10 = (bf16[512,128]{1,0:T(8,128)(2,1)S(1)}, bf16[512,128]{1,0:T(8,128)(2,1)S(1)}, u32[]{:S(2)}, u32[]{:S(2)}) collective-permute-start(bf16[512,128]{1,0:T(8,128)(2,1)S(1)} %get-tuple-element.74), channel_id=1, source_target_pairs={{0,6},{1,7},{2,4},{3,5},{4,2},{5,3},{6,0},{7,1},{8,14},{9,15},{10,... | collective-permute-start | bytes 393224 | tf_op jit(solution)/shard_map/ppermute | solution.py:24
  49.9 3.0 %collective-permute-start.8 = (bf16[272,128]{1,0:T(8,128)(2,1)S(1)}, bf16[272,128]{1,0:T(8,128)(2,1)S(1)}, u32[]{:S(2)}, u32[]{:S(2)}) collective-permute-start(bf16[272,128]{1,0:T(8,128)(2,1)S(1)} %get-tuple-element.71), channel_id=1, source_target_pairs={{0,4},{1,5},{2,6},{3,7},{4,0},{5,1},{6,2},{7,3},{8,12},{9,13},{10,... | collective-permute-start | bytes 208904 | tf_op jit(solution)/shard_map/ppermute | solution.py:24
  52.9 4.8 %collective-permute-done.11.refs_2_ = bf16[512,128]{1,0:T(8,128)(2,1)S(1)} collective-permute-done((bf16[512,128]{1,0:T(8,128)(2,1)S(1)}, bf16[512,128]{1,0:T(8,128)(2,1)S(1)}, u32[]{:S(2)}, u32[]{:S(2)}) %collective-permute-start.11) | collective-permute-done | bytes 131104 | tf_op jit(solution)/shard_map/ppermute | solution.py:24
  58.9 3.8 %collective-permute-done.13.refs_5_.refs_10_ = bf16[256,128]{1,0:T(8,128)(2,1)S(1)} collective-permute-done((bf16[256,128]{1,0:T(8,128)(2,1)S(1)}, bf16[256,128]{1,0:T(8,128)(2,1)S(1)}, u32[]{:S(2)}, u32[]{:S(2)}) %collective-permute-start.13) | collective-permute-done | bytes 65568 | tf_op jit(solution)/shard_map/ppermute | solution.py:24
  64.0 4.3 %collective-permute-start.14 = (bf16[512,128]{1,0:T(8,128)(2,1)S(1)}, bf16[512,128]{1,0:T(8,128)(2,1)S(1)}, u32[]{:S(2)}, u32[]{:S(2)}) collective-permute-start(bf16[512,128]{1,0:T(8,128)(2,1)S(1)} %shard_map.92), channel_id=1, source_target_pairs={{0,8},{8,16},{1,9},{9,17},{2,10},{10,18},{3,11},{11,19},{4,12},{12... | collective-permute-start | bytes 393224 | tf_op jit(solution)/shard_map/ppermute | solution.py:20
  69.3 4.6 %shard_map.93 = (f32[512,128]{1,0:T(8,128)S(1)}, f32[512,128]{1,0:T(8,128)S(1)}, f32[8,128]{1,0:T(8,128)S(1)}, bf16[1040,128]{1,0:T(8,128)(2,1)S(1)}, bf16[1040,...) custom-call(f32[512,128]{1,0:T(8,128)S(1)} %get-tuple-element.59.ref, ...), custom_call_target="tpu_custom_call" | custom-call | tf_op jit(solution)/shard_map/pallas_call | solution.py:214
  76.5 2.4 %collective-permute-start.22 = (bf16[512,128]{1,0:T(8,128)(2,1)S(1)}, bf16[512,128]{1,0:T(8,128)(2,1)S(1)}, u32[]{:S(2)}, u32[]{:S(2)}) collective-permute-start(bf16[512,128]{1,0:T(8,128)(2,1)S(1)} %get-tuple-element.91), channel_id=1, source_target_pairs={{0,2},{1,3},{2,0},{3,1},{4,6},{5,7},{6,4},{7,5},{8,10},{9,11},{10,... | collective-permute-start | bytes 393224 | tf_op jit(solution)/shard_map/ppermute | solution.py:24
  78.9 2.8 %collective-permute-done.16.got_ref = bf16[1040,128]{1,0:T(8,128)(2,1)S(1)} collective-permute-done((bf16[1040,128]{1,0:T(8,128)(2,1)S(1)}, bf16[1040,128]{1,0:T(8,128)(2,1)S(1)}, u32[]{:S(2)}, u32[]{:S(2)}) %collective-permute-start.16) | collective-permute-done | bytes 266272 | tf_op jit(solution)/shard_map/ppermute | solution.py:24
  81.8 3.0 %collective-permute-start.18 = (bf16[272,128]{1,0:T(8,128)(2,1)S(1)}, bf16[272,128]{1,0:T(8,128)(2,1)S(1)}, u32[]{:S(2)}, u32[]{:S(2)}) collective-permute-start(bf16[272,128]{1,0:T(8,128)(2,1)S(1)} %get-tuple-element.86), channel_id=1, source_target_pairs={{0,4},{1,5},{2,6},{3,7},{4,0},{5,1},{6,2},{7,3},{8,12},{9,13},{10,... | collective-permute-start | bytes 208904 | tf_op jit(solution)/shard_map/ppermute | solution.py:24
  89.9 2.8 %collective-permute-done.23.refs_11_ = bf16[256,128]{1,0:T(8,128)(2,1)S(1)} collective-permute-done((bf16[256,128]{1,0:T(8,128)(2,1)S(1)}, bf16[256,128]{1,0:T(8,128)(2,1)S(1)}, u32[]{:S(2)}, u32[]{:S(2)}) %collective-permute-start.23) | collective-permute-done | bytes 65568 | tf_op jit(solution)/shard_map/ppermute | solution.py:24
  92.7 4.7 %shard_map.96 = (f32[512,128]{1,0:T(8,128)S(1)}, f32[512,128]{1,0:T(8,128)S(1)}, f32[512,128]{1,0:T(8,128)S(1)}, f32[8,128]{1,0:T(8,128)S(1)}, bf16[1040,128]{1,...) custom-call(f32[512,128]{1,0:T(8,128)S(1)} %get-tuple-element.79.ref, ...), custom_call_target="tpu_custom_call" | custom-call | tf_op jit(solution)/shard_map/pallas_call | solution.py:214
  105.8 2.3 %collective-permute-start.25 = (bf16[272,128]{1,0:T(8,128)(2,1)S(1)}, bf16[272,128]{1,0:T(8,128)(2,1)S(1)}, u32[]{:S(2)}, u32[]{:S(2)}) collective-permute-start(bf16[272,128]{1,0:T(8,128)(2,1)S(1)} %get-tuple-element.100), channel_id=1, source_target_pairs={{0,2},{1,3},{2,0},{3,1},{4,6},{5,7},{6,4},{7,5},{8,10},{9,11},{10,... | collective-permute-start | bytes 208904 | tf_op jit(solution)/shard_map/ppermute | solution.py:24
  110.5 6.9 %collective-permute-done.29.refs_2_ = bf16[512,128]{1,0:T(8,128)(2,1)S(1)} collective-permute-done((bf16[512,128]{1,0:T(8,128)(2,1)S(1)}, bf16[512,128]{1,0:T(8,128)(2,1)S(1)}, u32[]{:S(2)}, u32[]{:S(2)}) %collective-permute-start.29) | collective-permute-done | bytes 131104 | tf_op jit(solution)/shard_map/ppermute | solution.py:24
  118.0 3.8 %collective-permute-done.31.refs_11_ = bf16[256,128]{1,0:T(8,128)(2,1)S(1)} collective-permute-done((bf16[256,128]{1,0:T(8,128)(2,1)S(1)}, bf16[256,128]{1,0:T(8,128)(2,1)S(1)}, u32[]{:S(2)}, u32[]{:S(2)}) %collective-permute-start.31) | collective-permute-done | bytes 65568 | tf_op jit(solution)/shard_map/ppermute | solution.py:24
  123.5 3.1 %collective-permute-done.32 = f32[8,128]{1,0:T(8,128)S(1)} collective-permute-done((f32[8,128]{1,0:T(8,128)S(1)}, f32[8,128]{1,0:T(8,128)S(1)}, u32[]{:S(2)}, u32[]{:S(2)}) %collective-permute-start.32) | collective-permute-done | bytes 4128 | tf_op jit(solution)/shard_map/ppermute | solution.py:24
  126.6 3.6 %collective-permute-done.33 = f32[8,128]{1,0:T(8,128)S(1)} collective-permute-done((f32[8,128]{1,0:T(8,128)S(1)}, f32[8,128]{1,0:T(8,128)S(1)}, u32[]{:S(2)}, u32[]{:S(2)}) %collective-permute-start.33) | collective-permute-done | bytes 4128 | tf_op jit(solution)/shard_map/ppermute | solution.py:24
  130.7 4.0 %collective-permute-done.34.refs_1_ = f32[8,128]{1,0:T(8,128)S(1)} collective-permute-done((f32[8,128]{1,0:T(8,128)S(1)}, f32[8,128]{1,0:T(8,128)S(1)}, u32[]{:S(2)}, u32[]{:S(2)}) %collective-permute-start.34) | collective-permute-done | bytes 4128 | tf_op jit(solution)/shard_map/ppermute | solution.py:24
  (75 shorter events, 35.7 us)
Async XLA Ops:
  2.9 33.6 %collective-permute-start = (bf16[17408,128]{1,0:T(8,128)(2,1)S(1)}, bf16[17408,128]{1,0:T(8,128)(2,1)S(1)}, u32[]{:S(2)}, u32[]{:S(2)}) collective-permute-start(bf16[17408,128]{1,0:T(8,128)(2,1)S(1)} %shard_map.86.refs_1_), channel_id=1, source_target_pairs={{0,8},{8,0},{16,24},{24,16},{1,9},{9,1},{17,25},{25,17},{2,10},{10... | collective-permute-start | bytes 13369352 | tf_op jit(solution)/shard_map/ppermute | solution.py:24
  5.2 31.4 %collective-permute-start.3 = (bf16[8704,128]{1,0:T(8,128)(2,1)S(1)}, bf16[8704,128]{1,0:T(8,128)(2,1)S(1)}, u32[]{:S(2)}, u32[]{:S(2)}) collective-permute-start(bf16[8704,128]{1,0:T(8,128)(2,1)S(1)} %shard_map.88), channel_id=1, source_target_pairs={{8,16},{16,8},{9,17},{17,9},{10,18},{18,10},{11,19},{19,11},{12,20... | collective-permute-start | bytes 6684680 | tf_op jit(solution)/shard_map/ppermute | solution.py:540
  9.1 59.2 %collective-permute-start.15 = (bf16[8704,128]{1,0:T(8,128)(2,1)S(1)}, bf16[8704,128]{1,0:T(8,128)(2,1)S(1)}, u32[]{:S(2)}, u32[]{:S(2)}) collective-permute-start(bf16[8704,128]{1,0:T(8,128)(2,1)S(1)} %get-tuple-element.63.refs_5_), channel_id=1, source_target_pairs={{8,16},{9,17},{10,18},{11,19},{12,20},{13,21},{14,22},{15,23}} | collective-permute-start | bytes 6684680 | tf_op jit(solution)/shard_map/ppermute | solution.py:20
  12.5 24.0 %collective-permute-start.1 = (bf16[512,128]{1,0:T(8,128)(2,1)S(1)}, bf16[512,128]{1,0:T(8,128)(2,1)S(1)}, u32[]{:S(2)}, u32[]{:S(2)}) collective-permute-start(bf16[512,128]{1,0:T(8,128)(2,1)S(1)} %get-tuple-element.61.refs_10_), channel_id=1, source_target_pairs={{0,8},{8,0},{16,24},{24,16},{1,9},{9,1},{17,25},{25,17},{2,10},{10... | collective-permute-start | bytes 393224 | tf_op jit(solution)/shard_map/ppermute | solution.py:24
  18.3 17.6 %collective-permute-start.2 = (s32[136]{0:T(256)S(1)}, s32[136]{0:T(256)S(1)}, u32[]{:S(2)}, u32[]{:S(2)}) collective-permute-start(s32[136]{0:T(256)S(1)} %get-tuple-element.62.refs_11_.refs_15_.refs_16_), channel_id=1, source_target_pairs={{0,8},{8,0},{16,24},{24,16},{1,9},{9,1},{17,25},{25,17},{2,10},{10... | collective-permute-start | bytes 1640 | tf_op jit(solution)/shard_map/ppermute | solution.py:24
  43.0 6.9 %collective-permute-start.10 = (bf16[512,128]{1,0:T(8,128)(2,1)S(1)}, bf16[512,128]{1,0:T(8,128)(2,1)S(1)}, u32[]{:S(2)}, u32[]{:S(2)}) collective-permute-start(bf16[512,128]{1,0:T(8,128)(2,1)S(1)} %get-tuple-element.74), channel_id=1, source_target_pairs={{0,6},{1,7},{2,4},{3,5},{4,2},{5,3},{6,0},{7,1},{8,14},{9,15},{10,... | collective-permute-start | bytes 393224 | tf_op jit(solution)/shard_map/ppermute | solution.py:24
  46.6 11.1 %collective-permute-start.11 = (bf16[512,128]{1,0:T(8,128)(2,1)S(1)}, bf16[512,128]{1,0:T(8,128)(2,1)S(1)}, u32[]{:S(2)}, u32[]{:S(2)}) collective-permute-start(bf16[512,128]{1,0:T(8,128)(2,1)S(1)} %get-tuple-element.75), channel_id=1, source_target_pairs={{0,4},{1,5},{2,6},{3,7},{4,0},{5,1},{6,2},{7,3},{8,12},{9,13},{10,... | collective-permute-start | bytes 393224 | tf_op jit(solution)/shard_map/ppermute | solution.py:24
  46.6 11.6 %collective-permute-start.12 = (bf16[512,128]{1,0:T(8,128)(2,1)S(1)}, bf16[512,128]{1,0:T(8,128)(2,1)S(1)}, u32[]{:S(2)}, u32[]{:S(2)}) collective-permute-start(bf16[512,128]{1,0:T(8,128)(2,1)S(1)} %get-tuple-element.76), channel_id=1, source_target_pairs={{0,2},{1,3},{2,0},{3,1},{4,6},{5,7},{6,4},{7,5},{8,10},{9,11},{10,... | collective-permute-start | bytes 393224 | tf_op jit(solution)/shard_map/ppermute | solution.py:24
  47.5 15.2 %collective-permute-start.7 = (bf16[272,128]{1,0:T(8,128)(2,1)S(1)}, bf16[272,128]{1,0:T(8,128)(2,1)S(1)}, u32[]{:S(2)}, u32[]{:S(2)}) collective-permute-start(bf16[272,128]{1,0:T(8,128)(2,1)S(1)} %get-tuple-element.70), channel_id=1, source_target_pairs={{0,2},{1,3},{2,0},{3,1},{4,6},{5,7},{6,4},{7,5},{8,10},{9,11},{10,... | collective-permute-start | bytes 208904 | tf_op jit(solution)/shard_map/ppermute | solution.py:24
  49.9 12.8 %collective-permute-start.8 = (bf16[272,128]{1,0:T(8,128)(2,1)S(1)}, bf16[272,128]{1,0:T(8,128)(2,1)S(1)}, u32[]{:S(2)}, u32[]{:S(2)}) collective-permute-start(bf16[272,128]{1,0:T(8,128)(2,1)S(1)} %get-tuple-element.71), channel_id=1, source_target_pairs={{0,4},{1,5},{2,6},{3,7},{4,0},{5,1},{6,2},{7,3},{8,12},{9,13},{10,... | collective-permute-start | bytes 208904 | tf_op jit(solution)/shard_map/ppermute | solution.py:24
  73.9 7.7 %collective-permute-start.16 = (bf16[1040,128]{1,0:T(8,128)(2,1)S(1)}, bf16[1040,128]{1,0:T(8,128)(2,1)S(1)}, u32[]{:S(2)}, u32[]{:S(2)}) collective-permute-start(bf16[1040,128]{1,0:T(8,128)(2,1)S(1)} %get-tuple-element.83), channel_id=1, source_target_pairs={{0,1},{1,0},{2,3},{3,2},{4,5},{5,4},{6,7},{7,6},{8,9},{9,8},{10,11... | collective-permute-start | bytes 798728 | tf_op jit(solution)/shard_map/ppermute | solution.py:24
  74.5 10.3 %collective-permute-start.20 = (bf16[512,128]{1,0:T(8,128)(2,1)S(1)}, bf16[512,128]{1,0:T(8,128)(2,1)S(1)}, u32[]{:S(2)}, u32[]{:S(2)}) collective-permute-start(bf16[512,128]{1,0:T(8,128)(2,1)S(1)} %get-tuple-element.89), channel_id=1, source_target_pairs={{0,6},{1,7},{2,4},{3,5},{4,2},{5,3},{6,0},{7,1},{8,14},{9,15},{10,... | collective-permute-start | bytes 393224 | tf_op jit(solution)/shard_map/ppermute | solution.py:24
  76.5 11.9 %collective-permute-start.21 = (bf16[512,128]{1,0:T(8,128)(2,1)S(1)}, bf16[512,128]{1,0:T(8,128)(2,1)S(1)}, u32[]{:S(2)}, u32[]{:S(2)}) collective-permute-start(bf16[512,128]{1,0:T(8,128)(2,1)S(1)} %get-tuple-element.90), channel_id=1, source_target_pairs={{0,4},{1,5},{2,6},{3,7},{4,0},{5,1},{6,2},{7,3},{8,12},{9,13},{10,... | collective-permute-start | bytes 393224 | tf_op jit(solution)/shard_map/ppermute | solution.py:24
  76.5 11.9 %collective-permute-start.22 = (bf16[512,128]{1,0:T(8,128)(2,1)S(1)}, bf16[512,128]{1,0:T(8,128)(2,1)S(1)}, u32[]{:S(2)}, u32[]{:S(2)}) collective-permute-start(bf16[512,128]{1,0:T(8,128)(2,1)S(1)} %get-tuple-element.91), channel_id=1, source_target_pairs={{0,2},{1,3},{2,0},{3,1},{4,6},{5,7},{6,4},{7,5},{8,10},{9,11},{10,... | collective-permute-start | bytes 393224 | tf_op jit(solution)/shard_map/ppermute | solution.py:24
  81.7 11.0 %collective-permute-start.17 = (bf16[272,128]{1,0:T(8,128)(2,1)S(1)}, bf16[272,128]{1,0:T(8,128)(2,1)S(1)}, u32[]{:S(2)}, u32[]{:S(2)}) collective-permute-start(bf16[272,128]{1,0:T(8,128)(2,1)S(1)} %get-tuple-element.85), channel_id=1, source_target_pairs={{0,2},{1,3},{2,0},{3,1},{4,6},{5,7},{6,4},{7,5},{8,10},{9,11},{10,... | collective-permute-start | bytes 208904 | tf_op jit(solution)/shard_map/ppermute | solution.py:24
  81.8 10.9 %collective-permute-start.18 = (bf16[272,128]{1,0:T(8,128)(2,1)S(1)}, bf16[272,128]{1,0:T(8,128)(2,1)S(1)}, u32[]{:S(2)}, u32[]{:S(2)}) collective-permute-start(bf16[272,128]{1,0:T(8,128)(2,1)S(1)} %get-tuple-element.86), channel_id=1, source_target_pairs={{0,4},{1,5},{2,6},{3,7},{4,0},{5,1},{6,2},{7,3},{8,12},{9,13},{10,... | collective-permute-start | bytes 208904 | tf_op jit(solution)/shard_map/ppermute | solution.py:24
  84.8 7.9 %collective-permute-start.19 = (bf16[272,128]{1,0:T(8,128)(2,1)S(1)}, bf16[272,128]{1,0:T(8,128)(2,1)S(1)}, u32[]{:S(2)}, u32[]{:S(2)}) collective-permute-start(bf16[272,128]{1,0:T(8,128)(2,1)S(1)} %get-tuple-element.87), channel_id=1, source_target_pairs={{0,6},{1,7},{2,4},{3,5},{4,2},{5,3},{6,0},{7,1},{8,14},{9,15},{10,... | collective-permute-start | bytes 208904 | tf_op jit(solution)/shard_map/ppermute | solution.py:24
  97.4 8.3 %collective-permute-start.24 = (bf16[1040,128]{1,0:T(8,128)(2,1)S(1)}, bf16[1040,128]{1,0:T(8,128)(2,1)S(1)}, u32[]{:S(2)}, u32[]{:S(2)}) collective-permute-start(bf16[1040,128]{1,0:T(8,128)(2,1)S(1)} %get-tuple-element.98), channel_id=1, source_target_pairs={{0,1},{1,0},{2,3},{3,2},{4,5},{5,4},{6,7},{7,6},{8,9},{9,8},{10,11... | collective-permute-start | bytes 798728 | tf_op jit(solution)/shard_map/ppermute | solution.py:24
  99.2 9.4 %collective-permute-start.28 = (bf16[512,128]{1,0:T(8,128)(2,1)S(1)}, bf16[512,128]{1,0:T(8,128)(2,1)S(1)}, u32[]{:S(2)}, u32[]{:S(2)}) collective-permute-start(bf16[512,128]{1,0:T(8,128)(2,1)S(1)} %get-tuple-element.104), channel_id=1, source_target_pairs={{0,6},{1,7},{2,4},{3,5},{4,2},{5,3},{6,0},{7,1},{8,14},{9,15},{10,... | collective-permute-start | bytes 393224 | tf_op jit(solution)/shard_map/ppermute | solution.py:24
  100.9 16.5 %collective-permute-start.29 = (bf16[512,128]{1,0:T(8,128)(2,1)S(1)}, bf16[512,128]{1,0:T(8,128)(2,1)S(1)}, u32[]{:S(2)}, u32[]{:S(2)}) collective-permute-start(bf16[512,128]{1,0:T(8,128)(2,1)S(1)} %get-tuple-element.105), channel_id=1, source_target_pairs={{0,4},{1,5},{2,6},{3,7},{4,0},{5,1},{6,2},{7,3},{8,12},{9,13},{10,... | collective-permute-start | bytes 393224 | tf_op jit(solution)/shard_map/ppermute | solution.py:24
  102.4 14.9 %collective-permute-start.30 = (bf16[512,128]{1,0:T(8,128)(2,1)S(1)}, bf16[512,128]{1,0:T(8,128)(2,1)S(1)}, u32[]{:S(2)}, u32[]{:S(2)}) collective-permute-start(bf16[512,128]{1,0:T(8,128)(2,1)S(1)} %get-tuple-element.106), channel_id=1, source_target_pairs={{0,2},{1,3},{2,0},{3,1},{4,6},{5,7},{6,4},{7,5},{8,10},{9,11},{10,... | collective-permute-start | bytes 393224 | tf_op jit(solution)/shard_map/ppermute | solution.py:24
  105.8 16.0 %collective-permute-start.25 = (bf16[272,128]{1,0:T(8,128)(2,1)S(1)}, bf16[272,128]{1,0:T(8,128)(2,1)S(1)}, u32[]{:S(2)}, u32[]{:S(2)}) collective-permute-start(bf16[272,128]{1,0:T(8,128)(2,1)S(1)} %get-tuple-element.100), channel_id=1, source_target_pairs={{0,2},{1,3},{2,0},{3,1},{4,6},{5,7},{6,4},{7,5},{8,10},{9,11},{10,... | collective-permute-start | bytes 208904 | tf_op jit(solution)/shard_map/ppermute | solution.py:24
  108.1 13.7 %collective-permute-start.26 = (bf16[272,128]{1,0:T(8,128)(2,1)S(1)}, bf16[272,128]{1,0:T(8,128)(2,1)S(1)}, u32[]{:S(2)}, u32[]{:S(2)}) collective-permute-start(bf16[272,128]{1,0:T(8,128)(2,1)S(1)} %get-tuple-element.101), channel_id=1, source_target_pairs={{0,4},{1,5},{2,6},{3,7},{4,0},{5,1},{6,2},{7,3},{8,12},{9,13},{10,... | collective-permute-start | bytes 208904 | tf_op jit(solution)/shard_map/ppermute | solution.py:24
  108.6 13.2 %collective-permute-start.27 = (bf16[272,128]{1,0:T(8,128)(2,1)S(1)}, bf16[272,128]{1,0:T(8,128)(2,1)S(1)}, u32[]{:S(2)}, u32[]{:S(2)}) collective-permute-start(bf16[272,128]{1,0:T(8,128)(2,1)S(1)} %get-tuple-element.102), channel_id=1, source_target_pairs={{0,6},{1,7},{2,4},{3,5},{4,2},{5,3},{6,0},{7,1},{8,14},{9,15},{10,... | collective-permute-start | bytes 208904 | tf_op jit(solution)/shard_map/ppermute | solution.py:24
  (16 other events, 96.0 us)
